TPU v7x, 32 devices: a whole 2x2x4 slice. The times are simulated.
32 devices in a mesh: groups: 2 (over y), tiles: 4 (over z), sub: 2 (over x), adj: 2 (over core).
Axes of the slice: x: 2, y: 2, z: 4, core: 2. Of those that a mesh axis runs over, the one named last changes fastest.
Arguments:
- innovation: float32 [128, 256], P(('groups', 'tiles'), 'sub'), parts along dimension 0, may hold values from -6 to 6
- cluster: int32 [128, 256], P(('groups', 'tiles'), 'sub'), parts along dimension 0, may hold values from 0 to 8
- kernel: float32 [36, 64, 256], P(None, 'tiles', 'sub'), may hold values from 0.2 to 1.5
- wind_x: float32 [36, 64, 256], P(None, 'tiles', 'sub'), may hold values from -0.24 to 0.24
- wind_y: float32 [36, 64, 256], P(None, 'tiles', 'sub'), may hold values from -0.24 to 0.24
- conv_strength: float32 [64, 256], P('tiles', 'sub'), may hold values from 0 to 0.9
- conv_matrix: float32 [36, 36], replicated, may hold values from 0 to 1, as said below
- margin_cell: int32 [6144, 8], P(('tiles', 'sub')), may hold values from 0 to 16383, as said below
- margin_weight: float32 [6144, 8], P(('tiles', 'sub')), may hold values from 0 to 1, as said below
Outputs:
- adjoint_field: float32 [16, 36, 64, 256], P(('groups', 'adj'), None, 'tiles', 'sub'), parts along dimension 0
- sensitivity: float32 [16, 6144], P(('groups', 'adj'), ('tiles', 'sub')), parts along dimension 0
There are 2 independent parts, one for each index of `groups`. A program takes and returns all parts, laid end to end along the dimension named above; an argument that names none is the same for every part. Nothing has to cross between parts.
Inputs may be any that keep to these rules, and one draw needn't show every extreme that they name: `conv_matrix`: entries are positive and every column sums to 1. `margin_cell`: state element e is owned by block b = e // 768, with t = b // 2 and s = b % 2; the column index of each of its cells lies in t * 16 - 16 to t * 16 + 2 * 16 - 1, taken modulo 64, and its row in s * 128 - 128 to s * 128 + 2 * 128 - 1 (within 0 to 255). `margin_weight`: each state element has 1 to 8 live slots first, element 0 all 8; the others have weight 0.
All inputs are finite; a program needn't handle non-finite values.
Results may differ from a plain program's by a relative error of at most 0.0003.
Values sent between devices are 32-bit elements; how exact they have to be, the bound alone decides.
No kernel may reach another device: no remote copies, remote signals or barrier semaphores. Data moves between devices by JAX's collectives and lax.ppermute only.
A program may use at most 64 MiB of HBM per device.

v0:
```python
import jax
import jax.numpy as jnp
from jax import lax
from jax.sharding import PartitionSpec as P

ADJ = 8
NSTEP = 2


def shifted(value, axis, steps):
    count = lax.axis_size(axis)
    pairs = [(source, (source + steps) % count) for source in range(count)]
    return lax.ppermute(value, axis, pairs)


def passed_along(block, axis, distance):
    devices = range(lax.axis_size(axis))
    route = [(i - distance, i) for i in devices if i - distance in devices]
    return lax.ppermute(block, axis, route)


def extended(cells, sides, width, closed):
    for axis, dim in sides:
        count = lax.axis_size(axis)
        ends = count if closed else count - 1
        head = lax.slice_in_dim(cells, 0, width, axis=dim)
        tail = lax.slice_in_dim(cells, cells.shape[dim] - width, cells.shape[dim], axis=dim)
        cells = jnp.concatenate(
            [
                lax.ppermute(tail, axis, [(i, (i + 1) % count) for i in range(ends)]),
                cells,
                lax.ppermute(head, axis, [((i + 1) % count, i) for i in range(ends)]),
            ],
            axis=dim,
        )
    return cells


def convect(adjoint, strength, matrix):
    mixed = jnp.einsum("lk,alxy->akxy", matrix, adjoint, precision=lax.Precision.HIGHEST)
    return adjoint + strength * (mixed - adjoint)


def combine(center, east, west, north, south, east_rate, west_rate, north_rate, south_rate):
    rate_sum = 1.0 - east_rate + west_rate - north_rate + south_rate
    return (
        center * rate_sum
        + east_rate * east
        - west_rate * west
        + north_rate * north
        - south_rate * south
    )


def body(
    innovation,
    cluster,
    kernel,
    wind_x,
    wind_y,
    conv_strength,
    conv_matrix,
    margin_cell,
    margin_weight,
):
    width_x = kernel.shape[1]
    width_y = kernel.shape[2]
    per_device = ADJ // lax.axis_size("adj")
    cluster_ids = lax.axis_index("adj") * per_device + jnp.arange(per_device, dtype=jnp.int32)
    chosen = cluster[None] == cluster_ids[:, None, None]
    adjoint = jnp.where(chosen, innovation[None], 0.0)[:, None] * kernel[None]
    west_col = shifted(wind_x[:, -1:], "tiles", 1)
    south_row = passed_along(wind_y[:, :, -1:], "sub", 1)
    east_rate = jnp.maximum(wind_x, 0.0)
    west_rate = jnp.minimum(jnp.concatenate([west_col, wind_x[:, :-1]], axis=1), 0.0)
    north_rate = jnp.maximum(wind_y, 0.0)
    south_rate = jnp.minimum(jnp.concatenate([south_row, wind_y[:, :, :-1]], axis=2), 0.0)
    for step in range(NSTEP):
        adjoint = convect(adjoint, conv_strength, conv_matrix)
        edge_x = jnp.concatenate([adjoint[:, :, :1], adjoint[:, :, -1:]], axis=2)
        seams_x = extended(edge_x, (("tiles", 2),), 1, True)
        edge_y = jnp.concatenate([adjoint[:, :, :, :1], adjoint[:, :, :, -1:]], axis=3)
        seams_y = extended(edge_y, (("sub", 3),), 1, False)
        east = jnp.concatenate([adjoint[:, :, 1:], seams_x[:, :, 3:4]], axis=2)
        west = jnp.concatenate([seams_x[:, :, 0:1], adjoint[:, :, :-1]], axis=2)
        north = jnp.concatenate([adjoint[:, :, :, 1:], seams_y[:, :, :, 3:4]], axis=3)
        south = jnp.concatenate([seams_y[:, :, :, 0:1], adjoint[:, :, :, :-1]], axis=3)
        adjoint = combine(
            adjoint, east, west, north, south, east_rate, west_rate, north_rate, south_rate
        )
    surface = adjoint[:, 0]
    cycle_cells = extended(surface, (("tiles", 1),), width_x, True)
    rim_cells = extended(cycle_cells, (("sub", 2),), width_y, False)
    flat_surface = rim_cells.reshape(per_device, 9 * width_x * width_y)
    tile_pos = lax.axis_index("tiles")
    cross_pos = lax.axis_index("sub")
    cycle_length = width_x * lax.axis_size("tiles")
    cross_length = width_y * lax.axis_size("sub")
    column_x = margin_cell // cross_length
    row_y = margin_cell % cross_length
    local_x = (column_x - tile_pos * width_x + width_x + cycle_length) % cycle_length
    local_y = row_y - cross_pos * width_y + width_y
    local_index = local_x * (3 * width_y) + local_y
    values = jnp.take(flat_surface, local_index.reshape(-1), axis=1).reshape(
        per_device, margin_cell.shape[0], margin_cell.shape[1]
    )
    sensed = jnp.sum(margin_weight[None] * values, axis=2)
    return (adjoint, sensed)


def solution(mesh):
    in_specs = (
        P(("groups", "tiles"), "sub"),
        P(("groups", "tiles"), "sub"),
        P(None, "tiles", "sub"),
        P(None, "tiles", "sub"),
        P(None, "tiles", "sub"),
        P("tiles", "sub"),
        P(),
        P(("tiles", "sub"), None),
        P(("tiles", "sub"), None),
    )
    out_specs = (P(("groups", "adj"), None, "tiles", "sub"), P(("groups", "adj"), ("tiles", "sub")))
    return jax.shard_map(body, mesh=mesh, in_specs=in_specs, out_specs=out_specs, check_vma=False)
```

profile of v0, /device:TPU:0, one launch (start us, length us, event | category | flops | bytes accessed | tf_op | source)
XLA Modules:
  0.0 118.1 jit_solution(2258256967415636589)
XLA Ops:
  0.6 0.0 copy-start
  0.6 1.1 copy.36
  1.7 0.8 compare_select_fusion.2
  2.5 2.2 %multiply_add_fusion = f32[4,36,16,128]{3,1,2,0:T(8,128)S(1)} fusion(f32[16,128]{1,0:T(8,128)} %param.14, f32[36,16,128]{2,0,1:T(8,128)S(1)} %copy.36, f32[4,16,128]{2,1,0:T(8,128)S(1)} %compare_select_fusion.2, f32[36,36]{1,0:T(8,128)S(1)} %copy-done), kind=kOutput, calls=%fused_computation.4 | convolution fusion | flops 128876544 | bytes 1520704 | tf_op jit(solution)/shard_map/lk,alxy->akxy/dot_general | solution.py:40
  4.7 0.7 fusion.60
  5.4 5.1 %collective-permute-start.2 = (f32[4,36,1,128]{3,1,2,0:T(8,128)}, f32[4,36,1,128]{3,1,2,0:T(8,128)S(1)}, u32[]{:S(2)}, u32[]{:S(2)}) collective-permute-start(f32[4,36,1,128]{3,1,2,0:T(8,128)} %get-tuple-element.26), channel_id=1, source_target_pairs={{4,0},{8,4},{12,8},{0,12},{5,1},{9,5},{13,9},{1,13},{6,2},{10,6},{... | collective-permute-start | bytes 221192 | tf_op jit(solution)/shard_map/ppermute | solution.py:32
  10.5 1.5 %fusion.58 = (f32[4,36,16,1]{3,1,2,0:T(8,128)S(1)}, f32[4,36,16,1]{3,1,2,0:T(8,128)}) fusion(f32[4,36,16,128]{3,1,2,0:T(8,128)S(1)} %multiply_add_fusion), kind=kLoop, calls=%fused_computation.83 | loop fusion | bytes 36864 | tf_op jit(solution)/shard_map/slice | solution.py:82
  12.0 1.9 %copy.42 = f32[4,36,16,1]{1,2,3,0:T(8,128)S(1)} copy(f32[4,36,16,1]{3,1,2,0:T(8,128)} %get-tuple-element.22) | data formatting | bytes 18432 | tf_op jit(solution)/shard_map/slice | solution.py:82
  13.9 1.3 %collective-permute-start.4 = (f32[4,36,16,1]{1,2,3,0:T(8,128)S(1)}, f32[4,36,16,1]{1,2,3,0:T(8,128)S(1)}, u32[]{:S(2)}, u32[]{:S(2)}) collective-permute-start(f32[4,36,16,1]{1,2,3,0:T(8,128)S(1)} %copy.42), channel_id=1, source_target_pairs={{2,0},{3,1},{6,4},{7,5},{10,8},{11,9},{14,12},{15,13},{18,16},{19,... | collective-permute-start | bytes 27656 | tf_op jit(solution)/shard_map/ppermute | solution.py:32
  15.2 0.5 copy.45
  15.8 4.5 %collective-permute-start.5 = (f32[4,36,16,1]{1,2,3,0:T(8,128)S(1)}, f32[4,36,16,1]{1,2,3,0:T(8,128)S(1)}, u32[]{:S(2)}, u32[]{:S(2)}) collective-permute-start(f32[4,36,16,1]{1,2,3,0:T(8,128)S(1)} %copy.45), channel_id=1, source_target_pairs={{0,2},{1,3},{4,6},{5,7},{8,10},{9,11},{12,14},{13,15},{16,18},{17,... | collective-permute-start | bytes 27656 | tf_op jit(solution)/shard_map/ppermute | solution.py:30
  20.3 0.1 collective-permute-start
  20.4 0.1 slice.65
  20.6 1.3 %collective-permute-start.1 = (f32[36,16,1]{2,1,0:T(8,128)S(1)}, f32[36,16,1]{2,1,0:T(8,128)S(1)}, u32[]{:S(2)}, u32[]{:S(2)}) collective-permute-start(f32[36,16,1]{2,1,0:T(8,128)S(1)} %slice.65), channel_id=1, source_target_pairs={{0,2},{1,3},{4,6},{5,7},{8,10},{9,11},{12,14},{13,15},{16,18},{17,... | collective-permute-start | bytes 6920 | tf_op jit(solution)/shard_map/ppermute | solution.py:19
  21.9 1.6 %fusion.61 = (f32[4,36,15,128]{3,1,2,0:T(8,128)}, f32[4,36,15,128]{3,1,2,0:T(8,128)}) fusion(f32[4,36,16,128]{3,1,2,0:T(8,128)S(1)} %multiply_add_fusion), kind=kLoop, calls=%fused_computation.86 | loop fusion | bytes 4423680 | tf_op jit(solution)/shard_map/slice | solution.py:85
  23.5 1.9 %fusion.59 = (f32[4,36,16,127]{3,1,2,0:T(8,128)}, f32[4,36,16,127]{3,1,2,0:T(8,128)}) fusion(f32[4,36,16,128]{3,1,2,0:T(8,128)S(1)} %multiply_add_fusion), kind=kLoop, calls=%fused_computation.84 | loop fusion | bytes 4681728 | tf_op jit(solution)/shard_map/slice | solution.py:87
  25.4 0.6 compare_and_fusion
  26.0 0.2 copy.54
  26.2 0.2 reshape.95
  26.5 0.0 collective-permute-done.4
  26.5 0.1 collective-permute-start.3
  26.5 1.6 %copy.43 = f32[4,36,16,1]{3,1,2,0:T(8,128)} copy(f32[4,36,16,1]{1,2,3,0:T(8,128)S(1)} %collective-permute-done.4) | data formatting | bytes 18432 | tf_op jit(solution)/shard_map/ppermute | solution.py:32
  28.2 0.0 collective-permute-done.5
  28.2 1.7 %copy.46 = f32[4,36,16,1]{3,1,2,0:T(8,128)} copy(f32[4,36,16,1]{1,2,3,0:T(8,128)S(1)} %collective-permute-done.5) | data formatting | bytes 18432 | tf_op jit(solution)/shard_map/ppermute | solution.py:30
  29.9 0.7 copy-done.10
  30.6 1.3 %subtract_add_fusion = (f32[36,16,128]{2,1,0:T(8,128)S(1)}, f32[36,16,128]{2,1,0:T(8,128)S(1)}, f32[36,16,128]{2,1,0:T(8,128)S(1)}, f32[36,16,128]{2,1,0:T(8,128)S(1)}, f32[36,16,128]{2,1,0:T(8,128)S(1)}) fusion(f32[36,16,128]{2,1,0:T(8,128)S(1)} %copy-done.9, f32[36,16,128]{2,1,0:T(8,128)S(1)} %copy-done.8, f32[36,15,128]{2,1,0:T(8,128)S(1)} %bitcast.37, ...), kind=kLoop, calls=%fused_computation.49 | loop fusion | flops 737280 | bytes 2654208 | tf_op jit(solution)/shard_map/add | solution.py:45
  31.9 0.1 copy.44
  32.0 0.0 copy-start.15
  32.0 0.1 copy.41
  32.1 0.1 copy.40
  32.2 0.0 copy-start.5
  32.3 0.1 copy.39
  32.4 0.1 copy.38
  32.5 0.3 collective-permute-done.3
  32.8 0.6 copy-done.2
  33.4 0.6 copy-done.1
  34.0 6.2 %fusion.6 = f32[4,36,16,128]{3,1,2,0:T(8,128)S(1)} fusion(f32[4,36,1,128]{3,1,2,0:T(8,128)S(1)} %collective-permute-done.2, f32[4,36,15,128]{3,1,2,0:T(8,128)} %get-tuple-element.28, f32[4,36,15,128]{3,1,2,0:T(8,128)} %get-tuple-element.27, f32[4,36,1,128]{3,1,2,0:T(8,128)S(1)} %collective-permute-done.3, f32[4,36,16,1]{3,1,2,0:T(8,128)S(1)} %copy-done.3, ...), kind=kOutput, calls=%fused_computation.11 | convolution fusion | flops 135954432 | bytes 8565824 | tf_op jit(solution)/shard_map/lk,alxy->akxy/dot_general | solution.py:40
  40.3 0.7 fusion.56
  41.0 1.5 %fusion.54 = (f32[4,36,16,1]{3,1,2,0:T(8,128)S(1)}, f32[4,36,16,1]{3,1,2,0:T(8,128)}) fusion(f32[4,36,16,128]{3,1,2,0:T(8,128)S(1)} %fusion.6), kind=kLoop, calls=%fused_computation.79 | loop fusion | bytes 36864 | tf_op jit(solution)/shard_map/slice | solution.py:82
  42.5 1.9 %fusion.55 = (f32[4,36,16,127]{3,1,2,0:T(8,128)}, f32[4,36,16,127]{3,1,2,0:T(8,128)}) fusion(f32[4,36,16,128]{3,1,2,0:T(8,128)S(1)} %fusion.6), kind=kLoop, calls=%fused_computation.80 | loop fusion | bytes 4681728 | tf_op jit(solution)/shard_map/slice | solution.py:87
  44.4 3.8 %collective-permute-start.6 = (f32[4,36,1,128]{3,1,2,0:T(8,128)}, f32[4,36,1,128]{3,1,2,0:T(8,128)S(1)}, u32[]{:S(2)}, u32[]{:S(2)}) collective-permute-start(f32[4,36,1,128]{3,1,2,0:T(8,128)} %get-tuple-element.18), channel_id=1, source_target_pairs={{4,0},{8,4},{12,8},{0,12},{5,1},{9,5},{13,9},{1,13},{6,2},{10,6},{... | collective-permute-start | bytes 221192 | tf_op jit(solution)/shard_map/ppermute | solution.py:32
  48.2 0.0 collective-permute-start.7
  48.2 1.9 %copy.48 = f32[4,36,16,1]{1,2,3,0:T(8,128)S(1)} copy(f32[4,36,16,1]{3,1,2,0:T(8,128)} %get-tuple-element.14) | data formatting | bytes 18432 | tf_op jit(solution)/shard_map/slice | solution.py:82
  50.0 1.3 %collective-permute-start.8 = (f32[4,36,16,1]{1,2,3,0:T(8,128)S(1)}, f32[4,36,16,1]{1,2,3,0:T(8,128)S(1)}, u32[]{:S(2)}, u32[]{:S(2)}) collective-permute-start(f32[4,36,16,1]{1,2,3,0:T(8,128)S(1)} %copy.48), channel_id=1, source_target_pairs={{2,0},{3,1},{6,4},{7,5},{10,8},{11,9},{14,12},{15,13},{18,16},{19,... | collective-permute-start | bytes 27656 | tf_op jit(solution)/shard_map/ppermute | solution.py:32
  51.3 1.1 copy.50
  52.5 4.7 %collective-permute-start.9 = (f32[4,36,16,1]{1,2,3,0:T(8,128)}, f32[4,36,16,1]{1,2,3,0:T(8,128)S(1)}, u32[]{:S(2)}, u32[]{:S(2)}) collective-permute-start(f32[4,36,16,1]{1,2,3,0:T(8,128)} %copy.50), channel_id=1, source_target_pairs={{0,2},{1,3},{4,6},{5,7},{8,10},{9,11},{12,14},{13,15},{16,18},{17,... | collective-permute-start | bytes 27656 | tf_op jit(solution)/shard_map/ppermute | solution.py:30
  57.2 1.6 %fusion.57 = (f32[4,36,15,128]{3,1,2,0:T(8,128)}, f32[4,36,15,128]{3,1,2,0:T(8,128)}) fusion(f32[4,36,16,128]{3,1,2,0:T(8,128)S(1)} %fusion.6), kind=kLoop, calls=%fused_computation.82 | loop fusion | bytes 4423680 | tf_op jit(solution)/shard_map/slice | solution.py:85
  58.8 0.0 collective-permute-done.8
  58.8 1.6 %copy.49 = f32[4,36,16,1]{3,1,2,0:T(8,128)} copy(f32[4,36,16,1]{1,2,3,0:T(8,128)S(1)} %collective-permute-done.8) | data formatting | bytes 18432 | tf_op jit(solution)/shard_map/ppermute | solution.py:32
  60.5 1.7 %copy.51 = f32[4,36,16,1]{3,1,2,0:T(8,128)} copy(f32[4,36,16,1]{1,2,3,0:T(8,128)S(1)} %collective-permute-done.9) | data formatting | bytes 18432 | tf_op jit(solution)/shard_map/ppermute | solution.py:30
  62.2 0.0 copy-start.14
  62.2 4.7 %fusion.33 = f32[4,36,16,128]{3,1,2,0:T(8,128)S(1)} fusion(f32[4,36,1,128]{3,1,2,0:T(8,128)S(1)} %collective-permute-done.6, f32[4,36,15,128]{3,1,2,0:T(8,128)} %get-tuple-element.20, f32[4,36,15,128]{3,1,2,0:T(8,128)} %get-tuple-element.19, f32[4,36,1,128]{3,1,2,0:T(8,128)S(1)} %collective-permute-done.7, f32[4,36,16,1]{3,1,2,0:T(8,128)} %copy.49, ...), kind=kLoop, calls=%fused_computation.34 | loop fusion | flops 3833856 | bytes 8552448 | tf_op jit(solution)/shard_map/sub | solution.py:47
  66.9 3.9 %collective-permute-start.11 = (f32[4,16,128]{2,1,0:T(8,128)S(1)}, f32[4,16,128]{2,1,0:T(8,128)S(1)}, u32[]{:S(2)}, u32[]{:S(2)}) collective-permute-start(f32[4,16,128]{2,1,0:T(8,128)S(1)} %bitcast.38), channel_id=1, source_target_pairs={{4,0},{8,4},{12,8},{0,12},{5,1},{9,5},{13,9},{1,13},{6,2},{10,6},{... | collective-permute-start | bytes 98312 | tf_op jit(solution)/shard_map/ppermute | solution.py:32
  70.8 1.6 %collective-permute-done.11 = f32[4,16,128]{2,1,0:T(8,128)S(1)} collective-permute-done((f32[4,16,128]{2,1,0:T(8,128)S(1)}, f32[4,16,128]{2,1,0:T(8,128)S(1)}, u32[]{:S(2)}, u32[]{:S(2)}) %collective-permute-start.11) | collective-permute-done | bytes 32800 | tf_op jit(solution)/shard_map/ppermute | solution.py:32
  72.4 4.1 %collective-permute-done.10 = f32[4,16,128]{2,1,0:T(8,128)S(1)} collective-permute-done((f32[4,16,128]{2,1,0:T(8,128)S(1)}, f32[4,16,128]{2,1,0:T(8,128)S(1)}, u32[]{:S(2)}, u32[]{:S(2)}) %collective-permute-start.10) | collective-permute-done | bytes 32800 | tf_op jit(solution)/shard_map/ppermute | solution.py:30
  76.5 1.3 %collective-permute-start.13 = (f32[4,48,128]{2,1,0:T(8,128)S(1)}, f32[4,48,128]{2,1,0:T(8,128)S(1)}, u32[]{:S(2)}, u32[]{:S(2)}) collective-permute-start(f32[4,48,128]{2,1,0:T(8,128)S(1)} %pad_maximum_fusion.1), channel_id=1, source_target_pairs={{2,0},{3,1},{6,4},{7,5},{10,8},{11,9},{14,12},{15,13},{18,16},{19,... | collective-permute-start | bytes 294920 | tf_op jit(solution)/shard_map/ppermute | solution.py:32
  77.8 4.6 %collective-permute-start.12 = (f32[4,48,128]{2,1,0:T(8,128)S(1)}, f32[4,48,128]{2,1,0:T(8,128)S(1)}, u32[]{:S(2)}, u32[]{:S(2)}) collective-permute-start(f32[4,48,128]{2,1,0:T(8,128)S(1)} %pad_maximum_fusion.1), channel_id=1, source_target_pairs={{0,2},{1,3},{4,6},{5,7},{8,10},{9,11},{12,14},{13,15},{16,18},{17,... | collective-permute-start | bytes 294920 | tf_op jit(solution)/shard_map/ppermute | solution.py:30
  82.4 0.9 copy.52
  83.3 0.2 copy.53
  83.5 1.2 %copy.56 = f32[4,36,16,128]{3,2,1,0:T(8,128)} copy(f32[4,36,16,128]{3,1,2,0:T(8,128)S(1)} %fusion.33) | data formatting | bytes 2359296
  84.8 5.7 %copy.62 = f32[4,48,384]{0,2,1:T(8,128)} copy(f32[4,48,384]{2,1,0:T(8,128)S(1)} %pad_maximum_fusion) | data formatting | bytes 589824 | tf_op jit(solution)/shard_map/reshape | solution.py:94
  90.5 19.8 %gather_fusion = f32[6144,4]{1,0:T(8,128)S(1)} fusion(f32[4,18432]{0,1:T(8,128)} %bitcast.35, s32[6144]{0:T(1024)S(1)} %broadcast_clamp_fusion), kind=kCustom, calls=%fused_computation | custom fusion | bytes 221184 | tf_op jit(solution)/shard_map/jit(_take)/gather | solution.py:104
  110.2 6.1 %fusion.1 = f32[4,768]{0,1:T(8,128)} fusion(f32[6144,4]{1,0:T(8,128)S(1)} %gather_fusion, f32[768,8]{1,0:T(8,128)} %copy.52, pred[768,8]{1,0:T(8,128)(4,1)S(1)} %copy.53), kind=kLoop, calls=%fused_computation.3 | loop fusion | flops 70656 | bytes 141312 | tf_op jit(solution)/shard_map/reduce_sum | solution.py:107
  116.4 1.7 %copy.57 = f32[4,768]{1,0:T(4,128)} copy(f32[4,768]{0,1:T(8,128)} %fusion.1) | data formatting | bytes 24576
  (41 shorter events, 0.2 us)
Async XLA Ops:
  0.6 1.9 %copy-start = (f32[36,36]{1,0:T(8,128)S(1)}, f32[36,36]{1,0:T(8,128)}, u32[]{:S(2)}) copy-start(f32[36,36]{1,0:T(8,128)} %param.15) | copy-start | bytes 15556
  5.4 27.1 %collective-permute-start.2 = (f32[4,36,1,128]{3,1,2,0:T(8,128)}, f32[4,36,1,128]{3,1,2,0:T(8,128)S(1)}, u32[]{:S(2)}, u32[]{:S(2)}) collective-permute-start(f32[4,36,1,128]{3,1,2,0:T(8,128)} %get-tuple-element.26), channel_id=1, source_target_pairs={{4,0},{8,4},{12,8},{0,12},{5,1},{9,5},{13,9},{1,13},{6,2},{10,6},{... | collective-permute-start | bytes 221192 | tf_op jit(solution)/shard_map/ppermute | solution.py:32
  12.0 8.3 %copy-start.9 = (f32[36,16,128]{2,1,0:T(8,128)S(1)}, f32[36,16,128]{2,1,0:T(8,128)}, u32[]{:S(2)}) copy-start(f32[36,16,128]{2,1,0:T(8,128)} %param.12) | copy-start | bytes 884740
  12.0 8.4 %copy-start.8 = (f32[36,16,128]{2,1,0:T(8,128)S(1)}, f32[36,16,128]{2,1,0:T(8,128)}, u32[]{:S(2)}) copy-start(f32[36,16,128]{2,1,0:T(8,128)} %param.13) | copy-start | bytes 884740
  13.9 12.5 %collective-permute-start.4 = (f32[4,36,16,1]{1,2,3,0:T(8,128)S(1)}, f32[4,36,16,1]{1,2,3,0:T(8,128)S(1)}, u32[]{:S(2)}, u32[]{:S(2)}) collective-permute-start(f32[4,36,16,1]{1,2,3,0:T(8,128)S(1)} %copy.42), channel_id=1, source_target_pairs={{2,0},{3,1},{6,4},{7,5},{10,8},{11,9},{14,12},{15,13},{18,16},{19,... | collective-permute-start | bytes 27656 | tf_op jit(solution)/shard_map/ppermute | solution.py:32
  15.8 12.4 %collective-permute-start.5 = (f32[4,36,16,1]{1,2,3,0:T(8,128)S(1)}, f32[4,36,16,1]{1,2,3,0:T(8,128)S(1)}, u32[]{:S(2)}, u32[]{:S(2)}) collective-permute-start(f32[4,36,16,1]{1,2,3,0:T(8,128)S(1)} %copy.45), channel_id=1, source_target_pairs={{0,2},{1,3},{4,6},{5,7},{8,10},{9,11},{12,14},{13,15},{16,18},{17,... | collective-permute-start | bytes 27656 | tf_op jit(solution)/shard_map/ppermute | solution.py:30
  20.3 9.5 %collective-permute-start = (f32[36,1,128]{2,1,0:T(1,128)S(1)}, f32[36,1,128]{2,1,0:T(1,128)S(1)}, u32[]{:S(2)}, u32[]{:S(2)}) collective-permute-start(f32[36,1,128]{2,1,0:T(1,128)S(1)} %slice.63), channel_id=1, source_target_pairs={{0,4},{4,8},{8,12},{12,0},{1,5},{5,9},{9,13},{13,1},{2,6},{6,10},{... | collective-permute-start | bytes 55304 | tf_op jit(solution)/shard_map/ppermute | solution.py:13
  20.6 9.3 %collective-permute-start.1 = (f32[36,16,1]{2,1,0:T(8,128)S(1)}, f32[36,16,1]{2,1,0:T(8,128)S(1)}, u32[]{:S(2)}, u32[]{:S(2)}) collective-permute-start(f32[36,16,1]{2,1,0:T(8,128)S(1)} %slice.65), channel_id=1, source_target_pairs={{0,2},{1,3},{4,6},{5,7},{8,10},{9,11},{12,14},{13,15},{16,18},{17,... | collective-permute-start | bytes 6920 | tf_op jit(solution)/shard_map/ppermute | solution.py:19
  23.5 1.9 %copy-start.12 = (s32[768,8]{0,1:T(8,128)S(1)}, s32[768,8]{0,1:T(8,128)}, u32[]{:S(2)}) copy-start(s32[768,8]{0,1:T(8,128)} %param.16) | copy-start | bytes 73732
  23.5 3.0 %copy-start.11 = (f32[4,36,1,128]{3,1,2,0:T(8,128)S(1)}, f32[4,36,1,128]{3,1,2,0:T(8,128)}, u32[]{:S(2)}) copy-start(f32[4,36,1,128]{3,1,2,0:T(8,128)} %get-tuple-element.25) | copy-start | bytes 221188
  26.5 6.3 %collective-permute-start.3 = (f32[4,36,1,128]{3,1,2,0:T(8,128)S(1)}, f32[4,36,1,128]{3,1,2,0:T(8,128)S(1)}, u32[]{:S(2)}, u32[]{:S(2)}) collective-permute-start(f32[4,36,1,128]{3,1,2,0:T(8,128)S(1)} %copy-done.11), channel_id=1, source_target_pairs={{0,4},{4,8},{8,12},{12,0},{1,5},{5,9},{9,13},{13,1},{2,6},{6,10},{... | collective-permute-start | bytes 221192 | tf_op jit(solution)/shard_map/ppermute | solution.py:30
  29.9 0.7 copy-start.10
  30.6 2.2 %copy-start.3 = (f32[4,36,16,1]{3,1,2,0:T(8,128)S(1)}, f32[4,36,16,1]{3,1,2,0:T(8,128)}, u32[]{:S(2)}) copy-start(f32[4,36,16,1]{3,1,2,0:T(8,128)} %copy.43) | copy-start | bytes 27652
  30.6 2.2 %copy-start.4 = (f32[4,36,16,1]{3,1,2,0:T(8,128)S(1)}, f32[4,36,16,1]{3,1,2,0:T(8,128)}, u32[]{:S(2)}) copy-start(f32[4,36,16,1]{3,1,2,0:T(8,128)} %copy.46) | copy-start | bytes 27652
  31.9 1.5 %copy-start.2 = (f32[4,36,16,127]{3,1,2,0:T(8,128)S(1)}, f32[4,36,16,127]{3,1,2,0:T(8,128)}, u32[]{:S(2)}) copy-start(f32[4,36,16,127]{3,1,2,0:T(8,128)} %get-tuple-element.24) | copy-start | bytes 3511300
  32.0 2.0 %copy-start.1 = (f32[4,36,16,127]{3,1,2,0:T(8,128)S(1)}, f32[4,36,16,127]{3,1,2,0:T(8,128)}, u32[]{:S(2)}) copy-start(f32[4,36,16,127]{3,1,2,0:T(8,128)} %get-tuple-element.23) | copy-start | bytes 3511300
  32.0 2.0 %copy-start.15 = (f32[16,128]{1,0:T(8,128)S(1)}, f32[16,128]{1,0:T(8,128)}, u32[]{:S(2)}) copy-start(f32[16,128]{1,0:T(8,128)} %param.14) | copy-start | bytes 24580
  32.2 8.0 %copy-start.5 = (f32[36,16,128]{2,0,1:T(8,128)}, f32[36,16,128]{2,0,1:T(8,128)S(1)}, u32[]{:S(2)}) copy-start(f32[36,16,128]{2,0,1:T(8,128)S(1)} %copy.40) | copy-start | bytes 884740
  32.4 7.9 %copy-start.6 = (f32[36,16,128]{2,0,1:T(8,128)}, f32[36,16,128]{2,0,1:T(8,128)S(1)}, u32[]{:S(2)}) copy-start(f32[36,16,128]{2,0,1:T(8,128)S(1)} %copy.39) | copy-start | bytes 884740
  32.5 7.8 %copy-start.7 = (f32[36,16,128]{2,0,1:T(8,128)}, f32[36,16,128]{2,0,1:T(8,128)S(1)}, u32[]{:S(2)}) copy-start(f32[36,16,128]{2,0,1:T(8,128)S(1)} %copy.38) | copy-start | bytes 884740
  44.4 17.8 %collective-permute-start.6 = (f32[4,36,1,128]{3,1,2,0:T(8,128)}, f32[4,36,1,128]{3,1,2,0:T(8,128)S(1)}, u32[]{:S(2)}, u32[]{:S(2)}) collective-permute-start(f32[4,36,1,128]{3,1,2,0:T(8,128)} %get-tuple-element.18), channel_id=1, source_target_pairs={{4,0},{8,4},{12,8},{0,12},{5,1},{9,5},{13,9},{1,13},{6,2},{10,6},{... | collective-permute-start | bytes 221192 | tf_op jit(solution)/shard_map/ppermute | solution.py:32
  48.2 14.0 %collective-permute-start.7 = (f32[4,36,1,128]{3,1,2,0:T(8,128)}, f32[4,36,1,128]{3,1,2,0:T(8,128)S(1)}, u32[]{:S(2)}, u32[]{:S(2)}) collective-permute-start(f32[4,36,1,128]{3,1,2,0:T(8,128)} %get-tuple-element.17), channel_id=1, source_target_pairs={{0,4},{4,8},{8,12},{12,0},{1,5},{5,9},{9,13},{13,1},{2,6},{6,10},{... | collective-permute-start | bytes 221192 | tf_op jit(solution)/shard_map/ppermute | solution.py:30
  50.0 8.8 %collective-permute-start.8 = (f32[4,36,16,1]{1,2,3,0:T(8,128)S(1)}, f32[4,36,16,1]{1,2,3,0:T(8,128)S(1)}, u32[]{:S(2)}, u32[]{:S(2)}) collective-permute-start(f32[4,36,16,1]{1,2,3,0:T(8,128)S(1)} %copy.48), channel_id=1, source_target_pairs={{2,0},{3,1},{6,4},{7,5},{10,8},{11,9},{14,12},{15,13},{18,16},{19,... | collective-permute-start | bytes 27656 | tf_op jit(solution)/shard_map/ppermute | solution.py:32
  52.5 8.0 %collective-permute-start.9 = (f32[4,36,16,1]{1,2,3,0:T(8,128)}, f32[4,36,16,1]{1,2,3,0:T(8,128)S(1)}, u32[]{:S(2)}, u32[]{:S(2)}) collective-permute-start(f32[4,36,16,1]{1,2,3,0:T(8,128)} %copy.50), channel_id=1, source_target_pairs={{0,2},{1,3},{4,6},{5,7},{8,10},{9,11},{12,14},{13,15},{16,18},{17,... | collective-permute-start | bytes 27656 | tf_op jit(solution)/shard_map/ppermute | solution.py:30
  62.2 20.2 %copy-start.13 = (f32[768,8]{0,1:T(8,128)S(1)}, f32[768,8]{0,1:T(8,128)}, u32[]{:S(2)}) copy-start(f32[768,8]{0,1:T(8,128)} %param.17) | copy-start | bytes 73732
  62.2 21.2 %copy-start.14 = (pred[768,8]{0,1:T(8,128)(4,1)S(1)}, pred[768,8]{0,1:T(8,128)(4,1)}, u32[]{:S(2)}) copy-start(pred[768,8]{0,1:T(8,128)(4,1)} %get-tuple-element.8) | copy-start | bytes 18436
  66.9 5.5 %collective-permute-start.11 = (f32[4,16,128]{2,1,0:T(8,128)S(1)}, f32[4,16,128]{2,1,0:T(8,128)S(1)}, u32[]{:S(2)}, u32[]{:S(2)}) collective-permute-start(f32[4,16,128]{2,1,0:T(8,128)S(1)} %bitcast.38), channel_id=1, source_target_pairs={{4,0},{8,4},{12,8},{0,12},{5,1},{9,5},{13,9},{1,13},{6,2},{10,6},{... | collective-permute-start | bytes 98312 | tf_op jit(solution)/shard_map/ppermute | solution.py:32
  70.8 5.7 %collective-permute-start.10 = (f32[4,16,128]{2,1,0:T(8,128)S(1)}, f32[4,16,128]{2,1,0:T(8,128)S(1)}, u32[]{:S(2)}, u32[]{:S(2)}) collective-permute-start(f32[4,16,128]{2,1,0:T(8,128)S(1)} %bitcast.39), channel_id=1, source_target_pairs={{0,4},{4,8},{8,12},{12,0},{1,5},{5,9},{9,13},{13,1},{2,6},{6,10},{... | collective-permute-start | bytes 98312 | tf_op jit(solution)/shard_map/ppermute | solution.py:30
  76.5 8.2 %collective-permute-start.13 = (f32[4,48,128]{2,1,0:T(8,128)S(1)}, f32[4,48,128]{2,1,0:T(8,128)S(1)}, u32[]{:S(2)}, u32[]{:S(2)}) collective-permute-start(f32[4,48,128]{2,1,0:T(8,128)S(1)} %pad_maximum_fusion.1), channel_id=1, source_target_pairs={{2,0},{3,1},{6,4},{7,5},{10,8},{11,9},{14,12},{15,13},{18,16},{19,... | collective-permute-start | bytes 294920 | tf_op jit(solution)/shard_map/ppermute | solution.py:32
  77.8 7.0 %collective-permute-start.12 = (f32[4,48,128]{2,1,0:T(8,128)S(1)}, f32[4,48,128]{2,1,0:T(8,128)S(1)}, u32[]{:S(2)}, u32[]{:S(2)}) collective-permute-start(f32[4,48,128]{2,1,0:T(8,128)S(1)} %pad_maximum_fusion.1), channel_id=1, source_target_pairs={{0,2},{1,3},{4,6},{5,7},{8,10},{9,11},{12,14},{13,15},{16,18},{17,... | collective-permute-start | bytes 294920 | tf_op jit(solution)/shard_map/ppermute | solution.py:30
where the time goes:
time: 119 us; the launch traced here: 118 us
  local copies, waits for them, and re-layouts  57.2 us (48%)
  starting transfers between devices  31.9 us (27%)
  other arithmetic  13.7 us (12%)
  matrix products  8.44 us (7%)
  waiting for transfers between devices  5.98 us (5%)
    gather x1, local copies, waits for them, and re-layouts, body(): jnp.take(flat_surface, local_index.reshape(-1), axis=1)  19.8 us
    ppermute x6, starting transfers between devices, extended(): lax.ppermute(head, axis, [((i + 1) % count, i) for i in range(ends)])  16.6 us
    ppermute x6, starting transfers between devices, extended(): lax.ppermute(tail, axis, [(i, (i + 1) % count) for i in range(ends)])  13.9 us
    dot_general x2, matrix products, convect(): jnp.einsum('lk,alxy->akxy', matrix, adjoint, precision=lax.Precision.HIGH...  8.44 us
    unnamed x36, local copies, waits for them, and re-layouts  6.99 us
    reduce_sum x1, other arithmetic, body(): sensed = jnp.sum(margin_weight[None] * values, axis=2)  6.14 us
    reshape x1, local copies, waits for them, and re-layouts, body(): flat_surface = rim_cells.reshape(per_device, 9 * width_x * width_y)  5.69 us
    sub x1, other arithmetic, combine(): center * rate_sum + east_rate * east - west_rate * west + north_rate * north  4.72 us
  transfers between devices with their start and end apart: 14, of which 3 were waited for; matrix products, arithmetic and copies ran while one was open for 20% of the time, Pallas kernels for 0%

commit v1 on v0

v1 whole, which is shorter than its diff:
```python
import functools

import jax
import jax.numpy as jnp
from jax import lax
from jax.experimental import pallas as pl
from jax.experimental.pallas import tpu as pltpu
from jax.sharding import PartitionSpec as P

ADJ = 8
NSTEP = 2
F32 = jnp.float32
BF16 = jnp.bfloat16


def vmem(value):
    return pltpu.with_memory_space_constraint(value, pltpu.VMEM)


def call(kernel, outs, args, scratch=(), hbm_out=(), name=None):
    out_shape = []
    out_specs = []
    for at, out in enumerate(outs):
        if at in hbm_out:
            out_shape.append(jax.ShapeDtypeStruct(out, F32))
            out_specs.append(pl.BlockSpec(memory_space=pl.ANY))
        else:
            out_shape.append(pltpu.VMEM(out, F32))
            out_specs.append(pl.BlockSpec(memory_space=pltpu.VMEM))
    return pl.pallas_call(
        kernel,
        out_shape=out_shape,
        in_specs=[pl.BlockSpec(memory_space=pltpu.VMEM)] * len(args),
        out_specs=out_specs,
        scratch_shapes=list(scratch),
        name=name,
    )(*[vmem(arg) for arg in args])


def split_matrix(matrix):
    lev = matrix.shape[0]
    turned = matrix.T
    high = turned.astype(BF16)
    high32 = high.astype(F32)
    low32 = turned - high32
    fill = jnp.zeros((-lev % 8, lev), F32)
    both = jnp.concatenate([high32, fill, low32, fill], axis=0).astype(BF16)
    return both, high


def mix(matrices, field):
    both, high_matrix = matrices
    lev = field.shape[0]
    pad = both.shape[0] // 2
    high = field.astype(BF16)
    low = (field - high.astype(F32)).astype(BF16)
    major = jnp.dot(both, high, preferred_element_type=F32)
    minor = jnp.dot(high_matrix, low, preferred_element_type=F32)
    return major[:lev] + (major[pad : pad + lev] + minor)


def lane_of(shape):
    return lax.broadcasted_iota(jnp.int32, shape, len(shape) - 1)


def turn(value, steps):
    steps = steps % value.shape[-1]
    return value if steps == 0 else pltpu.roll(value, steps, value.ndim - 1)


def column(ref, x, lev, width_x):
    return ref[pl.ds(x, lev, stride=width_x), :]


def pack_rim_kernel(lev, width_x, kernel_ref, wx_ref, wy_ref, innov_ref, cluster_ref, strength_ref, out_ref):
    lanes = kernel_ref.shape[1]
    pad = lev + -lev % 8
    half = 4 * width_x
    slot = lane_of((1, lanes)) // 4

    def packed(ref, first):
        total = jnp.zeros((lev, lanes), F32)
        for x in range(width_x):
            moved = turn(column(ref, x, lev, width_x), first + 4 * x + 2)
            total = jnp.where(slot == first // 4 + x, moved, total)
        return total

    def packed_row(value):
        total = jnp.zeros((1, lanes), F32)
        for x in range(width_x):
            total = jnp.where(slot == x, turn(value[x : x + 1], 4 * x + 2), total)
        return total

    upper = slot * 4 >= half
    out_ref[0:lev, :] = jnp.where(upper, packed(wy_ref, half), packed(kernel_ref, 0))
    out_ref[pad : pad + lev, :] = packed(wx_ref, 0)
    out_ref[2 * pad : 2 * pad + 1, :] = packed_row(innov_ref[...])
    out_ref[2 * pad + 1 : 2 * pad + 2, :] = packed_row(cluster_ref[...].astype(F32))
    out_ref[2 * pad + 2 : 2 * pad + 3, :] = packed_row(strength_ref[...])


def first_mix_kernel(lev, width_x, kernel_ref, innov_ref, strength_ref, matrix_ref, out_ref):
    matrices = split_matrix(matrix_ref[...])
    for x in range(0, width_x, 2):
        tiles = [column(kernel_ref, at, lev, width_x) * innov_ref[at : at + 1, :] for at in (x, x + 1)]
        lanes = tiles[0].shape[1]
        mixed = mix(matrices, jnp.concatenate(tiles, axis=1))
        for k, tile in enumerate(tiles):
            part = mixed[:, k * lanes : (k + 1) * lanes]
            out_ref[x + k, 0:lev, :] = tile + strength_ref[x + k : x + k + 1, :] * (part - tile)


def pack_ends_kernel(
    lev,
    width_x,
    subs,
    own_ref,
    south_ref,
    north_ref,
    c_ref,
    wx_ref,
    wy_ref,
    cluster_ref,
    strength_ref,
    matrix_ref,
    rim_ref,
    east_ref,
    west_ref,
):
    lanes = wx_ref.shape[1]
    pad = lev + -lev % 8
    half = 4 * width_x
    cross = lax.axis_index("sub")
    lane = lane_of((1, lanes))
    lower = lane < half
    southern = lane % 4 < 2
    present = jnp.where(southern, cross, subs - 1 - cross) > 0

    def halo(rows):
        value = jnp.where(southern, south_ref[rows, :], north_ref[rows, :])
        return jnp.where(present, value, 0.0)

    own = own_ref[0:lev, :]
    far = halo(slice(0, lev))
    far_misc = halo(slice(2 * pad, 2 * pad + 3))
    own_misc = own_ref[2 * pad : 2 * pad + 3, :]
    sources = [
        jnp.where(lower, own, 0.0) * own_misc[0:1],
        jnp.where(lower, far, 0.0) * far_misc[0:1],
    ]
    mixed = mix(split_matrix(matrix_ref[...]), jnp.concatenate(sources, axis=1))
    rim_c = sources[0] + own_misc[2:3] * (mixed[:, :lanes] - sources[0])
    far_c = sources[1] + far_misc[2:3] * (mixed[:, lanes:] - sources[1])
    own_wy = jnp.where(lower, turn(own, half), 0.0)
    far_wy = jnp.where(lower, turn(far, half), 0.0)
    far_wx = halo(slice(pad, pad + lev))
    for at, value in enumerate((rim_c, far_c, own_wy, far_wy, far_wx)):
        rim_ref[at * pad : at * pad + lev, :] = value
    base = 5 * pad
    rim_ref[base : base + 1, :] = own_misc[1:2]
    rim_ref[base + 1 : base + 2, :] = far_misc[1:2]
    rim_ref[base + 2 : base + 3, :] = far_misc[2:3]

    last = width_x - 1
    cluster = cluster_ref[...].astype(F32)
    corner_lane = lane // 4

    def corner(slot):
        away = -4 * slot
        value = turn(far_c, away)
        value = jnp.where(corner_lane == 1, turn(far_wy, away + 4), value)
        return jnp.where(corner_lane == 2, turn(far_wx, away + 8), value)

    def put(ref, tiles, near, next_one):
        for at, value in enumerate(tiles):
            ref[at * pad : at * pad + lev, :] = value
        base = len(tiles) * pad
        ref[base : base + 1, :] = cluster[near : near + 1]
        ref[base + 1 : base + 2, :] = cluster[next_one : next_one + 1]
        ref[base + 2 : base + 3, :] = strength_ref[near : near + 1, :]
        ref[base + 3 : base + 4, :] = turn(far_misc[1:2], -4 * near)

    put(
        east_ref,
        (
            c_ref[last, 0:lev, :],
            c_ref[last - 1, 0:lev, :],
            column(wx_ref, last, lev, width_x),
            column(wy_ref, last, lev, width_x),
            corner(last),
            column(wx_ref, last - 1, lev, width_x),
        ),
        last,
        last - 1,
    )
    put(
        west_ref,
        (
            c_ref[0, 0:lev, :],
            c_ref[1, 0:lev, :],
            column(wx_ref, 0, lev, width_x),
            column(wy_ref, 0, lev, width_x),
            corner(0),
        ),
        0,
        1,
    )


def steps_kernel(
    lev,
    width_x,
    subs,
    per_device,
    rim_ref,
    before_ref,
    after_ref,
    c_ref,
    wx_ref,
    wy_ref,
    cluster_ref,
    strength_ref,
    matrix_ref,
    out_ref,
    surface_ref,
    mixed_ref,
    field_ref,
    sem,
):
    lanes = wx_ref.shape[1]
    pad = lev + -lev % 8
    half = 4 * width_x
    cross = lax.axis_index("sub")
    first_id = (lax.axis_index("adj") * per_device).astype(F32)
    matrices = split_matrix(matrix_ref[...])
    lane = lane_of((1, lanes))
    place = lane % 4
    cluster = cluster_ref[...].astype(F32)

    def rows_of(ref, at):
        return ref[at * pad : at * pad + lev, :]

    before_base = 6 * pad
    after_base = 5 * pad
    rim_base = 5 * pad
    after_slot = lane // 4 == width_x
    before_slot = lane >= lanes - 4

    def with_corners(value, before, after):
        return jnp.where(before_slot, before, jnp.where(after_slot, after, value))

    corner_before = rows_of(before_ref, 4)
    corner_after = rows_of(after_ref, 4)
    rim_c = rows_of(rim_ref, 0)
    rim_wy = rows_of(rim_ref, 2)
    far_c = with_corners(rows_of(rim_ref, 1), turn(corner_before, -4), turn(corner_after, half))
    far_wy = with_corners(rows_of(rim_ref, 3), turn(corner_before, -8), turn(corner_after, half - 4))
    far_wx = jnp.where(before_slot, turn(corner_before, -12), rows_of(rim_ref, 4))
    rim_cluster = rim_ref[rim_base : rim_base + 1, :]
    far_cluster = with_corners(
        rim_ref[rim_base + 1 : rim_base + 2, :],
        turn(before_ref[before_base + 3 : before_base + 4, :], -4),
        turn(after_ref[after_base + 3 : after_base + 4, :], half),
    )
    far_strength = rim_ref[rim_base + 2 : rim_base + 3, :]

    def tile(ref, x):
        return column(ref, x, lev, width_x)

    def c_at(x):
        if x < 0:
            return rows_of(before_ref, -1 - x)
        if x >= width_x:
            return rows_of(after_ref, x - width_x)
        return c_ref[x, 0:lev, :]

    def wx_at(x):
        if x < 0:
            return rows_of(before_ref, 2 if x == -1 else 5)
        return rows_of(after_ref, 2) if x >= width_x else tile(wx_ref, x)

    def wy_at(x):
        if x < 0:
            return rows_of(before_ref, 3)
        return rows_of(after_ref, 3) if x >= width_x else tile(wy_ref, x)

    def cluster_at(x):
        if x < 0:
            return before_ref[before_base - 1 - x : before_base - x, :]
        if x >= width_x:
            at = after_base + x - width_x
            return after_ref[at : at + 1, :]
        return cluster[x : x + 1]

    def strength_at(x):
        if x < 0:
            return before_ref[before_base + 2 : before_base + 3, :]
        if x >= width_x:
            return after_ref[after_base + 2 : after_base + 3, :]
        return strength_ref[x : x + 1, :]

    def from_north(value, rim):
        return turn(jnp.where(lane == 0, rim, value), -1)

    def from_south(value, rim):
        return turn(jnp.where(lane == lanes - 1, rim, value), 1)

    def rates(wx, wx_west, wy, wy_south):
        east = jnp.maximum(wx, 0.0)
        west = jnp.maximum(-wx_west, 0.0)
        north = jnp.maximum(wy, 0.0)
        south = jnp.maximum(-wy_south, 0.0)
        return 1.0 - east - west - north - south, east, west, north, south

    def rates_at(x):
        wy = wy_at(x)
        return rates(wx_at(x), wx_at(x - 1), wy, from_south(wy, turn(far_wy, -4 * x - 2)))

    def parted(terms, clusters):
        fields = []
        for a in range(per_device):
            wanted = first_id + a
            parts = [jnp.where(where == wanted, term, 0.0) for term, where in zip(terms, clusters)]
            fields.append(((parts[0] + parts[1]) + (parts[2] + parts[3])) + parts[4])
        return fields

    def convect(fields, strength):
        mixed = mix(matrices, jnp.concatenate(fields, axis=1))
        return [f + strength * (mixed[:, k * lanes : (k + 1) * lanes] - f) for k, f in enumerate(fields)]

    for x in range(-1, width_x + 1):
        center, east, west, north, south = rates_at(x)
        own, own_cluster = c_at(x), cluster_at(x)
        rim = turn(far_c, -4 * x - 2)
        rim_row = turn(far_cluster, -4 * x - 2)
        terms = (
            center * own,
            east * c_at(x + 1),
            west * c_at(x - 1),
            north * from_north(own, rim),
            south * from_south(own, rim),
        )
        clusters = (
            own_cluster,
            cluster_at(x + 1),
            cluster_at(x - 1),
            from_north(own_cluster, rim_row),
            from_south(own_cluster, rim_row),
        )
        for a, value in enumerate(convect(parted(terms, clusters), strength_at(x))):
            mixed_ref[a, x + 1, 0:lev, :] = value

    def rim_north(far, own):
        return turn(jnp.where(place == 2, own, far), -1)

    def rim_south(far, own):
        return turn(jnp.where(place == 1, own, far), 1)

    center, east, west, north, south = rates(far_wx, turn(far_wx, 4), far_wy, rim_south(far_wy, rim_wy))
    terms = (
        center * far_c,
        east * turn(far_c, -4),
        west * turn(far_c, 4),
        north * rim_north(far_c, rim_c),
        south * rim_south(far_c, rim_c),
    )
    clusters = (
        far_cluster,
        turn(far_cluster, -4),
        turn(far_cluster, 4),
        rim_north(far_cluster, rim_cluster),
        rim_south(far_cluster, rim_cluster),
    )
    inside = jnp.where(lane < half, jnp.where(place < 2, cross, subs - 1 - cross), 0) > 0
    fields = [jnp.where(inside, f, 0.0) for f in parted(terms, clusters)]
    joined = [fields[a] + turn(fields[a + 1], half) for a in range(0, per_device, 2)]
    far_mixed = convect(joined, far_strength + turn(far_strength, half))

    copies = []
    for a in range(per_device):
        rim_field = far_mixed[a // 2]
        for x in range(width_x):
            center, east, west, north, south = rates_at(x)
            own = mixed_ref[a, x + 1, 0:lev, :]
            rim = turn(rim_field, -4 * x - 2 - half * (a % 2))
            value = (
                (center * own + east * mixed_ref[a, x + 2, 0:lev, :])
                + (west * mixed_ref[a, x, 0:lev, :] + north * from_north(own, rim))
                + south * from_south(own, rim)
            )
            field_ref[pl.ds(a * lev * width_x + x, lev, stride=width_x), :] = value
            surface_ref[a * width_x + x : a * width_x + x + 1, :] = value[0:1]
        rows = pl.ds(a * lev * width_x, lev * width_x)
        copies.append(pltpu.make_async_copy(field_ref.at[rows, :], out_ref.at[rows, :], sem.at[a]))
        copies[-1].start()
    for copy in copies:
        copy.wait()


def quotient(value, count):
    if count & (count - 1) == 0:
        return value >> (count.bit_length() - 1), value & (count - 1)
    return lax.div(value, count), lax.rem(value, count)


def sense_kernel(width_x, width_y, tiles, subs, per_device, n_rim, cell_ref, weight_ref, *refs):
    *blocks, out_ref = refs
    slots, elements = cell_ref.shape
    tile_pos = lax.axis_index("tiles")
    cross = lax.axis_index("sub")
    group = width_y
    rows = per_device * width_x

    def one_group(g, carry):
        lanes = pl.ds(pl.multiple_of(g * group, group), group)
        cell = cell_ref[:, lanes]
        weight = weight_ref[:, lanes]
        column_x, row_y = quotient(cell, width_y * subs)
        block_x, inner_x = quotient(column_x, width_x)
        block_y, lane_y = quotient(row_y, width_y)
        step = block_x - tile_pos
        step = jnp.where(step < -1, step + tiles, jnp.where(step > 1, step - tiles, step))
        if n_rim == 2:
            side = jnp.where(block_y == cross, 0, 1)
        else:
            side = block_y - cross + 1
        row_id = ((step + 1) * n_rim + side) * width_x + inner_x
        sums = [jnp.zeros((8, group), F32) for _ in range(per_device)]
        within = lax.broadcasted_iota(jnp.int32, (8, group), 0)
        for k in range(slots):
            pick = jnp.broadcast_to(lane_y[k : k + 1], (8, group))
            row = jnp.broadcast_to(row_id[k : k + 1], (8, group))
            share = jnp.broadcast_to(weight[k : k + 1], (8, group))
            for at in range(3 * n_rim):
                ref, base = blocks[at]
                for part in range(0, width_x, 8):
                    chosen = jnp.where(row == within + (at * width_x + part), share, 0.0)
                    for a in range(per_device):
                        first = base + a * width_x + part
                        value = jnp.take_along_axis(ref[first : first + 8, :], pick, axis=1)
                        sums[a] = sums[a] + chosen * value
        out_ref[:, lanes] = jnp.concatenate([jnp.sum(s, axis=0, keepdims=True) for s in sums], axis=0)
        return carry

    lax.fori_loop(0, elements // group, one_group, 0)


def ring(value, axis, steps):
    count = lax.axis_size(axis)
    return lax.ppermute(value, axis, [(i, (i + steps) % count) for i in range(count)])


def across(value):
    count = lax.axis_size("sub")
    if count == 2:
        other = ring(value, "sub", 1)
        return other, other
    from_south = lax.ppermute(value, "sub", [(i, i + 1) for i in range(count - 1)])
    from_north = lax.ppermute(value, "sub", [(i + 1, i) for i in range(count - 1)])
    return from_south, from_north


def body(
    innovation,
    cluster,
    kernel,
    wind_x,
    wind_y,
    conv_strength,
    conv_matrix,
    margin_cell,
    margin_weight,
):
    lev, width_x, width_y = kernel.shape
    tiles = lax.axis_size("tiles")
    subs = lax.axis_size("sub")
    per_device = ADJ // lax.axis_size("adj")
    pad = lev + -lev % 8
    flat_kernel = kernel.reshape(lev * width_x, width_y)
    flat_x = wind_x.reshape(lev * width_x, width_y)
    flat_y = wind_y.reshape(lev * width_x, width_y)

    (own_rim,) = call(
        functools.partial(pack_rim_kernel, lev, width_x),
        [(2 * pad + 8, width_y)],
        (flat_kernel, flat_x, flat_y, innovation, cluster, conv_strength),
        name="pack_rim",
    )
    south_rim, north_rim = across(own_rim)
    (first,) = call(
        functools.partial(first_mix_kernel, lev, width_x),
        [(width_x, pad, width_y)],
        (flat_kernel, innovation, conv_strength, conv_matrix),
        name="first_mix",
    )
    rim, to_east, to_west = call(
        functools.partial(pack_ends_kernel, lev, width_x, subs),
        [(5 * pad + 8, width_y), (6 * pad + 8, width_y), (5 * pad + 8, width_y)],
        (own_rim, south_rim, north_rim, first, flat_x, flat_y, cluster, conv_strength, conv_matrix),
        name="pack_ends",
    )
    before = ring(to_east, "tiles", 1)
    after = ring(to_west, "tiles", -1)
    field, surface = call(
        functools.partial(steps_kernel, lev, width_x, subs, per_device),
        [(per_device * lev * width_x, width_y), (per_device * width_x, width_y)],
        (rim, before, after, first, flat_x, flat_y, cluster, conv_strength, conv_matrix),
        scratch=(
            pltpu.VMEM((per_device, width_x + 2, pad, width_y), F32),
            pltpu.VMEM((per_device * lev * width_x, width_y), F32),
            pltpu.SemaphoreType.DMA((per_device,)),
        ),
        hbm_out=(0,),
        name="steps",
    )
    south_surface, north_surface = across(surface)
    if subs == 2:
        strip = [surface, south_surface]
    else:
        strip = [south_surface, surface, north_surface]
    n_rim = len(strip)
    whole = jnp.concatenate(strip, axis=0)
    surface_before = ring(whole, "tiles", 1)
    surface_after = ring(whole, "tiles", -1)
    rows = per_device * width_x

    def sense(cell_ref, weight_ref, before_ref, after_ref, *rest):
        *here, out_ref = rest
        blocks = [(before_ref, k * rows) for k in range(n_rim)]
        blocks += [(ref, 0) for ref in here]
        blocks += [(after_ref, k * rows) for k in range(n_rim)]
        sense_kernel(width_x, width_y, tiles, subs, per_device, n_rim, cell_ref, weight_ref, *blocks, out_ref)

    (sensed,) = call(
        sense,
        [(per_device, margin_cell.shape[0])],
        (margin_cell.T, margin_weight.T, surface_before, surface_after, *strip),
        name="sense",
    )
    return (field.reshape(per_device, lev, width_x, width_y), sensed)


def solution(mesh):
    in_specs = (
        P(("groups", "tiles"), "sub"),
        P(("groups", "tiles"), "sub"),
        P(None, "tiles", "sub"),
        P(None, "tiles", "sub"),
        P(None, "tiles", "sub"),
        P("tiles", "sub"),
        P(),
        P(("tiles", "sub"), None),
        P(("tiles", "sub"), None),
    )
    out_specs = (P(("groups", "adj"), None, "tiles", "sub"), P(("groups", "adj"), ("tiles", "sub")))
    return jax.shard_map(body, mesh=mesh, in_specs=in_specs, out_specs=out_specs, check_vma=False)
```

time: 119 us -> 45 us (0.38)
  local copies, waits for them, and re-layouts: 57.2 us -> 6.32 us
  starting transfers between devices: 31.9 us -> 11.7 us
  other arithmetic: 13.7 us -> 0 us
  Pallas kernels: 0 us -> 12.5 us
  matrix products: 8.44 us -> 0 us
  waiting for transfers between devices: 5.98 us -> 13.4 us
    ppermute x14 -> x6, starting transfers between devices: 31.9 us -> 11.7 us  [ring(): lax.ppermute(value, axis, [(i, (i + steps) % count) for i in range(count)])]
    gather x1 -> x0, local copies, waits for them, and re-layouts: 19.8 us -> none  [body(): jnp.take(flat_surface, local_index.reshape(-1), axis=1)]
    slice x15 -> x0, local copies, waits for them, and re-layouts: 17 us -> none  [the longest x4 4.67 us: body(): adjoint[:, :, :, -1:]]
    pallas_call x0 -> x5, Pallas kernels: none -> 12.5 us  [call(): pl.pallas_call(kernel, out_shape=out_shape, in_specs=[pl.BlockSpec(memory...]
    dot_general x2 -> x0, matrix products: 8.44 us -> none  [convect(): jnp.einsum('lk,alxy->akxy', matrix, adjoint, precision=lax.Precision.HIGH...]
    ppermute x14 -> x6, waiting for transfers between devices: 5.98 us -> 13.4 us  [ring(): lax.ppermute(value, axis, [(i, (i + steps) % count) for i in range(count)])]
    ppermute x4 -> x0, local copies, waits for them, and re-layouts: 6.63 us -> none  [the longest x2 3.35 us: extended(): lax.ppermute(tail, axis, [(i, (i + 1) % count) for i in range(ends)])]
    reduce_sum x1 -> x0, other arithmetic: 6.14 us -> none  [body(): sensed = jnp.sum(margin_weight[None] * values, axis=2)]
  transfers between devices with their start and end apart: 14 -> 6, of which waited for: 3 -> 5; matrix products, arithmetic and copies ran while one was open for 20% -> 0% of each run, Pallas kernels for 0% -> 1%
where the time goes in v1:
time: 45 us; the launch traced here: 44.6 us
  waiting for transfers between devices  13.4 us (30%)
  Pallas kernels  12.5 us (28%)
  starting transfers between devices  11.7 us (26%)
  local copies, waits for them, and re-layouts  6.32 us (14%)
  between operations  0.71 us (2%)
    ppermute x6, waiting for transfers between devices, ring(): lax.ppermute(value, axis, [(i, (i + steps) % count) for i in range(count)])  13.4 us
    pallas_call x5, Pallas kernels, call(): pl.pallas_call(kernel, out_shape=out_shape, in_specs=[pl.BlockSpec(memory...  12.5 us
    ppermute x6, starting transfers between devices, ring(): lax.ppermute(value, axis, [(i, (i + steps) % count) for i in range(count)])  11.7 us
    unnamed x24, local copies, waits for them, and re-layouts  6.32 us
  transfers between devices with their start and end apart: 6, of which 5 were waited for; matrix products, arithmetic and copies ran while one was open for 0% of the time, Pallas kernels for 1%

profile of v1, /device:TPU:0, one launch (start us, length us, event | category | flops | bytes accessed | tf_op | source)
XLA Modules:
  0.0 44.6 jit_solution(11418072115955790702)
XLA Ops:
  0.6 0.0 copy-start
  0.6 1.0 %copy-done = f32[36,16,128]{2,1,0:T(8,128)S(1)} copy-done((f32[36,16,128]{2,1,0:T(8,128)S(1)}, f32[36,16,128]{2,1,0:T(8,128)}, u32[]{:S(2)}) %copy-start) | copy-done | bytes 294936
  1.6 0.0 copy-start.2
  1.6 1.0 %copy-done.2 = f32[36,16,128]{2,1,0:T(8,128)S(1)} copy-done((f32[36,16,128]{2,1,0:T(8,128)S(1)}, f32[36,16,128]{2,1,0:T(8,128)}, u32[]{:S(2)}) %copy-start.2) | copy-done | bytes 294936
  2.6 0.0 copy-start.4
  2.6 1.0 %copy-done.4 = f32[36,16,128]{2,1,0:T(8,128)S(1)} copy-done((f32[36,16,128]{2,1,0:T(8,128)S(1)}, f32[36,16,128]{2,1,0:T(8,128)}, u32[]{:S(2)}) %copy-start.4) | copy-done | bytes 294936
  3.5 0.0 copy-start.6
  3.5 0.7 %copy-done.6 = f32[16,128]{1,0:T(8,128)S(1)} copy-done((f32[16,128]{1,0:T(8,128)S(1)}, f32[16,128]{1,0:T(8,128)}, u32[]{:S(2)}) %copy-start.6) | copy-done | bytes 8216
  4.2 0.0 copy-start.7
  4.2 0.7 %copy-done.7 = s32[16,128]{1,0:T(8,128)S(1)} copy-done((s32[16,128]{1,0:T(8,128)S(1)}, s32[16,128]{1,0:T(8,128)}, u32[]{:S(2)}) %copy-start.7) | copy-done | bytes 8216
  4.9 0.0 copy-start.8
  4.9 0.7 %copy-done.8 = f32[16,128]{1,0:T(8,128)S(1)} copy-done((f32[16,128]{1,0:T(8,128)S(1)}, f32[16,128]{1,0:T(8,128)}, u32[]{:S(2)}) %copy-start.8) | copy-done | bytes 8216
  5.6 0.0 copy-start.1
  5.6 0.0 copy-start.3
  5.6 0.4 pack_rim.1.own_ref
  6.0 3.0 %collective-permute-start = (f32[88,128]{1,0:T(8,128)S(1)}, f32[88,128]{1,0:T(8,128)S(1)}, u32[]{:S(2)}, u32[]{:S(2)}) collective-permute-start(f32[88,128]{1,0:T(8,128)S(1)} %pack_rim.1.own_ref), channel_id=1, source_target_pairs={{0,2},{2,0},{1,3},{3,1},{4,6},{6,4},{5,7},{7,5},{8,10},{10,8},{9,1... | collective-permute-start | bytes 135176 | tf_op jit(solution)/shard_map/ppermute | solution.py:450
  9.0 0.0 copy-start.5
  9.0 0.7 %copy-done.5 = f32[36,36]{1,0:T(8,128)S(1)} copy-done((f32[36,36]{1,0:T(8,128)S(1)}, f32[36,36]{1,0:T(8,128)}, u32[]{:S(2)}) %copy-start.5) | copy-done | bytes 5208
  9.8 0.3 first_mix.1.c_ref
  10.1 0.0 copy-start.9
  10.1 0.0 copy-start.10
  10.2 0.9 %collective-permute-done.south_ref.north_ref = f32[88,128]{1,0:T(8,128)S(1)} collective-permute-done((f32[88,128]{1,0:T(8,128)S(1)}, f32[88,128]{1,0:T(8,128)S(1)}, u32[]{:S(2)}, u32[]{:S(2)}) %collective-permute-start) | collective-permute-done | bytes 45088 | tf_op jit(solution)/shard_map/ppermute | solution.py:450
  11.1 0.0 copy-done.1
  11.1 0.0 copy-done.3
  11.1 0.3 pack_ends.1
  11.4 2.2 %collective-permute-start.1 = (f32[248,128]{1,0:T(8,128)S(1)}, f32[248,128]{1,0:T(8,128)S(1)}, u32[]{:S(2)}, u32[]{:S(2)}) collective-permute-start(f32[248,128]{1,0:T(8,128)S(1)} %get-tuple-element.8), channel_id=1, source_target_pairs={{0,4},{4,8},{8,12},{12,0},{1,5},{5,9},{9,13},{13,1},{2,6},{6,10},{... | collective-permute-start | bytes 380936 | tf_op jit(solution)/shard_map/ppermute | solution.py:450
  13.5 2.1 %collective-permute-start.2 = (f32[208,128]{1,0:T(8,128)S(1)}, f32[208,128]{1,0:T(8,128)S(1)}, u32[]{:S(2)}, u32[]{:S(2)}) collective-permute-start(f32[208,128]{1,0:T(8,128)S(1)} %get-tuple-element.9), channel_id=1, source_target_pairs={{0,12},{4,0},{8,4},{12,8},{1,13},{5,1},{9,5},{13,9},{2,14},{6,2},{... | collective-permute-start | bytes 319496 | tf_op jit(solution)/shard_map/ppermute | solution.py:450
  15.6 4.0 %collective-permute-done.2.after_ref = f32[208,128]{1,0:T(8,128)S(1)} collective-permute-done((f32[208,128]{1,0:T(8,128)S(1)}, f32[208,128]{1,0:T(8,128)S(1)}, u32[]{:S(2)}, u32[]{:S(2)}) %collective-permute-start.2) | collective-permute-done | bytes 106528 | tf_op jit(solution)/shard_map/ppermute | solution.py:450
  19.6 0.0 collective-permute-done.1.before_ref
  19.6 8.4 %steps.1 = (f32[2304,128]{1,0:T(8,128)}, f32[64,128]{1,0:T(8,128)S(1)}) custom-call(f32[208,128]{1,0:T(8,128)S(1)} %get-tuple-element.7.rim_ref, f32[248,128]{1,0:T(8,128)S(1)} %collective-permute-done.1.before_ref, f32[208,128]{1,0:T(8,128)S(1)} %collective-permute-done.2.after_ref, f32[16,40,128]{2,1,0:T(8,128)S(1)} %first_mix.1.c_ref, ...), custom_call_target="tpu_custom_call" | custom-call | tf_op jit(solution)/shard_map/steps/pallas_call | solution.py:30
  28.0 1.6 %collective-permute-start.3 = (f32[64,128]{1,0:T(8,128)S(1)}, f32[64,128]{1,0:T(8,128)S(1)}, u32[]{:S(2)}, u32[]{:S(2)}) collective-permute-start(f32[64,128]{1,0:T(8,128)S(1)} %get-tuple-element.11.rest_0_), channel_id=1, source_target_pairs={{0,2},{2,0},{1,3},{3,1},{4,6},{6,4},{5,7},{7,5},{8,10},{10,8},{9,1... | collective-permute-start | bytes 98312 | tf_op jit(solution)/shard_map/ppermute | solution.py:450
  29.6 2.4 %collective-permute-done.3.rest_1_ = f32[64,128]{1,0:T(8,128)S(1)} collective-permute-done((f32[64,128]{1,0:T(8,128)S(1)}, f32[64,128]{1,0:T(8,128)S(1)}, u32[]{:S(2)}, u32[]{:S(2)}) %collective-permute-start.3) | collective-permute-done | bytes 32800 | tf_op jit(solution)/shard_map/ppermute | solution.py:450
  32.0 2.9 %collective-permute-start.5 = (f32[128,128]{1,0:T(8,128)S(1)}, f32[128,128]{1,0:T(8,128)S(1)}, u32[]{:S(2)}, u32[]{:S(2)}) collective-permute-start(f32[128,128]{1,0:T(8,128)S(1)} %constant_dynamic-update-slice_fusion), channel_id=1, source_target_pairs={{0,12},{4,0},{8,4},{12,8},{1,13},{5,1},{9,5},{13,9},{2,14},{6,2},{... | collective-permute-start | bytes 196616 | tf_op jit(solution)/shard_map/ppermute | solution.py:450
  34.8 0.0 collective-permute-start.4
  34.8 2.1 %collective-permute-done.5.after_ref = f32[128,128]{1,0:T(8,128)S(1)} collective-permute-done((f32[128,128]{1,0:T(8,128)S(1)}, f32[128,128]{1,0:T(8,128)S(1)}, u32[]{:S(2)}, u32[]{:S(2)}) %collective-permute-start.5) | collective-permute-done | bytes 65568 | tf_op jit(solution)/shard_map/ppermute | solution.py:450
  37.0 4.0 %collective-permute-done.4.before_ref = f32[128,128]{1,0:T(8,128)S(1)} collective-permute-done((f32[128,128]{1,0:T(8,128)S(1)}, f32[128,128]{1,0:T(8,128)S(1)}, u32[]{:S(2)}, u32[]{:S(2)}) %collective-permute-start.4) | collective-permute-done | bytes 65568 | tf_op jit(solution)/shard_map/ppermute | solution.py:450
  40.9 0.0 copy-done.9
  40.9 0.0 copy-done.10
  40.9 3.1 %sense.1 = f32[4,768]{1,0:T(4,128)S(1)} custom-call(s32[8,768]{1,0:T(8,128)S(1)} %bitcast.14, f32[8,768]{1,0:T(8,128)S(1)} %bitcast.15, f32[128,128]{1,0:T(8,128)S(1)} %collective-permute-done.4.before_ref, f32[128,128]{1,0:T(8,128)S(1)} %collective-permute-done.5.after_ref, f32[64,128]{1,0:T(8,128)S(1)} %get-tuple-element.11.rest_0_, ...), custom_call_target="tpu_custom_call" | custom-call | tf_op jit(solution)/shard_map/sense/pallas_call | solution.py:30
  44.0 0.6 %copy.12 = f32[4,768]{1,0:T(4,128)} copy(f32[4,768]{1,0:T(4,128)S(1)} %sense.1) | data formatting | bytes 24576
  (2 shorter events, 0.0 us)
Async XLA Ops:
  0.6 1.0 %copy-start = (f32[36,16,128]{2,1,0:T(8,128)S(1)}, f32[36,16,128]{2,1,0:T(8,128)}, u32[]{:S(2)}) copy-start(f32[36,16,128]{2,1,0:T(8,128)} %param.12) | copy-start | bytes 884740
  1.6 1.0 %copy-start.2 = (f32[36,16,128]{2,1,0:T(8,128)S(1)}, f32[36,16,128]{2,1,0:T(8,128)}, u32[]{:S(2)}) copy-start(f32[36,16,128]{2,1,0:T(8,128)} %param.13) | copy-start | bytes 884740
  2.6 1.0 %copy-start.4 = (f32[36,16,128]{2,1,0:T(8,128)S(1)}, f32[36,16,128]{2,1,0:T(8,128)}, u32[]{:S(2)}) copy-start(f32[36,16,128]{2,1,0:T(8,128)} %param.11) | copy-start | bytes 884740
  3.5 0.7 %copy-start.6 = (f32[16,128]{1,0:T(8,128)S(1)}, f32[16,128]{1,0:T(8,128)}, u32[]{:S(2)}) copy-start(f32[16,128]{1,0:T(8,128)} %strength_ref.7) | copy-start | bytes 24580
  4.2 0.7 %copy-start.7 = (s32[16,128]{1,0:T(8,128)S(1)}, s32[16,128]{1,0:T(8,128)}, u32[]{:S(2)}) copy-start(s32[16,128]{1,0:T(8,128)} %cluster_ref.5) | copy-start | bytes 24580
  4.9 0.7 %copy-start.8 = (f32[16,128]{1,0:T(8,128)S(1)}, f32[16,128]{1,0:T(8,128)}, u32[]{:S(2)}) copy-start(f32[16,128]{1,0:T(8,128)} %innov_ref.3) | copy-start | bytes 24580
  5.6 5.5 %copy-start.1 = (f32[36,16,128]{2,1,0:T(8,128)S(1)}, f32[36,16,128]{2,1,0:T(8,128)}, u32[]{:S(2)}) copy-start(f32[36,16,128]{2,1,0:T(8,128)} %param.12) | copy-start | bytes 884740
  5.6 5.5 %copy-start.3 = (f32[36,16,128]{2,1,0:T(8,128)S(1)}, f32[36,16,128]{2,1,0:T(8,128)}, u32[]{:S(2)}) copy-start(f32[36,16,128]{2,1,0:T(8,128)} %param.13) | copy-start | bytes 884740
  6.0 5.1 %collective-permute-start = (f32[88,128]{1,0:T(8,128)S(1)}, f32[88,128]{1,0:T(8,128)S(1)}, u32[]{:S(2)}, u32[]{:S(2)}) collective-permute-start(f32[88,128]{1,0:T(8,128)S(1)} %pack_rim.1.own_ref), channel_id=1, source_target_pairs={{0,2},{2,0},{1,3},{3,1},{4,6},{6,4},{5,7},{7,5},{8,10},{10,8},{9,1... | collective-permute-start | bytes 135176 | tf_op jit(solution)/shard_map/ppermute | solution.py:450
  9.0 0.7 %copy-start.5 = (f32[36,36]{1,0:T(8,128)S(1)}, f32[36,36]{1,0:T(8,128)}, u32[]{:S(2)}) copy-start(f32[36,36]{1,0:T(8,128)} %matrix_ref.5) | copy-start | bytes 15556
  10.1 30.8 %copy-start.9 = (s32[768,8]{0,1:T(8,128)S(1)}, s32[768,8]{0,1:T(8,128)}, u32[]{:S(2)}) copy-start(s32[768,8]{0,1:T(8,128)} %param.16) | copy-start | bytes 73732
  10.1 30.8 %copy-start.10 = (f32[768,8]{0,1:T(8,128)S(1)}, f32[768,8]{0,1:T(8,128)}, u32[]{:S(2)}) copy-start(f32[768,8]{0,1:T(8,128)} %param.17) | copy-start | bytes 73732
  11.4 8.2 %collective-permute-start.1 = (f32[248,128]{1,0:T(8,128)S(1)}, f32[248,128]{1,0:T(8,128)S(1)}, u32[]{:S(2)}, u32[]{:S(2)}) collective-permute-start(f32[248,128]{1,0:T(8,128)S(1)} %get-tuple-element.8), channel_id=1, source_target_pairs={{0,4},{4,8},{8,12},{12,0},{1,5},{5,9},{9,13},{13,1},{2,6},{6,10},{... | collective-permute-start | bytes 380936 | tf_op jit(solution)/shard_map/ppermute | solution.py:450
  13.5 6.1 %collective-permute-start.2 = (f32[208,128]{1,0:T(8,128)S(1)}, f32[208,128]{1,0:T(8,128)S(1)}, u32[]{:S(2)}, u32[]{:S(2)}) collective-permute-start(f32[208,128]{1,0:T(8,128)S(1)} %get-tuple-element.9), channel_id=1, source_target_pairs={{0,12},{4,0},{8,4},{12,8},{1,13},{5,1},{9,5},{13,9},{2,14},{6,2},{... | collective-permute-start | bytes 319496 | tf_op jit(solution)/shard_map/ppermute | solution.py:450
  28.0 4.0 %collective-permute-start.3 = (f32[64,128]{1,0:T(8,128)S(1)}, f32[64,128]{1,0:T(8,128)S(1)}, u32[]{:S(2)}, u32[]{:S(2)}) collective-permute-start(f32[64,128]{1,0:T(8,128)S(1)} %get-tuple-element.11.rest_0_), channel_id=1, source_target_pairs={{0,2},{2,0},{1,3},{3,1},{4,6},{6,4},{5,7},{7,5},{8,10},{10,8},{9,1... | collective-permute-start | bytes 98312 | tf_op jit(solution)/shard_map/ppermute | solution.py:450
  32.0 5.0 %collective-permute-start.5 = (f32[128,128]{1,0:T(8,128)S(1)}, f32[128,128]{1,0:T(8,128)S(1)}, u32[]{:S(2)}, u32[]{:S(2)}) collective-permute-start(f32[128,128]{1,0:T(8,128)S(1)} %constant_dynamic-update-slice_fusion), channel_id=1, source_target_pairs={{0,12},{4,0},{8,4},{12,8},{1,13},{5,1},{9,5},{13,9},{2,14},{6,2},{... | collective-permute-start | bytes 196616 | tf_op jit(solution)/shard_map/ppermute | solution.py:450
  34.8 6.1 %collective-permute-start.4 = (f32[128,128]{1,0:T(8,128)S(1)}, f32[128,128]{1,0:T(8,128)S(1)}, u32[]{:S(2)}, u32[]{:S(2)}) collective-permute-start(f32[128,128]{1,0:T(8,128)S(1)} %constant_dynamic-update-slice_fusion), channel_id=1, source_target_pairs={{0,4},{4,8},{8,12},{12,0},{1,5},{5,9},{9,13},{13,1},{2,6},{6,10},{... | collective-permute-start | bytes 196616 | tf_op jit(solution)/shard_map/ppermute | solution.py:450

commit v2 on v0

v2 whole, which is shorter than its diff:
```python
import functools

import jax
import jax.numpy as jnp
from jax import lax
from jax.experimental import pallas as pl
from jax.experimental.pallas import tpu as pltpu
from jax.sharding import PartitionSpec as P

ADJ = 8
NSTEP = 2
F32 = jnp.float32
BF16 = jnp.bfloat16
VMEM_BYTES = 16 << 20


def call(kernel, outs, args, scratch=(), far_in=False, far_out=False, name=None, cost=0):
    near = pl.BlockSpec(memory_space=pltpu.VMEM)
    far = pl.BlockSpec(memory_space=pl.ANY)
    outs = [out if isinstance(out[-1], int) else out for out in outs]
    shapes = [(out, F32) if isinstance(out[-1], int) else out for out in outs]
    return pl.pallas_call(
        kernel,
        out_shape=[(jax.ShapeDtypeStruct if far_out else pltpu.VMEM)(*out) for out in shapes],
        in_specs=[far if far_in else near] * len(args),
        out_specs=[far if far_out else near] * len(outs),
        scratch_shapes=list(scratch),
        compiler_params=pltpu.CompilerParams(vmem_limit_bytes=VMEM_BYTES),
        cost_estimate=pl.CostEstimate(flops=cost, bytes_accessed=cost, transcendentals=0) if cost else None,
        name=name,
    )(*[pltpu.with_memory_space_constraint(arg, pltpu.HBM if far_in else pltpu.VMEM) for arg in args])


def round_up(count, unit):
    return count + -count % unit


def split(value):
    high = value.astype(BF16)
    return high, (value - high.astype(F32)).astype(BF16)


def mix(lhs, field):
    short = lhs.shape[1] // 3 - field.shape[0]
    if short:
        field = jnp.concatenate([field, jnp.zeros((short, field.shape[1]), F32)], axis=0)
    high, low = split(field)
    return jnp.dot(lhs, jnp.concatenate([high, high, low], axis=0), preferred_element_type=F32)


def lane_of(shape):
    return lax.broadcasted_iota(jnp.int32, shape, len(shape) - 1)


def turn(value, steps):
    steps = steps % value.shape[-1]
    return value if steps == 0 else pltpu.roll(value, steps, value.ndim - 1)


def total(parts):
    while len(parts) > 1:
        parts = [parts[i] + parts[i + 1] if i + 1 < len(parts) else parts[i] for i in range(0, len(parts), 2)]
    return parts[0]


def fetch_kernel(dims, *refs):
    lev, width_x, lanes = dims
    sources, (kernel, wx, wy, innov, cluster, strength, matrix, cell, weight, lhs, rim), scratch = (
        refs[:9],
        refs[9:20],
        refs[20:],
    )
    (sem,) = scratch
    pad = round_up(lev, 8)
    deep = lhs.shape[1] // 3
    half = 4 * width_x
    whole = lev * width_x
    targets = [ref.at[pl.ds(0, whole), :] for ref in (kernel, wx, wy)]
    targets += [innov, cluster, strength, matrix, cell, weight]
    copies = [pltpu.make_async_copy(s, t, sem.at[i]) for i, (s, t) in enumerate(zip(sources, targets))]
    for copy in copies:
        copy.start()
    for ref in (kernel, wx, wy):
        ref[pl.ds(whole, (pad - lev) * width_x), :] = jnp.zeros(((pad - lev) * width_x, lanes), F32)
    slot = lane_of((1, lanes)) // 4

    def packed(ref, first, r):
        value = jnp.zeros((8, lanes), F32)
        for x in range(width_x):
            moved = turn(ref[pl.ds(8 * r * width_x + x, 8, stride=width_x), :], first + 4 * x + 2)
            value = jnp.where(slot == first // 4 + x, moved, value)
        return value

    def packed_row(value):
        row = jnp.zeros((1, lanes), F32)
        for x in range(width_x):
            row = jnp.where(slot == x, turn(value[x : x + 1], 4 * x + 2), row)
        return row

    for copy in copies[3:7]:
        copy.wait()
    rim[2 * pad : 2 * pad + 1, :] = packed_row(innov[...])
    rim[2 * pad + 1 : 2 * pad + 2, :] = packed_row(cluster[...].astype(F32))
    rim[2 * pad + 2 : 2 * pad + 3, :] = packed_row(strength[...])
    rim[2 * pad + 3 : 2 * pad + 8, :] = jnp.zeros((5, lanes), F32)
    turned = matrix[...].T
    turned = jnp.concatenate([turned, jnp.zeros((pad - lev, lev), F32)], axis=0)
    turned = jnp.concatenate([turned, jnp.zeros((pad, deep - lev), F32)], axis=1)
    high = turned.astype(BF16).astype(F32)
    lhs[...] = jnp.concatenate([high, turned - high, high], axis=1).astype(BF16)
    for copy in copies[:3]:
        copy.wait()
    for r in range(pad // 8):
        rim[8 * r : 8 * r + 8, :] = jnp.where(slot * 4 >= half, packed(wy, half, r), packed(kernel, 0, r))
        rim[pad + 8 * r : pad + 8 * r + 8, :] = packed(wx, 0, r)
    for copy in copies[7:]:
        copy.wait()


def first_mix_kernel(dims, kernel_ref, innov_ref, strength_ref, lhs_ref, out_ref):
    lev, width_x, lanes = dims
    pad = round_up(lev, 8)
    lhs = lhs_ref[...]
    for x in range(0, width_x, 2):
        tiles = [kernel_ref[pl.ds(at, pad, stride=width_x), :] * innov_ref[at : at + 1, :] for at in (x, x + 1)]
        mixed = mix(lhs, jnp.concatenate(tiles, axis=1))
        for k, tile in enumerate(tiles):
            part = mixed[:, k * lanes : (k + 1) * lanes]
            out_ref[x + k, :, :] = tile + strength_ref[x + k : x + k + 1, :] * (part - tile)


def pack_ends_kernel(dims, subs, *refs):
    lev, width_x, lanes = dims
    own_ref, south_ref, north_ref, c_ref, wx_ref, wy_ref, cluster_ref, strength_ref, lhs_ref = refs[:9]
    rim_ref, east_ref, west_ref = refs[9:]
    pad = round_up(lev, 8)
    half = 4 * width_x
    cross = lax.axis_index("sub")
    lane = lane_of((1, lanes))
    lower = lane < half
    southern = lane % 4 < 2
    present = jnp.where(southern, cross, subs - 1 - cross) > 0

    def halo(rows):
        value = jnp.where(southern, south_ref[rows, :], north_ref[rows, :])
        return jnp.where(present, value, 0.0)

    own = own_ref[0:pad, :]
    far = halo(slice(0, pad))
    far_misc = halo(slice(2 * pad, 2 * pad + 8))
    own_misc = own_ref[2 * pad : 2 * pad + 8, :]
    sources = [
        jnp.where(lower, own, 0.0) * own_misc[0:1],
        jnp.where(lower, far, 0.0) * far_misc[0:1],
    ]
    mixed = mix(lhs_ref[...], jnp.concatenate(sources, axis=1))
    rim_c = sources[0] + own_misc[2:3] * (mixed[:, :lanes] - sources[0])
    far_c = sources[1] + far_misc[2:3] * (mixed[:, lanes:] - sources[1])
    own_wy = jnp.where(lower, turn(own, half), 0.0)
    far_wy = jnp.where(lower, turn(far, half), 0.0)
    far_wx = halo(slice(pad, 2 * pad))
    for at, value in enumerate((rim_c, far_c, own_wy, far_wy, far_wx)):
        rim_ref[at * pad : (at + 1) * pad, :] = value
    base = 5 * pad
    rim_ref[base : base + 1, :] = own_misc[1:2]
    rim_ref[base + 1 : base + 2, :] = far_misc[1:2]
    rim_ref[base + 2 : base + 8, :] = far_misc[2:8]

    last = width_x - 1
    cluster = cluster_ref[...].astype(F32)

    def upright(value):
        square = jnp.concatenate([value, jnp.zeros((lanes - pad, lanes), F32)], axis=0).T
        return square[0:4], square[4 * last : 4 * last + 4]

    corners = [
        c + turn(wy, pad) + turn(wx, 2 * pad)
        for c, wy, wx in zip(upright(far_c), upright(far_wy), upright(far_wx))
    ]

    def put(ref, tiles, near, next_one, corner):
        for at, value in enumerate(tiles):
            top = min(pad, ref.shape[0] - at * lev)
            ref[at * lev : at * lev + top, :] = value[:top]
        base = len(tiles) * lev
        ref[base : base + 1, :] = cluster[near : near + 1]
        ref[base + 1 : base + 2, :] = cluster[next_one : next_one + 1]
        ref[base + 2 : base + 3, :] = strength_ref[near : near + 1, :]
        ref[base + 3 : base + 4, :] = turn(far_misc[1:2], -4 * near)
        ref[base + 4 : base + 8, :] = corner

    def column(ref, x):
        return ref[pl.ds(x, pad, stride=width_x), :]

    ends = (c_ref[last], c_ref[last - 1], column(wx_ref, last), column(wy_ref, last), column(wx_ref, last - 1))
    put(east_ref, ends, last, last - 1, corners[1])
    put(west_ref, (c_ref[0], c_ref[1], column(wx_ref, 0), column(wy_ref, 0)), 0, 1, corners[0])


def rates_of(wx, wx_west, wy, wy_south):
    east = jnp.maximum(wx, 0.0)
    west = jnp.maximum(-wx_west, 0.0)
    north = jnp.maximum(wy, 0.0)
    south = jnp.maximum(-wy_south, 0.0)
    return (1.0 - east) - west - (north + south), east, west, north, south


def from_north(value, halo):
    lanes = value.shape[1]
    return jnp.where(lane_of((1, lanes)) == lanes - 1, halo, turn(value, -1))


def from_south(value, halo):
    return jnp.where(lane_of((1, value.shape[1])) == 0, halo, turn(value, 1))


def crossed(far):
    place = lane_of((1, far.shape[1])) % 4
    return jnp.where(place == 1, turn(far, -1), turn(far, 1))


def halo_of(far, x):
    return turn(far, -4 * x - 2)


def parted(terms, clusters, ids):
    return [total([jnp.where(c == wanted, t, 0.0) for t, c in zip(terms, clusters)]) for wanted in ids]


def convect(lhs, fields, strength):
    lanes = strength.shape[1]
    mixed = mix(lhs, jnp.concatenate(fields, axis=1))
    return [f + strength * (mixed[:, k * lanes : (k + 1) * lanes] - f) for k, f in enumerate(fields)]


def advance(dims, ids, lhs, x, at, rim):
    lev, width_x, lanes = dims
    pad = round_up(lev, 8)
    own_cluster = at.cluster(x)
    rim_row = halo_of(rim.cluster, x)
    clusters = (
        own_cluster,
        at.cluster(x + 1),
        at.cluster(x - 1),
        from_north(own_cluster, rim_row),
        from_south(own_cluster, rim_row),
    )
    clusters = [jnp.broadcast_to(c, (8, lanes)) for c in clusters]
    groups = []
    for r in range(pad // 8):
        wy, own = at.wy(x, r), at.c(x, r)
        south_wy = from_south(wy, halo_of(rim.wy(r), x))
        center, east, west, north, south = rates_of(at.wx(x, r), at.wx(x - 1, r), wy, south_wy)
        halo = halo_of(rim.c(r), x)
        terms = (
            center * own,
            east * at.c(x + 1, r),
            west * at.c(x - 1, r),
            north * from_north(own, halo),
            south * from_south(own, halo),
        )
        groups.append(parted(terms, clusters, ids))
    fields = [jnp.concatenate([group[a] for group in groups], axis=0) for a in range(len(ids))]
    return convect(lhs, fields, at.strength(x))


class Columns:
    def __init__(self, dims, c_ref, wx_ref, wy_ref, cluster_ref, strength_ref, before_ref=None, after_ref=None):
        self.lev, self.width_x, self.lanes = dims
        self.c_ref, self.wx_ref, self.wy_ref = c_ref, wx_ref, wy_ref
        self.cluster_rows = cluster_ref[...].astype(F32)
        self.strength_ref = strength_ref
        self.before_ref, self.after_ref = before_ref, after_ref

    def sent(self, ref, tile, r):
        first = tile * self.lev + 8 * r
        return ref[first : first + 8, :]

    def strided(self, ref, x, r):
        return ref[pl.ds(8 * r * self.width_x + x, 8, stride=self.width_x), :]

    def c(self, x, r):
        if x < 0:
            return self.sent(self.before_ref, -1 - x, r)
        if x >= self.width_x:
            return self.sent(self.after_ref, x - self.width_x, r)
        return self.c_ref[x, 8 * r : 8 * r + 8, :]

    def wx(self, x, r):
        if x < 0:
            return self.sent(self.before_ref, 2 if x == -1 else 4, r)
        return self.sent(self.after_ref, 2, r) if x >= self.width_x else self.strided(self.wx_ref, x, r)

    def wy(self, x, r):
        if x < 0:
            return self.sent(self.before_ref, 3, r)
        return self.sent(self.after_ref, 3, r) if x >= self.width_x else self.strided(self.wy_ref, x, r)

    def misc(self, ref, tiles, row):
        return ref[tiles * self.lev + row : tiles * self.lev + row + 1, :]

    def cluster(self, x):
        if x < 0:
            return self.misc(self.before_ref, 5, -1 - x)
        if x >= self.width_x:
            return self.misc(self.after_ref, 4, x - self.width_x)
        return self.cluster_rows[x : x + 1]

    def strength(self, x):
        if x < 0:
            return self.misc(self.before_ref, 5, 2)
        if x >= self.width_x:
            return self.misc(self.after_ref, 4, 2)
        return self.strength_ref[x : x + 1, :]


class Rim:
    def __init__(self, c, wy, cluster):
        self.c_tile, self.wy_tile, self.cluster = crossed(c), crossed(wy), crossed(cluster)

    def c(self, r):
        return self.c_tile[8 * r : 8 * r + 8]

    def wy(self, r):
        return self.wy_tile[8 * r : 8 * r + 8]


def adjoint_ids(per_device):
    first = (lax.axis_index("adj") * per_device).astype(F32)
    return [first + a for a in range(per_device)]


def inner_kernel(dims, per_device, rim_ref, c_ref, wx_ref, wy_ref, cluster_ref, strength_ref, lhs_ref, mixed_ref):
    lev, width_x, lanes = dims
    pad = round_up(lev, 8)
    at = Columns(dims, c_ref, wx_ref, wy_ref, cluster_ref, strength_ref)
    base = 5 * pad
    rim = Rim(rim_ref[pad : 2 * pad, :], rim_ref[3 * pad : 4 * pad, :], rim_ref[base + 1 : base + 2, :])
    ids = adjoint_ids(per_device)
    lhs = lhs_ref[...]
    for x in range(1, width_x - 1):
        for a, value in enumerate(advance(dims, ids, lhs, x, at, rim)):
            mixed_ref[a, x - 1, :, :] = value


def mixed_at(dims, inner_ref, ends_ref, a, x, r):
    width_x = dims[1]
    rows = slice(8 * r, 8 * r + 8)
    if 1 <= x < width_x - 1:
        return inner_ref[a, x - 1, rows, :]
    return ends_ref[a, x + 1 if x < 1 else x - width_x + 3, rows, :]


def second_transport(dims, at, rim_wy, far, inner_ref, ends_ref, ids, x, r):
    half = 4 * dims[1]
    wy = at.wy(x, r)
    south_wy = from_south(wy, halo_of(rim_wy, x))
    center, east, west, north, south = rates_of(at.wx(x, r), at.wx(x - 1, r), wy, south_wy)
    values = []
    for a in range(len(ids)):
        own = mixed_at(dims, inner_ref, ends_ref, a, x, r)
        halo = turn(far(a // 2, r), -4 * x - 2 - half * (a % 2))
        parts = [
            center * own,
            east * mixed_at(dims, inner_ref, ends_ref, a, x + 1, r),
            west * mixed_at(dims, inner_ref, ends_ref, a, x - 1, r),
            north * from_north(own, halo),
            south * from_south(own, halo),
        ]
        values.append(total(parts))
    return values


def ends_kernel(dims, subs, per_device, *refs):
    lev, width_x, lanes = dims
    rim_ref, before_ref, after_ref, inner_ref, c_ref, wx_ref, wy_ref, cluster_ref, strength_ref, lhs_ref = refs[:10]
    ends_ref, far_ref, surface_ref = refs[10:]
    pad = round_up(lev, 8)
    half = 4 * width_x
    cross = lax.axis_index("sub")
    lane = lane_of((1, lanes))
    place = lane % 4
    after_slot = lane // 4 == width_x
    before_slot = lane >= lanes - 4
    at = Columns(dims, c_ref, wx_ref, wy_ref, cluster_ref, strength_ref, before_ref, after_ref)
    ids = adjoint_ids(per_device)
    lhs = lhs_ref[...]

    def upright(ref, tiles):
        rows = ref[tiles * lev + 4 : tiles * lev + 8, :]
        square = jnp.concatenate([rows, jnp.zeros((lanes - 4, lanes), F32)], axis=0).T
        return [square[i * pad : (i + 1) * pad] for i in range(3)]

    def with_corners(value, before, after):
        return jnp.where(before_slot, turn(before, -4), jnp.where(after_slot, turn(after, half), value))

    corner_before = upright(before_ref, 5)
    corner_after = upright(after_ref, 4)
    base = 5 * pad
    rim_c = rim_ref[0:pad, :]
    rim_wy = rim_ref[2 * pad : 3 * pad, :]
    far_c = with_corners(rim_ref[pad : 2 * pad, :], corner_before[0], corner_after[0])
    far_wy = with_corners(rim_ref[3 * pad : 4 * pad, :], corner_before[1], corner_after[1])
    far_wx = with_corners(rim_ref[4 * pad : 5 * pad, :], corner_before[2], corner_after[2])
    rim_cluster = rim_ref[base : base + 1, :]
    far_cluster = with_corners(
        rim_ref[base + 1 : base + 2, :], at.misc(before_ref, 5, 3), at.misc(after_ref, 4, 3)
    )
    far_strength = rim_ref[base + 2 : base + 3, :]
    rim = Rim(far_c, far_wy, far_cluster)
    for k, x in enumerate((-1, 0, width_x - 1, width_x)):
        for a, value in enumerate(advance(dims, ids, lhs, x, at, rim)):
            ends_ref[a, k, :, :] = value

    def rim_north(far, own):
        return turn(jnp.where(place == 2, own, far), -1)

    def rim_south(far, own):
        return turn(jnp.where(place == 1, own, far), 1)

    center, east, west, north, south = rates_of(far_wx, turn(far_wx, 4), far_wy, rim_south(far_wy, rim_wy))
    terms = (
        center * far_c,
        east * turn(far_c, -4),
        west * turn(far_c, 4),
        north * rim_north(far_c, rim_c),
        south * rim_south(far_c, rim_c),
    )
    clusters = (
        far_cluster,
        turn(far_cluster, -4),
        turn(far_cluster, 4),
        rim_north(far_cluster, rim_cluster),
        rim_south(far_cluster, rim_cluster),
    )
    inside = jnp.where(lane < half, jnp.where(place < 2, cross, subs - 1 - cross), 0) > 0
    fields = [jnp.where(inside, f, 0.0) for f in parted(terms, clusters, ids)]
    joined = [fields[a] + turn(fields[a + 1], half) for a in range(0, per_device, 2)]
    far_mixed = [crossed(f) for f in convect(lhs, joined, far_strength + turn(far_strength, half))]
    for at_pair, value in enumerate(far_mixed):
        far_ref[at_pair, 0:pad, :] = value
    far_ref[0, pad : pad + 8, :] = jnp.zeros((8, lanes), F32)
    for pair in range(1, len(far_mixed)):
        far_ref[pair, pad : pad + 8, :] = jnp.zeros((8, lanes), F32)

    def far(pair, r):
        return far_mixed[pair][8 * r : 8 * r + 8]

    for x in range(width_x):
        values = second_transport(dims, at, rim.wy(0), far, inner_ref, ends_ref, ids, x, 0)
        for a, value in enumerate(values):
            surface_ref[a * width_x + x : a * width_x + x + 1, :] = value[0:1]


def output_kernel(dims, per_device, *refs):
    lev, width_x, lanes = dims
    rim_ref, before_ref, inner_ref, ends_ref, far_ref, wx_ref, wy_ref, cluster_ref, strength_ref = refs[:9]
    out_ref, field_ref, sem = refs[9:]
    pad = round_up(lev, 8)
    at = Columns(dims, None, wx_ref, wy_ref, cluster_ref, strength_ref, before_ref)
    ids = range(per_device)

    def far(pair, r):
        return far_ref[pair, 8 * r : 8 * r + 8, :]

    rim_wys = [crossed(rim_ref[3 * pad + 8 * r : 3 * pad + 8 * r + 8, :]) for r in range(pad // 8)]
    copies = []
    for x in range(width_x):
        for r in range(pad // 8):
            rim_wy = rim_wys[r]
            values = second_transport(dims, at, rim_wy, far, inner_ref, ends_ref, ids, x, r)
            for a, value in enumerate(values):
                field_ref[a, x, 8 * r : 8 * r + 8, :] = value
        for a in range(per_device):
            source = field_ref.at[a, x, pl.ds(0, lev), :]
            copies.append(pltpu.make_async_copy(source, out_ref.at[a, :, x, 0, :], sem.at[len(copies)]))
            copies[-1].start()
    for copy in copies:
        copy.wait()


def quotient(value, count):
    if count & (count - 1) == 0:
        return value >> (count.bit_length() - 1), value & (count - 1)
    return lax.div(value, count), lax.rem(value, count)


def sense_kernel(width_x, width_y, tiles, subs, per_device, n_rim, blocks, cell_ref, weight_ref, partial_ref, out_ref):
    slots, elements = cell_ref.shape
    tile_pos = lax.axis_index("tiles")
    cross = lax.axis_index("sub")
    group = width_y

    def one_group(g, carry):
        lanes = pl.ds(pl.multiple_of(g * group, group), group)
        cell = cell_ref[:, lanes]
        weight = weight_ref[:, lanes]
        column_x, row_y = quotient(cell, width_y * subs)
        block_x, inner_x = quotient(column_x, width_x)
        block_y, lane_y = quotient(row_y, width_y)
        step = block_x - tile_pos
        step = jnp.where(step < -1, step + tiles, jnp.where(step > 1, step - tiles, step))
        if n_rim == 2:
            side = jnp.where(block_y == cross, 0, 1)
        else:
            side = block_y - cross + 1
        row_id = ((step + 1) * n_rim + side) * width_x + inner_x
        sums = [jnp.zeros((8, group), F32) for _ in range(per_device)]
        within = lax.broadcasted_iota(jnp.int32, (8, group), 0)
        for k in range(slots):
            pick = jnp.broadcast_to(lane_y[k : k + 1], (8, group))
            row = jnp.broadcast_to(row_id[k : k + 1], (8, group)) - within
            share = jnp.broadcast_to(weight[k : k + 1], (8, group))
            for at_step, at_side, ref, base in blocks:
                for part in range(0, width_x, 8):
                    first_id = ((at_step + 1) * n_rim + at_side) * width_x + part
                    chosen = jnp.where(row == first_id, share, 0.0)
                    for a in range(per_device):
                        first = base + a * width_x + part
                        value = jnp.take_along_axis(ref[first : first + 8, :], pick, axis=1)
                        sums[a] = sums[a] + chosen * value
        sensed = jnp.concatenate([jnp.sum(s, axis=0, keepdims=True) for s in sums], axis=0)
        if partial_ref is not None:
            sensed = sensed + partial_ref[:, lanes]
        out_ref[:, lanes] = sensed
        return carry

    lax.fori_loop(0, elements // group, one_group, 0)


def ring(value, axis, steps):
    count = lax.axis_size(axis)
    return lax.ppermute(value, axis, [(i, (i + steps) % count) for i in range(count)])


def across(value):
    count = lax.axis_size("sub")
    if count == 2:
        other = ring(value, "sub", 1)
        return other, other
    from_south = lax.ppermute(value, "sub", [(i, i + 1) for i in range(count - 1)])
    from_north = lax.ppermute(value, "sub", [(i + 1, i) for i in range(count - 1)])
    return from_south, from_north


def body(
    innovation,
    cluster,
    kernel,
    wind_x,
    wind_y,
    conv_strength,
    conv_matrix,
    margin_cell,
    margin_weight,
):
    dims = kernel.shape
    lev, width_x, width_y = dims
    tiles = lax.axis_size("tiles")
    subs = lax.axis_size("sub")
    per_device = ADJ // lax.axis_size("adj")
    pad = round_up(lev, 8)
    deep = round_up(lev, 16)
    flat = (lev * width_x, width_y)
    tall = (pad * width_x, width_y)
    small = innovation.shape
    sources = (
        kernel.reshape(flat),
        wind_x.reshape(flat),
        wind_y.reshape(flat),
        innovation,
        cluster,
        conv_strength,
        conv_matrix,
        margin_cell.T,
        margin_weight.T,
    )
    outs = [tall, tall, tall, small, (small, jnp.int32), small, conv_matrix.shape]
    outs += [(sources[7].shape, jnp.int32), sources[8].shape, ((pad, 3 * deep), BF16), (2 * pad + 8, width_y)]
    fetched = call(
        functools.partial(fetch_kernel, dims),
        outs,
        sources,
        scratch=(pltpu.SemaphoreType.DMA((len(sources),)),),
        far_in=True,
        name="fetch",
    )
    air, wx, wy, innov, group, strength, _, cell, weight, lhs, own_rim = fetched
    south_rim, north_rim = across(own_rim)
    (first,) = call(
        functools.partial(first_mix_kernel, dims),
        [(width_x, pad, width_y)],
        (air, innov, strength, lhs),
        name="first_mix",
        cost=400000,
    )
    rim, to_east, to_west = call(
        functools.partial(pack_ends_kernel, dims, subs),
        [(5 * pad + 8, width_y), (5 * lev + 8, width_y), (4 * lev + 8, width_y)],
        (own_rim, south_rim, north_rim, first, wx, wy, group, strength, lhs),
        name="pack_ends",
    )
    before = ring(to_east, "tiles", 1)
    after = ring(to_west, "tiles", -1)
    (inner,) = call(
        functools.partial(inner_kernel, dims, per_device),
        [(per_device, width_x - 2, pad, width_y)],
        (rim, first, wx, wy, group, strength, lhs),
        name="inner",
        cost=4000000,
    )
    ends, far, surface = call(
        functools.partial(ends_kernel, dims, subs, per_device),
        [
            (per_device, 4, pad, width_y),
            ((per_device + 1) // 2, pad + 8, width_y),
            (per_device * width_x, width_y),
        ],
        (rim, before, after, inner, first, wx, wy, group, strength, lhs),
        name="ends",
    )
    south_surface, north_surface = across(surface)
    (field,) = call(
        functools.partial(output_kernel, dims, per_device),
        [(per_device, lev, width_x, 1, width_y)],
        (rim, before, inner, ends, far, wx, wy, group, strength),
        scratch=(
            pltpu.VMEM((per_device, width_x, pad, width_y), F32),
            pltpu.SemaphoreType.DMA((per_device * width_x,)),
        ),
        far_out=True,
        name="output",
        cost=4000000,
    )
    if subs == 2:
        strip = [surface, south_surface]
    else:
        strip = [south_surface, surface, north_surface]
    n_rim = len(strip)
    whole = jnp.concatenate(strip, axis=0)
    surface_after = ring(whole, "tiles", -1)
    surface_before = ring(whole, "tiles", 1)
    rows = per_device * width_x
    looked_up = functools.partial(sense_kernel, width_x, width_y, tiles, subs, per_device, n_rim)

    def sense_here(cell_ref, weight_ref, *rest):
        *here, out_ref = rest
        looked_up([(0, k, ref, 0) for k, ref in enumerate(here)], cell_ref, weight_ref, None, out_ref)

    def sense_beside(step, cell_ref, weight_ref, partial_ref, block_ref, out_ref):
        blocks = [(step, k, block_ref, k * rows) for k in range(n_rim)]
        looked_up(blocks, cell_ref, weight_ref, partial_ref, out_ref)

    sensed_shape = [(per_device, cell.shape[1])]
    (sensed,) = call(sense_here, sensed_shape, (cell, weight, *strip), name="sense_here", cost=2000000)
    for step, block in ((1, surface_after), (-1, surface_before)):
        (sensed,) = call(
            functools.partial(sense_beside, step), sensed_shape, (cell, weight, sensed, block), name="sense_beside", cost=2000000
        )
    return (field.reshape(per_device, lev, width_x, width_y), sensed)


def solution(mesh):
    in_specs = (
        P(("groups", "tiles"), "sub"),
        P(("groups", "tiles"), "sub"),
        P(None, "tiles", "sub"),
        P(None, "tiles", "sub"),
        P(None, "tiles", "sub"),
        P("tiles", "sub"),
        P(),
        P(("tiles", "sub"), None),
        P(("tiles", "sub"), None),
    )
    out_specs = (P(("groups", "adj"), None, "tiles", "sub"), P(("groups", "adj"), ("tiles", "sub")))
    return jax.shard_map(body, mesh=mesh, in_specs=in_specs, out_specs=out_specs, check_vma=False)
```

time: 119 us -> 32 us (0.27)
  local copies, waits for them, and re-layouts: 57.2 us -> 0.61 us
  starting transfers between devices: 31.9 us -> 11.7 us
  other arithmetic: 13.7 us -> 0 us
  Pallas kernels: 0 us -> 12 us
  matrix products: 8.44 us -> 0 us
    ppermute x14 -> x6, starting transfers between devices: 31.9 us -> 11.7 us  [ring(): lax.ppermute(value, axis, [(i, (i + steps) % count) for i in range(count)])]
    gather x1 -> x0, local copies, waits for them, and re-layouts: 19.8 us -> none  [body(): jnp.take(flat_surface, local_index.reshape(-1), axis=1)]
    slice x15 -> x0, local copies, waits for them, and re-layouts: 17 us -> none  [the longest x4 4.67 us: body(): adjoint[:, :, :, -1:]]
    pallas_call x0 -> x9, Pallas kernels: none -> 12 us  [call(): pl.pallas_call(kernel, out_shape=[(jax.ShapeDtypeStruct if far_out else p...]
    dot_general x2 -> x0, matrix products: 8.44 us -> none  [convect(): jnp.einsum('lk,alxy->akxy', matrix, adjoint, precision=lax.Precision.HIGH...]
    ppermute x4 -> x0, local copies, waits for them, and re-layouts: 6.63 us -> none  [the longest x2 3.35 us: extended(): lax.ppermute(tail, axis, [(i, (i + 1) % count) for i in range(ends)])]
    unnamed x36 -> x2, local copies, waits for them, and re-layouts: 6.99 us -> 0.61 us
    reduce_sum x1 -> x0, other arithmetic: 6.14 us -> none  [body(): sensed = jnp.sum(margin_weight[None] * values, axis=2)]
  transfers between devices with their start and end apart: 14 -> 6, of which waited for: 3 -> 4; matrix products, arithmetic and copies ran while one was open for 20% -> 0% of each run, Pallas kernels for 0% -> 22%
where the time goes in v2:
time: 32 us; the launch traced here: 31.9 us
  Pallas kernels  12 us (38%)
  starting transfers between devices  11.7 us (37%)
  waiting for transfers between devices  6.87 us (21%)
  between operations  0.71 us (2%)
  local copies, waits for them, and re-layouts  0.61 us (2%)
    pallas_call x9, Pallas kernels, call(): pl.pallas_call(kernel, out_shape=[(jax.ShapeDtypeStruct if far_out else p...  12 us
    ppermute x6, starting transfers between devices, ring(): lax.ppermute(value, axis, [(i, (i + steps) % count) for i in range(count)])  11.7 us
    ppermute x6, waiting for transfers between devices, ring(): lax.ppermute(value, axis, [(i, (i + steps) % count) for i in range(count)])  6.87 us
  transfers between devices with their start and end apart: 6, of which 4 were waited for; matrix products, arithmetic and copies ran while one was open for 0% of the time, Pallas kernels for 22%

profile of v2, /device:TPU:0, one launch (start us, length us, event | category | flops | bytes accessed | tf_op | source)
XLA Modules:
  0.0 31.9 jit_solution(13176621514043351217)
XLA Ops:
  0.6 2.2 %fetch.1 = (f32[640,128]{1,0:T(8,128)S(1)}, f32[640,128]{1,0:T(8,128)S(1)}, f32[640,128]{1,0:T(8,128)S(1)}, f32[16,128]{1,0:T(8,128)S(1)}, s32[16,128]{1,0:T(8,1...) custom-call(f32[576,128]{1,0:T(8,128)} %bitcast.7, ...), custom_call_target="tpu_custom_call" | custom-call | tf_op jit(solution)/shard_map/fetch/pallas_call | solution.py:22
  2.9 3.0 %collective-permute-start = (f32[88,128]{1,0:T(8,128)S(1)}, f32[88,128]{1,0:T(8,128)S(1)}, u32[]{:S(2)}, u32[]{:S(2)}) collective-permute-start(f32[88,128]{1,0:T(8,128)S(1)} %get-tuple-element.18.refs_0_), channel_id=1, source_target_pairs={{0,2},{2,0},{1,3},{3,1},{4,6},{6,4},{5,7},{7,5},{8,10},{10,8},{9,1... | collective-permute-start | bytes 135176 | tf_op jit(solution)/shard_map/ppermute | solution.py:533
  5.9 0.3 first_mix.1.refs_3_.c_ref.refs_4_
  6.2 1.8 %collective-permute-done.refs_1_.refs_2_ = f32[88,128]{1,0:T(8,128)S(1)} collective-permute-done((f32[88,128]{1,0:T(8,128)S(1)}, f32[88,128]{1,0:T(8,128)S(1)}, u32[]{:S(2)}, u32[]{:S(2)}) %collective-permute-start) | collective-permute-done | bytes 45088 | tf_op jit(solution)/shard_map/ppermute | solution.py:533
  7.9 0.3 pack_ends.1
  8.2 2.2 %collective-permute-start.1 = (f32[188,128]{1,0:T(8,128)S(1)}, f32[188,128]{1,0:T(8,128)S(1)}, u32[]{:S(2)}, u32[]{:S(2)}) collective-permute-start(f32[188,128]{1,0:T(8,128)S(1)} %get-tuple-element.27), channel_id=1, source_target_pairs={{0,4},{4,8},{8,12},{12,0},{1,5},{5,9},{9,13},{13,1},{2,6},{6,10},{... | collective-permute-start | bytes 288776 | tf_op jit(solution)/shard_map/ppermute | solution.py:533
  10.4 2.1 %collective-permute-start.2 = (f32[152,128]{1,0:T(8,128)S(1)}, f32[152,128]{1,0:T(8,128)S(1)}, u32[]{:S(2)}, u32[]{:S(2)}) collective-permute-start(f32[152,128]{1,0:T(8,128)S(1)} %get-tuple-element.28), channel_id=1, source_target_pairs={{0,12},{4,0},{8,4},{12,8},{1,13},{5,1},{9,5},{13,9},{2,14},{6,2},{... | collective-permute-start | bytes 233480 | tf_op jit(solution)/shard_map/ppermute | solution.py:533
  12.5 1.3 %inner.1.refs_3_.refs_2_ = f32[4,14,40,128]{3,2,1,0:T(8,128)S(1)} custom-call(f32[208,128]{1,0:T(8,128)S(1)} %get-tuple-element.26.rim_ref.refs_0_, f32[16,40,128]{2,1,0:T(8,128)S(1)} %first_mix.1.refs_3_.c_ref.refs_4_, f32[640,128]{1,0:T(8,128)S(1)} %get-tuple-element.23.refs_4_.wx_ref.refs_5_, f32[640,128]{1,0:T(8,128)S(1)} %get-tuple-element.24.refs_5_.wy_ref.refs_6_, ...), custom_call_target="tpu_custom_call" | custom-call | flops 4000000 | bytes 4000000 | tf_op jit(solution)/shard_map/inner/pallas_call | solution.py:22
  13.8 2.0 %collective-permute-done.2.refs_2_ = f32[152,128]{1,0:T(8,128)S(1)} collective-permute-done((f32[152,128]{1,0:T(8,128)S(1)}, f32[152,128]{1,0:T(8,128)S(1)}, u32[]{:S(2)}, u32[]{:S(2)}) %collective-permute-start.2) | collective-permute-done | bytes 77856 | tf_op jit(solution)/shard_map/ppermute | solution.py:533
  15.9 0.0 collective-permute-done.1.refs_1_
  15.9 1.1 %ends.1 = (f32[4,4,40,128]{3,2,1,0:T(8,128)S(1)}, f32[2,48,128]{2,1,0:T(8,128)S(1)}, f32[64,128]{1,0:T(8,128)S(1)}) custom-call(f32[208,128]{1,0:T(8,128)S(1)} %get-tuple-element.26.rim_ref.refs_0_, f32[188,128]{1,0:T(8,128)S(1)} %collective-permute-done.1.refs_1_, f32[152,128]{1,0:T(8,128)S(1)} %collective-permute-done.2.refs_2_, ...), custom_call_target="tpu_custom_call" | custom-call | tf_op jit(solution)/shard_map/ends/pallas_call | solution.py:22
  17.0 1.6 %collective-permute-start.3 = (f32[64,128]{1,0:T(8,128)S(1)}, f32[64,128]{1,0:T(8,128)S(1)}, u32[]{:S(2)}, u32[]{:S(2)}) collective-permute-start(f32[64,128]{1,0:T(8,128)S(1)} %get-tuple-element.33.rest_0_), channel_id=1, source_target_pairs={{0,2},{2,0},{1,3},{3,1},{4,6},{6,4},{5,7},{7,5},{8,10},{10,8},{9,1... | collective-permute-start | bytes 98312 | tf_op jit(solution)/shard_map/ppermute | solution.py:533
  18.5 2.4 %collective-permute-done.3.rest_1_ = f32[64,128]{1,0:T(8,128)S(1)} collective-permute-done((f32[64,128]{1,0:T(8,128)S(1)}, f32[64,128]{1,0:T(8,128)S(1)}, u32[]{:S(2)}, u32[]{:S(2)}) %collective-permute-start.3) | collective-permute-done | bytes 32800 | tf_op jit(solution)/shard_map/ppermute | solution.py:533
  20.9 2.8 %collective-permute-start.4 = (f32[128,128]{1,0:T(8,128)S(1)}, f32[128,128]{1,0:T(8,128)S(1)}, u32[]{:S(2)}, u32[]{:S(2)}) collective-permute-start(f32[128,128]{1,0:T(8,128)S(1)} %constant_dynamic-update-slice_fusion), channel_id=1, source_target_pairs={{0,12},{4,0},{8,4},{12,8},{1,13},{5,1},{9,5},{13,9},{2,14},{6,2},{... | collective-permute-start | bytes 196616 | tf_op jit(solution)/shard_map/ppermute | solution.py:533
  23.8 0.0 collective-permute-start.5
  23.8 2.5 %output.1 = f32[4,36,16,1,128]{4,3,2,1,0:T(1,128)} custom-call(f32[208,128]{1,0:T(8,128)S(1)} %get-tuple-element.26.rim_ref.refs_0_, f32[188,128]{1,0:T(8,128)S(1)} %collective-permute-done.1.refs_1_, f32[4,14,40,128]{3,2,1,0:T(8,128)S(1)} %inner.1.refs_3_.refs_2_, f32[4,4,40,128]{3,2,1,0:T(8,128)S(1)} %get-tuple-element.29.refs_3_, ...), custom_call_target="tpu_custom_call" | custom-call | flops 4000000 | bytes 4000000 | tf_op jit(solution)/shard_map/output/pallas_call | solution.py:22
  26.3 1.5 %sense_here.1.partial_ref = f32[4,768]{1,0:T(4,128)S(1)} custom-call(s32[8,768]{1,0:T(8,128)S(1)} %get-tuple-element.31.cell_ref, f32[8,768]{1,0:T(8,128)S(1)} %get-tuple-element.32.weight_ref, f32[64,128]{1,0:T(8,128)S(1)} %get-tuple-element.33.rest_0_, f32[64,128]{1,0:T(8,128)S(1)} %collective-permute-done.3.rest_1_), custom_call_target="tpu_custom_call" | custom-call | flops 2000000 | bytes 2000000 | tf_op jit(solution)/shard_map/sense_here/pallas_call | solution.py:22
  27.7 0.0 collective-permute-done.4.block_ref
  27.7 1.5 %sense_beside.2.partial_ref = f32[4,768]{1,0:T(4,128)S(1)} custom-call(s32[8,768]{1,0:T(8,128)S(1)} %get-tuple-element.31.cell_ref, f32[8,768]{1,0:T(8,128)S(1)} %get-tuple-element.32.weight_ref, f32[4,768]{1,0:T(4,128)S(1)} %sense_here.1.partial_ref, f32[128,128]{1,0:T(8,128)S(1)} %collective-permute-done.4.block_ref), custom_call_target="tpu_custom_call" | custom-call | flops 2000000 | bytes 2000000 | tf_op jit(solution)/shard_map/sense_beside/pallas_call | solution.py:22
  29.2 0.7 %collective-permute-done.5.block_ref = f32[128,128]{1,0:T(8,128)S(1)} collective-permute-done((f32[128,128]{1,0:T(8,128)S(1)}, f32[128,128]{1,0:T(8,128)S(1)}, u32[]{:S(2)}, u32[]{:S(2)}) %collective-permute-start.5) | collective-permute-done | bytes 65568 | tf_op jit(solution)/shard_map/ppermute | solution.py:533
  29.8 1.4 %sense_beside.3 = f32[4,768]{1,0:T(4,128)S(1)} custom-call(s32[8,768]{1,0:T(8,128)S(1)} %get-tuple-element.31.cell_ref, f32[8,768]{1,0:T(8,128)S(1)} %get-tuple-element.32.weight_ref, f32[4,768]{1,0:T(4,128)S(1)} %sense_beside.2.partial_ref, f32[128,128]{1,0:T(8,128)S(1)} %collective-permute-done.5.block_ref), custom_call_target="tpu_custom_call" | custom-call | flops 2000000 | bytes 2000000 | tf_op jit(solution)/shard_map/sense_beside/pallas_call | solution.py:22
  31.3 0.6 %copy.12 = f32[4,768]{1,0:T(4,128)} copy(f32[4,768]{1,0:T(4,128)S(1)} %sense_beside.3) | data formatting | bytes 24576
  (2 shorter events, 0.0 us)
Async XLA Ops:
  2.9 5.1 %collective-permute-start = (f32[88,128]{1,0:T(8,128)S(1)}, f32[88,128]{1,0:T(8,128)S(1)}, u32[]{:S(2)}, u32[]{:S(2)}) collective-permute-start(f32[88,128]{1,0:T(8,128)S(1)} %get-tuple-element.18.refs_0_), channel_id=1, source_target_pairs={{0,2},{2,0},{1,3},{3,1},{4,6},{6,4},{5,7},{7,5},{8,10},{10,8},{9,1... | collective-permute-start | bytes 135176 | tf_op jit(solution)/shard_map/ppermute | solution.py:533
  8.2 7.6 %collective-permute-start.1 = (f32[188,128]{1,0:T(8,128)S(1)}, f32[188,128]{1,0:T(8,128)S(1)}, u32[]{:S(2)}, u32[]{:S(2)}) collective-permute-start(f32[188,128]{1,0:T(8,128)S(1)} %get-tuple-element.27), channel_id=1, source_target_pairs={{0,4},{4,8},{8,12},{12,0},{1,5},{5,9},{9,13},{13,1},{2,6},{6,10},{... | collective-permute-start | bytes 288776 | tf_op jit(solution)/shard_map/ppermute | solution.py:533
  10.4 5.5 %collective-permute-start.2 = (f32[152,128]{1,0:T(8,128)S(1)}, f32[152,128]{1,0:T(8,128)S(1)}, u32[]{:S(2)}, u32[]{:S(2)}) collective-permute-start(f32[152,128]{1,0:T(8,128)S(1)} %get-tuple-element.28), channel_id=1, source_target_pairs={{0,12},{4,0},{8,4},{12,8},{1,13},{5,1},{9,5},{13,9},{2,14},{6,2},{... | collective-permute-start | bytes 233480 | tf_op jit(solution)/shard_map/ppermute | solution.py:533
  17.0 4.0 %collective-permute-start.3 = (f32[64,128]{1,0:T(8,128)S(1)}, f32[64,128]{1,0:T(8,128)S(1)}, u32[]{:S(2)}, u32[]{:S(2)}) collective-permute-start(f32[64,128]{1,0:T(8,128)S(1)} %get-tuple-element.33.rest_0_), channel_id=1, source_target_pairs={{0,2},{2,0},{1,3},{3,1},{4,6},{6,4},{5,7},{7,5},{8,10},{10,8},{9,1... | collective-permute-start | bytes 98312 | tf_op jit(solution)/shard_map/ppermute | solution.py:533
  20.9 6.8 %collective-permute-start.4 = (f32[128,128]{1,0:T(8,128)S(1)}, f32[128,128]{1,0:T(8,128)S(1)}, u32[]{:S(2)}, u32[]{:S(2)}) collective-permute-start(f32[128,128]{1,0:T(8,128)S(1)} %constant_dynamic-update-slice_fusion), channel_id=1, source_target_pairs={{0,12},{4,0},{8,4},{12,8},{1,13},{5,1},{9,5},{13,9},{2,14},{6,2},{... | collective-permute-start | bytes 196616 | tf_op jit(solution)/shard_map/ppermute | solution.py:533
  23.8 6.1 %collective-permute-start.5 = (f32[128,128]{1,0:T(8,128)S(1)}, f32[128,128]{1,0:T(8,128)S(1)}, u32[]{:S(2)}, u32[]{:S(2)}) collective-permute-start(f32[128,128]{1,0:T(8,128)S(1)} %constant_dynamic-update-slice_fusion), channel_id=1, source_target_pairs={{0,4},{4,8},{8,12},{12,0},{1,5},{5,9},{9,13},{13,1},{2,6},{6,10},{... | collective-permute-start | bytes 196616 | tf_op jit(solution)/shard_map/ppermute | solution.py:533

commit v3 on v2

--- a/solution.py
+++ b/solution.py
@@ -14,16 +14,16 @@
 VMEM_BYTES = 16 << 20
 
 
-def call(kernel, outs, args, scratch=(), far_in=False, far_out=False, name=None, cost=0):
+def call(kernel, outs, args, scratch=(), far_in=False, far_out=(), name=None, cost=0):
     near = pl.BlockSpec(memory_space=pltpu.VMEM)
     far = pl.BlockSpec(memory_space=pl.ANY)
     outs = [out if isinstance(out[-1], int) else out for out in outs]
     shapes = [(out, F32) if isinstance(out[-1], int) else out for out in outs]
     return pl.pallas_call(
         kernel,
-        out_shape=[(jax.ShapeDtypeStruct if far_out else pltpu.VMEM)(*out) for out in shapes],
+        out_shape=[(jax.ShapeDtypeStruct if at in far_out else pltpu.VMEM)(*out) for at, out in enumerate(shapes)],
         in_specs=[far if far_in else near] * len(args),
-        out_specs=[far if far_out else near] * len(outs),
+        out_specs=[far if at in far_out else near for at in range(len(outs))],
         scratch_shapes=list(scratch),
         compiler_params=pltpu.CompilerParams(vmem_limit_bytes=VMEM_BYTES),
         cost_estimate=pl.CostEstimate(flops=cost, bytes_accessed=cost, transcendentals=0) if cost else None,
@@ -455,7 +455,8 @@
 def output_kernel(dims, per_device, *refs):
     lev, width_x, lanes = dims
     rim_ref, before_ref, inner_ref, ends_ref, far_ref, wx_ref, wy_ref, cluster_ref, strength_ref = refs[:9]
-    out_ref, field_ref, sem = refs[9:]
+    out_ref, token_ref, field_ref, sem = refs[9:]
+    token_ref[...] = jnp.zeros(token_ref.shape, F32)
     pad = round_up(lev, 8)
     at = Columns(dims, None, wx_ref, wy_ref, cluster_ref, strength_ref, before_ref)
     ids = range(per_device)
@@ -485,47 +486,87 @@
     return lax.div(value, count), lax.rem(value, count)
 
 
-def sense_kernel(width_x, width_y, tiles, subs, per_device, n_rim, blocks, cell_ref, weight_ref, partial_ref, out_ref):
+def tables_kernel(dims, tiles, subs, n_rim, cell_ref, weight_ref, hot_ref, share_ref):
+    _, width_x, width_y = dims
     slots, elements = cell_ref.shape
     tile_pos = lax.axis_index("tiles")
     cross = lax.axis_index("sub")
+    column_x, row_y = quotient(cell_ref[...], width_y * subs)
+    block_x, inner_x = quotient(column_x, width_x)
+    block_y, lane_y = quotient(row_y, width_y)
+    step = block_x - tile_pos
+    step = jnp.where(step < -1, step + tiles, jnp.where(step > 1, step - tiles, step))
+    if n_rim == 2:
+        side = jnp.where(block_y == cross, 0, 1)
+    else:
+        side = block_y - cross + 1
+    at_y = side * width_y + lane_y
+    at_x = (step + 1) * width_x + inner_x
+    weight = weight_ref[...]
     group = width_y
-
-    def one_group(g, carry):
-        lanes = pl.ds(pl.multiple_of(g * group, group), group)
-        cell = cell_ref[:, lanes]
-        weight = weight_ref[:, lanes]
-        column_x, row_y = quotient(cell, width_y * subs)
-        block_x, inner_x = quotient(column_x, width_x)
-        block_y, lane_y = quotient(row_y, width_y)
-        step = block_x - tile_pos
-        step = jnp.where(step < -1, step + tiles, jnp.where(step > 1, step - tiles, step))
-        if n_rim == 2:
-            side = jnp.where(block_y == cross, 0, 1)
-        else:
-            side = block_y - cross + 1
-        row_id = ((step + 1) * n_rim + side) * width_x + inner_x
-        sums = [jnp.zeros((8, group), F32) for _ in range(per_device)]
-        within = lax.broadcasted_iota(jnp.int32, (8, group), 0)
+    rows = lax.broadcasted_iota(jnp.int32, (16, group), 0)
+    for g in range(0, elements, group):
+        lanes = slice(g, g + group)
         for k in range(slots):
-            pick = jnp.broadcast_to(lane_y[k : k + 1], (8, group))
-            row = jnp.broadcast_to(row_id[k : k + 1], (8, group)) - within
-            share = jnp.broadcast_to(weight[k : k + 1], (8, group))
-            for at_step, at_side, ref, base in blocks:
-                for part in range(0, width_x, 8):
-                    first_id = ((at_step + 1) * n_rim + at_side) * width_x + part
-                    chosen = jnp.where(row == first_id, share, 0.0)
-                    for a in range(per_device):
-                        first = base + a * width_x + part
-                        value = jnp.take_along_axis(ref[first : first + 8, :], pick, axis=1)
-                        sums[a] = sums[a] + chosen * value
-        sensed = jnp.concatenate([jnp.sum(s, axis=0, keepdims=True) for s in sums], axis=0)
-        if partial_ref is not None:
-            sensed = sensed + partial_ref[:, lanes]
-        out_ref[:, lanes] = sensed
-        return carry
-
-    lax.fori_loop(0, elements // group, one_group, 0)
+            y = jnp.broadcast_to(at_y[k : k + 1, lanes], (16, group)) - rows
+            for first in range(0, n_rim * width_y, 16):
+                hot_ref[k, first : first + 16, lanes] = jnp.where(y == first, 1.0, 0.0).astype(BF16)
+            x = jnp.broadcast_to(at_x[k : k + 1, lanes], (16, group)) - rows
+            w = jnp.broadcast_to(weight[k : k + 1, lanes], (16, group))
+            for first in range(0, 3 * width_x, 16):
+                share_ref[k, first : first + 16, lanes] = jnp.where(x == first, w, 0.0)
+
+
+def looked_up(dims, per_device, n_rim, blocks, hot_ref, share_ref, lanes):
+    width_x = dims[1]
+    rows = per_device * width_x
+    surfaces = [split(jnp.concatenate(places, axis=1)) for _, places in blocks]
+    lhs = jnp.concatenate([part for pair in surfaces for part in pair], axis=0)
+    sums = [None] * per_device
+    for k in range(hot_ref.shape[0]):
+        found = jnp.dot(lhs, hot_ref[k, :, lanes], preferred_element_type=F32)
+        for at, (step, _) in enumerate(blocks):
+            share = share_ref[k, (step + 1) * width_x : (step + 2) * width_x, lanes]
+            for a in range(per_device):
+                high = 2 * at * rows + a * width_x
+                low = high + rows
+                value = (found[high : high + width_x] + found[low : low + width_x]) * share
+                sums[a] = value if sums[a] is None else sums[a] + value
+    return jnp.concatenate([jnp.sum(s, axis=0, keepdims=True) for s in sums], axis=0)
+
+
+def wide_lanes(elements):
+    wide = 256 if elements % 256 == 0 else 128
+    return [slice(g, g + wide) for g in range(0, elements, wide)]
+
+
+def sense_here_kernel(dims, per_device, hot_ref, share_ref, *refs):
+    *here, out_ref = refs
+    blocks = [(0, [ref[...] for ref in here])]
+    for lanes in wide_lanes(out_ref.shape[1]):
+        out_ref[:, lanes] = looked_up(dims, per_device, len(here), blocks, hot_ref, share_ref, lanes)
+
+
+def sense_kernel(dims, per_device, n_rim, hot_ref, share_ref, partial_ref, before_ref, after_ref, out_ref, own_ref, sem):
+    rows = per_device * dims[1]
+    blocks = [
+        (step, [ref[k * rows : (k + 1) * rows, :] for k in range(n_rim)])
+        for step, ref in ((-1, before_ref), (1, after_ref))
+    ]
+    for lanes in wide_lanes(own_ref.shape[1]):
+        value = looked_up(dims, per_device, n_rim, blocks, hot_ref, share_ref, lanes)
+        own_ref[:, lanes] = partial_ref[:, lanes] + value
+    copy = pltpu.make_async_copy(own_ref, out_ref, sem)
+    copy.start()
+    copy.wait()
+
+
+def join_kernel(*refs):
+    *parts, _, out_ref = refs
+    first = 0
+    for part in parts:
+        out_ref[first : first + part.shape[0], :] = part[...]
+        first += part.shape[0]
 
 
 def ring(value, axis, steps):
@@ -620,15 +661,15 @@
         name="ends",
     )
     south_surface, north_surface = across(surface)
-    (field,) = call(
+    field, token = call(
         functools.partial(output_kernel, dims, per_device),
-        [(per_device, lev, width_x, 1, width_y)],
+        [(per_device, lev, width_x, 1, width_y), (8, width_y)],
         (rim, before, inner, ends, far, wx, wy, group, strength),
         scratch=(
             pltpu.VMEM((per_device, width_x, pad, width_y), F32),
             pltpu.SemaphoreType.DMA((per_device * width_x,)),
         ),
-        far_out=True,
+        far_out=(0,),
         name="output",
         cost=4000000,
     )
@@ -637,26 +678,33 @@
     else:
         strip = [south_surface, surface, north_surface]
     n_rim = len(strip)
-    whole = jnp.concatenate(strip, axis=0)
+    rows = per_device * width_x
+    (whole,) = call(join_kernel, [(n_rim * rows, width_y)], (*strip, token), name="join")
+    surface_before = ring(whole, "tiles", 1)
     surface_after = ring(whole, "tiles", -1)
-    surface_before = ring(whole, "tiles", 1)
-    rows = per_device * width_x
-    looked_up = functools.partial(sense_kernel, width_x, width_y, tiles, subs, per_device, n_rim)
-
-    def sense_here(cell_ref, weight_ref, *rest):
-        *here, out_ref = rest
-        looked_up([(0, k, ref, 0) for k, ref in enumerate(here)], cell_ref, weight_ref, None, out_ref)
-
-    def sense_beside(step, cell_ref, weight_ref, partial_ref, block_ref, out_ref):
-        blocks = [(step, k, block_ref, k * rows) for k in range(n_rim)]
-        looked_up(blocks, cell_ref, weight_ref, partial_ref, out_ref)
-
-    sensed_shape = [(per_device, cell.shape[1])]
-    (sensed,) = call(sense_here, sensed_shape, (cell, weight, *strip), name="sense_here", cost=2000000)
-    for step, block in ((1, surface_after), (-1, surface_before)):
-        (sensed,) = call(
-            functools.partial(sense_beside, step), sensed_shape, (cell, weight, sensed, block), name="sense_beside", cost=2000000
-        )
+    slots, elements = cell.shape
+    hot, share = call(
+        functools.partial(tables_kernel, dims, tiles, subs, n_rim),
+        [((slots, n_rim * width_y, elements), BF16), (slots, 3 * width_x, elements)],
+        (cell, weight),
+        name="tables",
+        cost=2000000,
+    )
+    (partial,) = call(
+        functools.partial(sense_here_kernel, dims, per_device),
+        [(per_device, elements)],
+        (hot, share, *strip),
+        name="sense_here",
+        cost=2000000,
+    )
+    (sensed,) = call(
+        functools.partial(sense_kernel, dims, per_device, n_rim),
+        [(per_device, elements)],
+        (hot, share, partial, surface_before, surface_after),
+        scratch=(pltpu.VMEM((per_device, elements), F32), pltpu.SemaphoreType.DMA),
+        far_out=(0,),
+        name="sense",
+    )
     return (field.reshape(per_device, lev, width_x, width_y), sensed)
 
 

time: 32 us -> 29 us (0.906)
  waiting for transfers between devices: 6.87 us -> 4.69 us
  Pallas kernels: 12 us -> 10.7 us
  starting transfers between devices: 11.7 us -> 12.7 us
  local copies, waits for them, and re-layouts: 0.61 us -> 0 us
    ppermute x6, waiting for transfers between devices: 6.87 us -> 4.69 us  [ring(): lax.ppermute(value, axis, [(i, (i + steps) % count) for i in range(count)])]
    pallas_call x9 -> x10, Pallas kernels: 12 us -> 10.7 us  [call(): pl.pallas_call(kernel, out_shape=[(jax.ShapeDtypeStruct if at in far_out...]
    ppermute x6, starting transfers between devices: 11.7 us -> 12.7 us  [ring(): lax.ppermute(value, axis, [(i, (i + steps) % count) for i in range(count)])]
    unnamed x2 -> x0, local copies, waits for them, and re-layouts: 0.61 us -> none
  transfers between devices with their start and end apart: 6 -> 6, of which waited for: 4 -> 3; matrix products, arithmetic and copies ran while one was open for 0% -> 0% of each run, Pallas kernels for 22% -> 19%
where the time goes in v3:
time: 29 us; the launch traced here: 28.8 us
  starting transfers between devices  12.7 us (44%)
  Pallas kernels  10.7 us (37%)
  waiting for transfers between devices  4.69 us (16%)
  between operations  0.71 us (2%)
    ppermute x6, starting transfers between devices, ring(): lax.ppermute(value, axis, [(i, (i + steps) % count) for i in range(count)])  12.7 us
    pallas_call x10, Pallas kernels, call(): pl.pallas_call(kernel, out_shape=[(jax.ShapeDtypeStruct if at in far_out...  10.7 us
    ppermute x6, waiting for transfers between devices, ring(): lax.ppermute(value, axis, [(i, (i + steps) % count) for i in range(count)])  4.69 us
  transfers between devices with their start and end apart: 6, of which 3 were waited for; matrix products, arithmetic and copies ran while one was open for 0% of the time, Pallas kernels for 19%

profile of v3, /device:TPU:0, one launch (start us, length us, event | category | flops | bytes accessed | tf_op | source)
XLA Modules:
  0.0 28.8 jit_solution(16534038708344744653)
XLA Ops:
  0.6 2.2 %fetch.1 = (f32[640,128]{1,0:T(8,128)S(1)}, f32[640,128]{1,0:T(8,128)S(1)}, f32[640,128]{1,0:T(8,128)S(1)}, f32[16,128]{1,0:T(8,128)S(1)}, s32[16,128]{1,0:T(8,1...) custom-call(f32[576,128]{1,0:T(8,128)} %bitcast.6, ...), custom_call_target="tpu_custom_call" | custom-call | tf_op jit(solution)/shard_map/fetch/pallas_call | solution.py:22
  2.9 3.0 %collective-permute-start = (f32[88,128]{1,0:T(8,128)S(1)}, f32[88,128]{1,0:T(8,128)S(1)}, u32[]{:S(2)}, u32[]{:S(2)}) collective-permute-start(f32[88,128]{1,0:T(8,128)S(1)} %get-tuple-element.22.refs_0_), channel_id=1, source_target_pairs={{0,2},{2,0},{1,3},{3,1},{4,6},{6,4},{5,7},{7,5},{8,10},{10,8},{9,1... | collective-permute-start | bytes 135176 | tf_op jit(solution)/shard_map/ppermute | solution.py:574
  5.9 0.3 first_mix.1.refs_3_.c_ref.refs_4_
  6.2 1.8 %collective-permute-done.refs_1_.refs_2_ = f32[88,128]{1,0:T(8,128)S(1)} collective-permute-done((f32[88,128]{1,0:T(8,128)S(1)}, f32[88,128]{1,0:T(8,128)S(1)}, u32[]{:S(2)}, u32[]{:S(2)}) %collective-permute-start) | collective-permute-done | bytes 45088 | tf_op jit(solution)/shard_map/ppermute | solution.py:574
  7.9 0.3 %pack_ends.1 = (f32[208,128]{1,0:T(8,128)S(1)}, f32[188,128]{1,0:T(8,128)S(1)}, f32[152,128]{1,0:T(8,128)S(1)}) custom-call(f32[88,128]{1,0:T(8,128)S(1)} %get-tuple-element.22.refs_0_, f32[88,128]{1,0:T(8,128)S(1)} %collective-permute-done.refs_1_.refs_2_, f32[88,128]{1,0:T(8,128)S(1)} %collective-permute-done.refs_1_.refs_2_, ...), custom_call_target="tpu_custom_call" | custom-call | tf_op jit(solution)/shard_map/pack_ends/pallas_call | solution.py:22
  8.2 2.2 %collective-permute-start.1 = (f32[188,128]{1,0:T(8,128)S(1)}, f32[188,128]{1,0:T(8,128)S(1)}, u32[]{:S(2)}, u32[]{:S(2)}) collective-permute-start(f32[188,128]{1,0:T(8,128)S(1)} %get-tuple-element.31), channel_id=1, source_target_pairs={{0,4},{4,8},{8,12},{12,0},{1,5},{5,9},{9,13},{13,1},{2,6},{6,10},{... | collective-permute-start | bytes 288776 | tf_op jit(solution)/shard_map/ppermute | solution.py:574
  10.4 2.1 %collective-permute-start.2 = (f32[152,128]{1,0:T(8,128)S(1)}, f32[152,128]{1,0:T(8,128)S(1)}, u32[]{:S(2)}, u32[]{:S(2)}) collective-permute-start(f32[152,128]{1,0:T(8,128)S(1)} %get-tuple-element.32), channel_id=1, source_target_pairs={{0,12},{4,0},{8,4},{12,8},{1,13},{5,1},{9,5},{13,9},{2,14},{6,2},{... | collective-permute-start | bytes 233480 | tf_op jit(solution)/shard_map/ppermute | solution.py:574
  12.5 1.3 %inner.1.refs_3_.refs_2_ = f32[4,14,40,128]{3,2,1,0:T(8,128)S(1)} custom-call(f32[208,128]{1,0:T(8,128)S(1)} %get-tuple-element.30.rim_ref.refs_0_, f32[16,40,128]{2,1,0:T(8,128)S(1)} %first_mix.1.refs_3_.c_ref.refs_4_, f32[640,128]{1,0:T(8,128)S(1)} %get-tuple-element.27.refs_4_.wx_ref.refs_5_, f32[640,128]{1,0:T(8,128)S(1)} %get-tuple-element.28.refs_5_.wy_ref.refs_6_, ...), custom_call_target="tpu_custom_call" | custom-call | flops 4000000 | bytes 4000000 | tf_op jit(solution)/shard_map/inner/pallas_call | solution.py:22
  13.8 2.0 %collective-permute-done.2.refs_2_ = f32[152,128]{1,0:T(8,128)S(1)} collective-permute-done((f32[152,128]{1,0:T(8,128)S(1)}, f32[152,128]{1,0:T(8,128)S(1)}, u32[]{:S(2)}, u32[]{:S(2)}) %collective-permute-start.2) | collective-permute-done | bytes 77856 | tf_op jit(solution)/shard_map/ppermute | solution.py:574
  15.9 0.0 collective-permute-done.1.refs_1_
  15.9 1.1 %ends.1 = (f32[4,4,40,128]{3,2,1,0:T(8,128)S(1)}, f32[2,48,128]{2,1,0:T(8,128)S(1)}, f32[64,128]{1,0:T(8,128)S(1)}) custom-call(f32[208,128]{1,0:T(8,128)S(1)} %get-tuple-element.30.rim_ref.refs_0_, f32[188,128]{1,0:T(8,128)S(1)} %collective-permute-done.1.refs_1_, f32[152,128]{1,0:T(8,128)S(1)} %collective-permute-done.2.refs_2_, ...), custom_call_target="tpu_custom_call" | custom-call | tf_op jit(solution)/shard_map/ends/pallas_call | solution.py:22
  16.9 1.6 %collective-permute-start.3 = (f32[64,128]{1,0:T(8,128)S(1)}, f32[64,128]{1,0:T(8,128)S(1)}, u32[]{:S(2)}, u32[]{:S(2)}) collective-permute-start(f32[64,128]{1,0:T(8,128)S(1)} %get-tuple-element.40.refs_0_), channel_id=1, source_target_pairs={{0,2},{2,0},{1,3},{3,1},{4,6},{6,4},{5,7},{7,5},{8,10},{10,8},{9,1... | collective-permute-start | bytes 98312 | tf_op jit(solution)/shard_map/ppermute | solution.py:574
  18.5 2.5 %output.1 = (f32[4,36,16,1,128]{4,3,2,1,0:T(1,128)}, f32[8,128]{1,0:T(8,128)S(1)}) custom-call(f32[208,128]{1,0:T(8,128)S(1)} %get-tuple-element.30.rim_ref.refs_0_, f32[188,128]{1,0:T(8,128)S(1)} %collective-permute-done.1.refs_1_, f32[4,14,40,128]{3,2,1,0:T(8,128)S(1)} %inner.1.refs_3_.refs_2_, f32[4,4,40,128]{3,2,1,0:T(8,128)S(1)} %get-tuple-element.33.refs_3_, ...), custom_call_target="tpu_custom_call" | custom-call | flops 4000000 | bytes 4000000 | tf_op jit(solution)/shard_map/output/pallas_call | solution.py:22
  21.0 0.0 collective-permute-done.3.refs_1_
  21.0 0.9 %collective-permute-start.4 = (f32[128,128]{1,0:T(8,128)S(1)}, f32[128,128]{1,0:T(8,128)S(1)}, u32[]{:S(2)}, u32[]{:S(2)}) collective-permute-start(f32[128,128]{1,0:T(8,128)S(1)} %join.1), channel_id=1, source_target_pairs={{0,4},{4,8},{8,12},{12,0},{1,5},{5,9},{9,13},{13,1},{2,6},{6,10},{... | collective-permute-start | bytes 196616 | tf_op jit(solution)/shard_map/ppermute | solution.py:574
  21.9 3.0 %collective-permute-start.5 = (f32[128,128]{1,0:T(8,128)S(1)}, f32[128,128]{1,0:T(8,128)S(1)}, u32[]{:S(2)}, u32[]{:S(2)}) collective-permute-start(f32[128,128]{1,0:T(8,128)S(1)} %join.1), channel_id=1, source_target_pairs={{0,12},{4,0},{8,4},{12,8},{1,13},{5,1},{9,5},{13,9},{2,14},{6,2},{... | collective-permute-start | bytes 196616 | tf_op jit(solution)/shard_map/ppermute | solution.py:574
  24.9 0.8 %tables.1 = (bf16[8,256,768]{2,1,0:T(8,128)(2,1)S(1)}, f32[8,48,768]{2,1,0:T(8,128)S(1)}) custom-call(s32[8,768]{1,0:T(8,128)S(1)} %get-tuple-element.36.cell_ref, f32[8,768]{1,0:T(8,128)S(1)} %get-tuple-element.37.weight_ref), custom_call_target="tpu_custom_call" | custom-call | flops 2000000 | bytes 2000000 | tf_op jit(solution)/shard_map/tables/pallas_call | solution.py:22
  25.7 0.6 %sense_here.1.partial_ref = f32[4,768]{1,0:T(4,128)S(1)} custom-call(bf16[8,256,768]{2,1,0:T(8,128)(2,1)S(1)} %get-tuple-element.38.hot_ref, f32[8,48,768]{2,1,0:T(8,128)S(1)} %get-tuple-element.39.share_ref, f32[64,128]{1,0:T(8,128)S(1)} %get-tuple-element.40.refs_0_, f32[64,128]{1,0:T(8,128)S(1)} %collective-permute-done.3.refs_1_), custom_call_target="tpu_custom_call" | custom-call | flops 2000000 | bytes 2000000 | tf_op jit(solution)/shard_map/sense_here/pallas_call | solution.py:22
  26.3 0.9 %collective-permute-done.4.before_ref = f32[128,128]{1,0:T(8,128)S(1)} collective-permute-done((f32[128,128]{1,0:T(8,128)S(1)}, f32[128,128]{1,0:T(8,128)S(1)}, u32[]{:S(2)}, u32[]{:S(2)}) %collective-permute-start.4) | collective-permute-done | bytes 65568 | tf_op jit(solution)/shard_map/ppermute | solution.py:574
  27.2 0.0 collective-permute-done.5.after_ref
  27.2 1.6 %sense.1 = f32[4,768]{1,0:T(4,128)} custom-call(bf16[8,256,768]{2,1,0:T(8,128)(2,1)S(1)} %get-tuple-element.38.hot_ref, f32[8,48,768]{2,1,0:T(8,128)S(1)} %get-tuple-element.39.share_ref, f32[4,768]{1,0:T(4,128)S(1)} %sense_here.1.partial_ref, f32[128,128]{1,0:T(8,128)S(1)} %collective-permute-done.4.before_ref, f32[128,128]{1,0:T(8,128)S(1)} %collective-permute-done.5.after_ref), custom_call_target="tpu_custom_call" | custom-call | tf_op jit(solution)/shard_map/sense/pallas_call | solution.py:22
  (1 shorter events, 0.0 us)
Async XLA Ops:
  2.9 5.1 %collective-permute-start = (f32[88,128]{1,0:T(8,128)S(1)}, f32[88,128]{1,0:T(8,128)S(1)}, u32[]{:S(2)}, u32[]{:S(2)}) collective-permute-start(f32[88,128]{1,0:T(8,128)S(1)} %get-tuple-element.22.refs_0_), channel_id=1, source_target_pairs={{0,2},{2,0},{1,3},{3,1},{4,6},{6,4},{5,7},{7,5},{8,10},{10,8},{9,1... | collective-permute-start | bytes 135176 | tf_op jit(solution)/shard_map/ppermute | solution.py:574
  8.2 7.6 %collective-permute-start.1 = (f32[188,128]{1,0:T(8,128)S(1)}, f32[188,128]{1,0:T(8,128)S(1)}, u32[]{:S(2)}, u32[]{:S(2)}) collective-permute-start(f32[188,128]{1,0:T(8,128)S(1)} %get-tuple-element.31), channel_id=1, source_target_pairs={{0,4},{4,8},{8,12},{12,0},{1,5},{5,9},{9,13},{13,1},{2,6},{6,10},{... | collective-permute-start | bytes 288776 | tf_op jit(solution)/shard_map/ppermute | solution.py:574
  10.4 5.5 %collective-permute-start.2 = (f32[152,128]{1,0:T(8,128)S(1)}, f32[152,128]{1,0:T(8,128)S(1)}, u32[]{:S(2)}, u32[]{:S(2)}) collective-permute-start(f32[152,128]{1,0:T(8,128)S(1)} %get-tuple-element.32), channel_id=1, source_target_pairs={{0,12},{4,0},{8,4},{12,8},{1,13},{5,1},{9,5},{13,9},{2,14},{6,2},{... | collective-permute-start | bytes 233480 | tf_op jit(solution)/shard_map/ppermute | solution.py:574
  16.9 4.0 %collective-permute-start.3 = (f32[64,128]{1,0:T(8,128)S(1)}, f32[64,128]{1,0:T(8,128)S(1)}, u32[]{:S(2)}, u32[]{:S(2)}) collective-permute-start(f32[64,128]{1,0:T(8,128)S(1)} %get-tuple-element.40.refs_0_), channel_id=1, source_target_pairs={{0,2},{2,0},{1,3},{3,1},{4,6},{6,4},{5,7},{7,5},{8,10},{10,8},{9,1... | collective-permute-start | bytes 98312 | tf_op jit(solution)/shard_map/ppermute | solution.py:574
  21.0 6.2 %collective-permute-start.4 = (f32[128,128]{1,0:T(8,128)S(1)}, f32[128,128]{1,0:T(8,128)S(1)}, u32[]{:S(2)}, u32[]{:S(2)}) collective-permute-start(f32[128,128]{1,0:T(8,128)S(1)} %join.1), channel_id=1, source_target_pairs={{0,4},{4,8},{8,12},{12,0},{1,5},{5,9},{9,13},{13,1},{2,6},{6,10},{... | collective-permute-start | bytes 196616 | tf_op jit(solution)/shard_map/ppermute | solution.py:574
  21.9 5.3 %collective-permute-start.5 = (f32[128,128]{1,0:T(8,128)S(1)}, f32[128,128]{1,0:T(8,128)S(1)}, u32[]{:S(2)}, u32[]{:S(2)}) collective-permute-start(f32[128,128]{1,0:T(8,128)S(1)} %join.1), channel_id=1, source_target_pairs={{0,12},{4,0},{8,4},{12,8},{1,13},{5,1},{9,5},{13,9},{2,14},{6,2},{... | collective-permute-start | bytes 196616 | tf_op jit(solution)/shard_map/ppermute | solution.py:574

commit v4 on v3

--- a/solution.py
+++ b/solution.py
@@ -12,6 +12,7 @@
 F32 = jnp.float32
 BF16 = jnp.bfloat16
 VMEM_BYTES = 16 << 20
+RIM_TILES = 6
 
 
 def call(kernel, outs, args, scratch=(), far_in=False, far_out=(), name=None, cost=0):
@@ -75,10 +76,10 @@
     deep = lhs.shape[1] // 3
     half = 4 * width_x
     whole = lev * width_x
+    copies = [pltpu.make_async_copy(s, t, sem.at[i]) for i, (s, t) in enumerate(zip(sources[3:], refs[12:18]))]
     targets = [ref.at[pl.ds(0, whole), :] for ref in (kernel, wx, wy)]
-    targets += [innov, cluster, strength, matrix, cell, weight]
-    copies = [pltpu.make_async_copy(s, t, sem.at[i]) for i, (s, t) in enumerate(zip(sources, targets))]
-    for copy in copies:
+    large = [pltpu.make_async_copy(s, t, sem.at[6 + i]) for i, (s, t) in enumerate(zip(sources, targets))]
+    for copy in copies[:4] + large + copies[4:]:
         copy.start()
     for ref in (kernel, wx, wy):
         ref[pl.ds(whole, (pad - lev) * width_x), :] = jnp.zeros(((pad - lev) * width_x, lanes), F32)
@@ -92,12 +93,11 @@
         return value
 
     def packed_row(value):
-        row = jnp.zeros((1, lanes), F32)
-        for x in range(width_x):
-            row = jnp.where(slot == x, turn(value[x : x + 1], 4 * x + 2), row)
-        return row
-
-    for copy in copies[3:7]:
+        moved = pltpu.roll(value, 2, 1, stride=4, stride_axis=0)
+        own = lax.broadcasted_iota(jnp.int32, value.shape, 0) == slot
+        return jnp.sum(jnp.where(own, moved, 0.0), axis=0, keepdims=True)
+
+    for copy in copies[:4]:
         copy.wait()
     rim[2 * pad : 2 * pad + 1, :] = packed_row(innov[...])
     rim[2 * pad + 1 : 2 * pad + 2, :] = packed_row(cluster[...].astype(F32))
@@ -108,31 +108,57 @@
     turned = jnp.concatenate([turned, jnp.zeros((pad, deep - lev), F32)], axis=1)
     high = turned.astype(BF16).astype(F32)
     lhs[...] = jnp.concatenate([high, turned - high, high], axis=1).astype(BF16)
-    for copy in copies[:3]:
+    groups = [slice(8 * r, 8 * r + 8) for r in range(pad // 8)]
+    large[0].wait()
+    lower = [packed(kernel, 0, r) for r in range(pad // 8)]
+    large[2].wait()
+    for r, rows in enumerate(groups):
+        rim[rows, :] = jnp.where(slot * 4 >= half, packed(wy, half, r), lower[r])
+    large[1].wait()
+    for r in range(pad // 8):
+        rim[pad + 8 * r : pad + 8 * r + 8, :] = packed(wx, 0, r)
+    for copy in copies[4:]:
         copy.wait()
-    for r in range(pad // 8):
-        rim[8 * r : 8 * r + 8, :] = jnp.where(slot * 4 >= half, packed(wy, half, r), packed(kernel, 0, r))
-        rim[pad + 8 * r : pad + 8 * r + 8, :] = packed(wx, 0, r)
-    for copy in copies[7:]:
-        copy.wait()
-
-
-def first_mix_kernel(dims, kernel_ref, innov_ref, strength_ref, lhs_ref, out_ref):
+
+
+def first_mix_kernel(dims, *refs):
     lev, width_x, lanes = dims
+    kernel_ref, innov_ref, strength_ref, lhs_ref, wx_ref, wy_ref, cluster_ref, out_ref, east_ref, west_ref = refs
     pad = round_up(lev, 8)
     lhs = lhs_ref[...]
-    for x in range(0, width_x, 2):
-        tiles = [kernel_ref[pl.ds(at, pad, stride=width_x), :] * innov_ref[at : at + 1, :] for at in (x, x + 1)]
+    last = width_x - 1
+    cluster = cluster_ref[...].astype(F32)
+    held = {}
+    order = [0, width_x - 2] + list(range(2, width_x - 2, 2))
+
+    def column(ref, x):
+        return ref[pl.ds(x, pad, stride=width_x), :]
+
+    def put(ref, tiles, near, next_one):
+        for at, value in enumerate(tiles):
+            top = min(pad, ref.shape[0] - at * lev)
+            ref[at * lev : at * lev + top, :] = value[:top]
+        base = len(tiles) * lev
+        ref[base : base + 1, :] = cluster[near : near + 1]
+        ref[base + 1 : base + 2, :] = cluster[next_one : next_one + 1]
+        ref[base + 2 : base + 3, :] = strength_ref[near : near + 1, :]
+        ref[base + 3 : base + 4, :] = jnp.zeros((1, lanes), F32)
+
+    for x in order:
+        tiles = [column(kernel_ref, at) * innov_ref[at : at + 1, :] for at in (x, x + 1)]
         mixed = mix(lhs, jnp.concatenate(tiles, axis=1))
         for k, tile in enumerate(tiles):
             part = mixed[:, k * lanes : (k + 1) * lanes]
-            out_ref[x + k, :, :] = tile + strength_ref[x + k : x + k + 1, :] * (part - tile)
-
-
-def pack_ends_kernel(dims, subs, *refs):
+            held[x + k] = tile + strength_ref[x + k : x + k + 1, :] * (part - tile)
+            out_ref[x + k, :, :] = held[x + k]
+        if x == width_x - 2:
+            ends = (held[last], held[last - 1], column(wx_ref, last), column(wy_ref, last), column(wx_ref, last - 1))
+            put(east_ref, ends, last, last - 1)
+            put(west_ref, (held[0], held[1], column(wx_ref, 0), column(wy_ref, 0)), 0, 1)
+
+
+def rim_kernel(dims, subs, own_ref, south_ref, north_ref, lhs_ref, rim_ref):
     lev, width_x, lanes = dims
-    own_ref, south_ref, north_ref, c_ref, wx_ref, wy_ref, cluster_ref, strength_ref, lhs_ref = refs[:9]
-    rim_ref, east_ref, west_ref = refs[9:]
     pad = round_up(lev, 8)
     half = 4 * width_x
     cross = lax.axis_index("sub")
@@ -159,42 +185,13 @@
     own_wy = jnp.where(lower, turn(own, half), 0.0)
     far_wy = jnp.where(lower, turn(far, half), 0.0)
     far_wx = halo(slice(pad, 2 * pad))
-    for at, value in enumerate((rim_c, far_c, own_wy, far_wy, far_wx)):
+    for at, value in enumerate((rim_c, far_c, own_wy, far_wy, far_wx, own_ref[pad : 2 * pad, :])):
         rim_ref[at * pad : (at + 1) * pad, :] = value
-    base = 5 * pad
+    base = RIM_TILES * pad
     rim_ref[base : base + 1, :] = own_misc[1:2]
-    rim_ref[base + 1 : base + 2, :] = far_misc[1:2]
-    rim_ref[base + 2 : base + 8, :] = far_misc[2:8]
-
-    last = width_x - 1
-    cluster = cluster_ref[...].astype(F32)
-
-    def upright(value):
-        square = jnp.concatenate([value, jnp.zeros((lanes - pad, lanes), F32)], axis=0).T
-        return square[0:4], square[4 * last : 4 * last + 4]
-
-    corners = [
-        c + turn(wy, pad) + turn(wx, 2 * pad)
-        for c, wy, wx in zip(upright(far_c), upright(far_wy), upright(far_wx))
-    ]
-
-    def put(ref, tiles, near, next_one, corner):
-        for at, value in enumerate(tiles):
-            top = min(pad, ref.shape[0] - at * lev)
-            ref[at * lev : at * lev + top, :] = value[:top]
-        base = len(tiles) * lev
-        ref[base : base + 1, :] = cluster[near : near + 1]
-        ref[base + 1 : base + 2, :] = cluster[next_one : next_one + 1]
-        ref[base + 2 : base + 3, :] = strength_ref[near : near + 1, :]
-        ref[base + 3 : base + 4, :] = turn(far_misc[1:2], -4 * near)
-        ref[base + 4 : base + 8, :] = corner
-
-    def column(ref, x):
-        return ref[pl.ds(x, pad, stride=width_x), :]
-
-    ends = (c_ref[last], c_ref[last - 1], column(wx_ref, last), column(wy_ref, last), column(wx_ref, last - 1))
-    put(east_ref, ends, last, last - 1, corners[1])
-    put(west_ref, (c_ref[0], c_ref[1], column(wx_ref, 0), column(wy_ref, 0)), 0, 1, corners[0])
+    rim_ref[base + 1 : base + 3, :] = far_misc[1:3]
+    rim_ref[base + 3 : base + 4, :] = own_misc[2:3]
+    rim_ref[base + 4 : base + 8, :] = jnp.zeros((4, lanes), F32)
 
 
 def rates_of(wx, wx_west, wy, wy_south):
@@ -330,17 +327,20 @@
     return [first + a for a in range(per_device)]
 
 
-def inner_kernel(dims, per_device, rim_ref, c_ref, wx_ref, wy_ref, cluster_ref, strength_ref, lhs_ref, mixed_ref):
+def inner_kernel(
+    dims, per_device, rim_ref, c_ref, wx_ref, wy_ref, cluster_ref, strength_ref, lhs_ref, mixed_ref, ground_ref
+):
     lev, width_x, lanes = dims
     pad = round_up(lev, 8)
     at = Columns(dims, c_ref, wx_ref, wy_ref, cluster_ref, strength_ref)
-    base = 5 * pad
+    base = RIM_TILES * pad
     rim = Rim(rim_ref[pad : 2 * pad, :], rim_ref[3 * pad : 4 * pad, :], rim_ref[base + 1 : base + 2, :])
     ids = adjoint_ids(per_device)
     lhs = lhs_ref[...]
     for x in range(1, width_x - 1):
         for a, value in enumerate(advance(dims, ids, lhs, x, at, rim)):
             mixed_ref[a, x - 1, :, :] = value
+            ground_ref[a, x + 1 : x + 2, :] = value[0:1]
 
 
 def mixed_at(dims, inner_ref, ends_ref, a, x, r):
@@ -373,8 +373,8 @@
 
 def ends_kernel(dims, subs, per_device, *refs):
     lev, width_x, lanes = dims
-    rim_ref, before_ref, after_ref, inner_ref, c_ref, wx_ref, wy_ref, cluster_ref, strength_ref, lhs_ref = refs[:10]
-    ends_ref, far_ref, surface_ref = refs[10:]
+    rim_ref, before_ref, after_ref, inner_ground_ref, c_ref, wx_ref, wy_ref, cluster_ref, strength_ref, lhs_ref = refs[:10]
+    ends_ref, far_ref, surface_ref, full_ref, ground_ref, west_ref, beside_ref = refs[10:]
     pad = round_up(lev, 8)
     half = 4 * width_x
     cross = lax.axis_index("sub")
@@ -386,31 +386,46 @@
     ids = adjoint_ids(per_device)
     lhs = lhs_ref[...]
 
-    def upright(ref, tiles):
-        rows = ref[tiles * lev + 4 : tiles * lev + 8, :]
-        square = jnp.concatenate([rows, jnp.zeros((lanes - 4, lanes), F32)], axis=0).T
-        return [square[i * pad : (i + 1) * pad] for i in range(3)]
-
-    def with_corners(value, before, after):
-        return jnp.where(before_slot, turn(before, -4), jnp.where(after_slot, turn(after, half), value))
-
-    corner_before = upright(before_ref, 5)
-    corner_after = upright(after_ref, 4)
-    base = 5 * pad
-    rim_c = rim_ref[0:pad, :]
-    rim_wy = rim_ref[2 * pad : 3 * pad, :]
-    far_c = with_corners(rim_ref[pad : 2 * pad, :], corner_before[0], corner_after[0])
-    far_wy = with_corners(rim_ref[3 * pad : 4 * pad, :], corner_before[1], corner_after[1])
-    far_wx = with_corners(rim_ref[4 * pad : 5 * pad, :], corner_before[2], corner_after[2])
+    base = RIM_TILES * pad
+    rim_c, far_c, rim_wy, far_wy, far_wx, rim_wx = (rim_ref[i * pad : (i + 1) * pad, :] for i in range(RIM_TILES))
     rim_cluster = rim_ref[base : base + 1, :]
-    far_cluster = with_corners(
-        rim_ref[base + 1 : base + 2, :], at.misc(before_ref, 5, 3), at.misc(after_ref, 4, 3)
-    )
+    far_cluster = rim_ref[base + 1 : base + 2, :]
     far_strength = rim_ref[base + 2 : base + 3, :]
     rim = Rim(far_c, far_wy, far_cluster)
-    for k, x in enumerate((-1, 0, width_x - 1, width_x)):
+
+    def sent(ref, tile):
+        return jnp.concatenate([at.sent(ref, tile, r) for r in range(pad // 8)], axis=0)
+
+    def full(value, before, after):
+        return jnp.where(before_slot, turn(before, -2), jnp.where(after_slot, turn(after, half + 2), value))
+
+    full_c = full(rim_c, sent(before_ref, 0), sent(after_ref, 0))
+    full_wy = full(rim_wy, sent(before_ref, 3), sent(after_ref, 3))
+    full_wx = full(rim_wx, sent(before_ref, 2), rim_wx)
+    for i, value in enumerate((full_c, full_wy, full_wx)):
+        full_ref[i * pad : (i + 1) * pad, :] = value
+    rows = [
+        full(rim_cluster, at.cluster(-1), at.cluster(width_x)),
+        full(rim_ref[base + 3 : base + 4, :], at.strength(-1), at.strength(width_x)),
+    ]
+    full_ref[3 * pad : 3 * pad + 2, :] = jnp.concatenate(rows, axis=0)
+    full_ref[3 * pad + 2 : 3 * pad + 8, :] = jnp.zeros((6, lanes), F32)
+    picked = jnp.where(before_slot | after_slot, full_c, 0.0)
+    wy_slot = (lane < 4) | (lane // 4 == width_x + 1)
+    wx_slot = lane // 4 == 1
+    moved_wy = full(jnp.zeros_like(rim_wy), turn(sent(before_ref, 3), 0), turn(sent(after_ref, 3), 0))
+    picked = jnp.where(wy_slot, turn(moved_wy, 4), picked)
+    picked = jnp.where(wx_slot, turn(sent(before_ref, 2), 6), picked).T
+    picked = jnp.concatenate([picked, jnp.zeros((lanes, lanes - pad), F32)], axis=1)
+    packet = picked[half : half + 8] + turn(picked[lanes - 8 : lanes], pad) + turn(picked[0:8], 2 * pad)
+    tail = per_device * width_x
+    surface_ref[tail : tail + 8, :] = packet
+    surface_ref[tail + 8 : tail + 10, :] = jnp.concatenate(rows, axis=0)
+    surface_ref[tail + 10 : tail + 16, :] = jnp.zeros((6, lanes), F32)
+    for k, x in ((1, 0), (2, width_x - 1), (0, -1), (3, width_x)):
         for a, value in enumerate(advance(dims, ids, lhs, x, at, rim)):
             ends_ref[a, k, :, :] = value
+            ground_ref[a, x + 1 : x + 2, :] = value[0:1]
 
     def rim_north(far, own):
         return turn(jnp.where(place == 2, own, far), -1)
@@ -443,19 +458,38 @@
     for pair in range(1, len(far_mixed)):
         far_ref[pair, pad : pad + 8, :] = jnp.zeros((8, lanes), F32)
 
-    def far(pair, r):
-        return far_mixed[pair][8 * r : 8 * r + 8]
-
+    rows = [rim.wy_tile[0:1]] + [turn(far_mixed[a // 2][0:1], half * (a % 2)) for a in range(per_device)]
+    tall = round_up(len(rows), 8)
+    stack = jnp.concatenate(rows + [jnp.zeros((tall - len(rows), lanes), F32)], axis=0)
     for x in range(width_x):
-        values = second_transport(dims, at, rim.wy(0), far, inner_ref, ends_ref, ids, x, 0)
-        for a, value in enumerate(values):
-            surface_ref[a * width_x + x : a * width_x + x + 1, :] = value[0:1]
+        beside_ref[x * tall : (x + 1) * tall, :] = halo_of(stack, x)
+
+    def beside(at_row):
+        return beside_ref[pl.ds(at_row, width_x, stride=tall), :]
+
+    west_ref[0:1, :] = at.sent(before_ref, 2, 0)[0:1]
+    west_ref[1 : width_x + 1, :] = wx_ref[0:width_x, :]
+    wx, wy = wx_ref[0:width_x, :], wy_ref[0:width_x, :]
+    south_wy = from_south(wy, beside(0))
+    center, east, west, north, south = rates_of(wx, west_ref[0:width_x, :], wy, south_wy)
+    for a in range(per_device):
+        ground_ref[a, 2:width_x, :] = inner_ground_ref[a, 2:width_x, :]
+        own = ground_ref[a, 1 : width_x + 1, :]
+        rim_rows = beside(1 + a)
+        parts = [
+            center * own,
+            east * ground_ref[a, 2 : width_x + 2, :],
+            west * ground_ref[a, 0:width_x, :],
+            north * from_north(own, rim_rows),
+            south * from_south(own, rim_rows),
+        ]
+        surface_ref[a * width_x : (a + 1) * width_x, :] = total(parts)
 
 
 def output_kernel(dims, per_device, *refs):
     lev, width_x, lanes = dims
     rim_ref, before_ref, inner_ref, ends_ref, far_ref, wx_ref, wy_ref, cluster_ref, strength_ref = refs[:9]
-    out_ref, token_ref, field_ref, sem = refs[9:]
+    out_ref, token_ref, edge_ref, field_ref, sem = refs[9:]
     token_ref[...] = jnp.zeros(token_ref.shape, F32)
     pad = round_up(lev, 8)
     at = Columns(dims, None, wx_ref, wy_ref, cluster_ref, strength_ref, before_ref)
@@ -471,8 +505,11 @@
             rim_wy = rim_wys[r]
             values = second_transport(dims, at, rim_wy, far, inner_ref, ends_ref, ids, x, r)
             for a, value in enumerate(values):
-                field_ref[a, x, 8 * r : 8 * r + 8, :] = value
-        for a in range(per_device):
+                if x in (0, width_x - 1):
+                    edge_ref[a, min(x, 1), 8 * r : 8 * r + 8, :] = value
+                else:
+                    field_ref[a, x, 8 * r : 8 * r + 8, :] = value
+        for a in range(per_device if 0 < x < width_x - 1 else 0):
             source = field_ref.at[a, x, pl.ds(0, lev), :]
             copies.append(pltpu.make_async_copy(source, out_ref.at[a, :, x, 0, :], sem.at[len(copies)]))
             copies[-1].start()
@@ -540,11 +577,11 @@
     return [slice(g, g + wide) for g in range(0, elements, wide)]
 
 
-def sense_here_kernel(dims, per_device, hot_ref, share_ref, *refs):
-    *here, out_ref = refs
-    blocks = [(0, [ref[...] for ref in here])]
+def sense_here_kernel(dims, per_device, n_rim, hot_ref, share_ref, here_ref, out_ref):
+    rows = per_device * dims[1]
+    blocks = [(0, [here_ref[k * rows : (k + 1) * rows, :] for k in range(n_rim)])]
     for lanes in wide_lanes(out_ref.shape[1]):
-        out_ref[:, lanes] = looked_up(dims, per_device, len(here), blocks, hot_ref, share_ref, lanes)
+        out_ref[:, lanes] = looked_up(dims, per_device, n_rim, blocks, hot_ref, share_ref, lanes)
 
 
 def sense_kernel(dims, per_device, n_rim, hot_ref, share_ref, partial_ref, before_ref, after_ref, out_ref, own_ref, sem):
@@ -561,12 +598,157 @@
     copy.wait()
 
 
-def join_kernel(*refs):
-    *parts, _, out_ref = refs
-    first = 0
-    for part in parts:
-        out_ref[first : first + part.shape[0], :] = part[...]
-        first += part.shape[0]
+class Seam:
+    def __init__(self, dims, c, wy, wx, cluster, strength):
+        _, self.width_x, lanes = dims
+        self.lane = lane_of((1, lanes))
+        self.place = self.lane % 4
+        slot = self.lane // 4
+        self.first, self.last = slot == 0, slot == self.width_x - 1
+        self.beside = (slot == lanes // 4 - 1) | (slot == self.width_x)
+        self.c, self.cluster, self.strength = c, cluster, strength
+        self.east = jnp.maximum(wx, 0.0)
+        self.west = jnp.maximum(-turn(wx, 4), 0.0)
+        self.north = jnp.maximum(wy, 0.0)
+        self.south = jnp.maximum(-turn(wy, 1), 0.0)
+
+    def missing(self, lhs, ids):
+        near = (self.place == 1) | (self.place == 2)
+        wanted_slots = near & (self.beside | self.first | self.last)
+        moved = [(turn(self.c, k), turn(self.cluster, k)) for k in (-1, 1, 4, -4)]
+        fields = []
+        for wanted in ids:
+            own = jnp.where(self.cluster == wanted, self.c, 0.0)
+            from_n, from_s, from_w, from_e = (jnp.where(row == wanted, c, 0.0) for c, row in moved)
+            upright = jnp.where(self.place == 1, self.north * from_n, self.south * (from_s - own))
+            level = jnp.where(self.first, self.west * (from_w - own), self.east * from_e)
+            fields.append(jnp.where(wanted_slots, jnp.where(self.beside, upright, level), 0.0))
+        return convect(lhs, fields, self.strength)
+
+
+def seam_transport(dims, rates, missing):
+    width_x = dims[1]
+    east, west, north, south = rates
+    lane = lane_of((1, missing.shape[1]))
+    place, slot = lane % 4, lane // 4
+    level = jnp.where(slot == 0, west * turn(missing, 4), east * turn(missing, -4))
+    return level + jnp.where(place == 1, north * turn(missing, -1), south * turn(missing, 1))
+
+
+def own_places(subs):
+    cross = lax.axis_index("sub")
+    if subs == 2:
+        own_south = (cross == 0).astype(jnp.int32)
+        return [own_south]
+    return [jnp.int32(0), jnp.int32(1)]
+
+
+def patch_kernel(dims, subs, per_device, n_rim, *refs):
+    lev, width_x, lanes = dims
+    rim_ref, full_ref, own_ref, south_ref, north_ref, lhs_ref, _, whole_ref, seam_ref = refs
+    pad = round_up(lev, 8)
+    half = 4 * width_x
+    rows = per_device * width_x
+    lane = lane_of((1, lanes))
+    southern = lane % 4 < 2
+    before_slot = lane >= lanes - 4
+    after_slot = lane // 4 == width_x
+    ids = adjoint_ids(per_device)
+    lhs = lhs_ref[...]
+    cross = lax.axis_index("sub")
+    present = jnp.where(southern, cross, subs - 1 - cross) > 0
+
+    def upright(ref):
+        turned = ref[rows : rows + 8, :].T
+        turned = jnp.concatenate([turned, jnp.zeros((lanes, lanes - 8), F32)], axis=1)
+        return [turned[i * pad : (i + 1) * pad] for i in range(3)]
+
+    def beyond(value, south, north, before, after):
+        def placed(tile):
+            moved = turn(tile[0], lanes - 4 - before)
+            return moved if after is None else jnp.where(after_slot, turn(tile[1], half - after), moved)
+
+        moved = placed(south) if south is north else jnp.where(southern, placed(south), placed(north))
+        moved = jnp.where(present, moved, 0.0)
+        slots = before_slot if after is None else before_slot | after_slot
+        return jnp.where(slots, moved, value)
+
+    south = upright(south_ref)
+    north = south if subs == 2 else upright(north_ref)
+
+    def pair(first, second):
+        one = (south[first], south[second])
+        return one, one if subs == 2 else (north[first], north[second])
+
+    far_c, far_wy, far_wx = (rim_ref[i * pad : (i + 1) * pad, :] for i in (1, 3, 4))
+    c_pair, wy_pair = pair(1, 0), pair(2, 0)
+    if subs == 2:
+        c_pair, wy_pair = (c_pair[0], c_pair[0]), (wy_pair[0], wy_pair[0])
+    far_c = beyond(far_c, *c_pair, 4, 0)
+    far_wx = beyond(far_wx, *wy_pair, 4, None)
+    far_wy = beyond(far_wy, *wy_pair, 0, 4)
+    base = RIM_TILES * pad
+
+    def beyond_row(value, at_row):
+        south_row = south_ref[rows + at_row : rows + at_row + 1, :]
+        north_row = north_ref[rows + at_row : rows + at_row + 1, :]
+        moved = jnp.where(present, jnp.where(southern, south_row, north_row), 0.0)
+        return jnp.where(before_slot | after_slot, moved, value)
+
+    far_cluster = beyond_row(rim_ref[base + 1 : base + 2, :], 8)
+    far_strength = beyond_row(rim_ref[base + 2 : base + 3, :], 9)
+    full_c, full_wy, full_wx = (full_ref[i * pad : (i + 1) * pad, :] for i in range(3))
+    full_cluster = full_ref[3 * pad : 3 * pad + 1, :]
+    full_strength = full_ref[3 * pad + 1 : 3 * pad + 2, :]
+    surfaces = [own_ref, south_ref] if subs == 2 else [south_ref, own_ref, north_ref]
+    for k, ref in enumerate(surfaces):
+        whole_ref[k * rows : (k + 1) * rows, :] = ref[0:rows, :]
+    for k, own_south in enumerate(own_places(subs)):
+        mine = jnp.where(southern, own_south, 1 - own_south) > 0
+        seam = Seam(
+            dims,
+            jnp.where(mine, full_c, far_c),
+            jnp.where(mine, full_wy, far_wy),
+            jnp.where(mine, full_wx, far_wx),
+            jnp.where(mine, full_cluster, far_cluster),
+            jnp.where(mine, full_strength, far_strength),
+        )
+        missing = seam.missing(lhs, ids)
+        rates = (seam.east, seam.west, seam.north, seam.south)
+        for i, value in enumerate(rates + tuple(missing)):
+            seam_ref[k, i * pad : (i + 1) * pad, :] = value
+        far_at = 1 if subs == 2 else 2 * k
+        own_at = 0 if subs == 2 else 1
+        own_lane = jnp.where(own_south > 0, lanes - 1, 0)
+        for a, value in enumerate(missing):
+            change = seam_transport(dims, [rate[0:8] for rate in rates], value[0:8])[0:1]
+            for x in (0, width_x - 1):
+                row = turn(change, -4 * x - 2)
+                for block, at_lane in ((own_at, own_lane), (far_at, lanes - 1 - own_lane)):
+                    at = block * rows + a * width_x + x
+                    whole_ref[at : at + 1, :] = whole_ref[at : at + 1, :] + jnp.where(lane == at_lane, row, 0.0)
+
+
+def output_ends_kernel(dims, subs, per_device, _, seam_ref, edge_ref, out_ref, done_ref, sem):
+    lev, width_x, lanes = dims
+    pad = round_up(lev, 8)
+    lane = lane_of((1, lanes))
+    copies = []
+    for a in range(per_device):
+        columns = [edge_ref[a, 0], edge_ref[a, 1]]
+        for k, own_south in enumerate(own_places(subs)):
+            rates = [seam_ref[k, i * pad : (i + 1) * pad, :] for i in range(4)]
+            change = seam_transport(dims, rates, seam_ref[k, (4 + a) * pad : (5 + a) * pad, :])
+            own = lane == jnp.where(own_south > 0, lanes - 1, 0)
+            for i, x in enumerate((0, width_x - 1)):
+                columns[i] = columns[i] + jnp.where(own, turn(change, -4 * x - 2), 0.0)
+        for i, x in enumerate((0, width_x - 1)):
+            done_ref[a, i, :, :] = columns[i]
+            source = done_ref.at[a, i, pl.ds(0, lev), :]
+            copies.append(pltpu.make_async_copy(source, out_ref.at[a, :, x, 0, :], sem.at[len(copies)]))
+            copies[-1].start()
+    for copy in copies:
+        copy.wait()
 
 
 def ring(value, axis, steps):
@@ -628,42 +810,49 @@
     )
     air, wx, wy, innov, group, strength, _, cell, weight, lhs, own_rim = fetched
     south_rim, north_rim = across(own_rim)
-    (first,) = call(
+    first, to_east, to_west = call(
         functools.partial(first_mix_kernel, dims),
-        [(width_x, pad, width_y)],
-        (air, innov, strength, lhs),
+        [(width_x, pad, width_y), (5 * lev + 4, width_y), (4 * lev + 4, width_y)],
+        (air, innov, strength, lhs, wx, wy, group),
         name="first_mix",
         cost=400000,
     )
-    rim, to_east, to_west = call(
-        functools.partial(pack_ends_kernel, dims, subs),
-        [(5 * pad + 8, width_y), (5 * lev + 8, width_y), (4 * lev + 8, width_y)],
-        (own_rim, south_rim, north_rim, first, wx, wy, group, strength, lhs),
-        name="pack_ends",
-    )
     before = ring(to_east, "tiles", 1)
     after = ring(to_west, "tiles", -1)
-    (inner,) = call(
+    (rim,) = call(
+        functools.partial(rim_kernel, dims, subs),
+        [(RIM_TILES * pad + 8, width_y)],
+        (own_rim, south_rim, north_rim, lhs),
+        name="rim",
+        cost=400000,
+    )
+    inner, ground = call(
         functools.partial(inner_kernel, dims, per_device),
-        [(per_device, width_x - 2, pad, width_y)],
+        [(per_device, width_x - 2, pad, width_y), (per_device, width_x + 8, width_y)],
         (rim, first, wx, wy, group, strength, lhs),
         name="inner",
         cost=4000000,
     )
-    ends, far, surface = call(
+    ends, far, surface, full = call(
         functools.partial(ends_kernel, dims, subs, per_device),
         [
             (per_device, 4, pad, width_y),
             ((per_device + 1) // 2, pad + 8, width_y),
-            (per_device * width_x, width_y),
+            (per_device * width_x + 16, width_y),
+            (3 * pad + 8, width_y),
         ],
-        (rim, before, after, inner, first, wx, wy, group, strength, lhs),
+        (rim, before, after, ground, first, wx, wy, group, strength, lhs),
+        scratch=(
+            pltpu.VMEM((per_device, width_x + 8, width_y), F32),
+            pltpu.VMEM((width_x + 8, width_y), F32),
+            pltpu.VMEM((width_x * round_up(per_device + 1, 8), width_y), F32),
+        ),
         name="ends",
     )
     south_surface, north_surface = across(surface)
-    field, token = call(
+    field, token, edge = call(
         functools.partial(output_kernel, dims, per_device),
-        [(per_device, lev, width_x, 1, width_y), (8, width_y)],
+        [(per_device, lev, width_x, 1, width_y), (8, width_y), (per_device, 2, pad, width_y)],
         (rim, before, inner, ends, far, wx, wy, group, strength),
         scratch=(
             pltpu.VMEM((per_device, width_x, pad, width_y), F32),
@@ -673,15 +862,29 @@
         name="output",
         cost=4000000,
     )
-    if subs == 2:
-        strip = [surface, south_surface]
-    else:
-        strip = [south_surface, surface, north_surface]
-    n_rim = len(strip)
+    n_rim = min(subs, 3)
     rows = per_device * width_x
-    (whole,) = call(join_kernel, [(n_rim * rows, width_y)], (*strip, token), name="join")
+    seams = 1 if subs == 2 else 2
+    whole, seam = call(
+        functools.partial(patch_kernel, dims, subs, per_device, n_rim),
+        [(n_rim * rows, width_y), (seams, (4 + per_device) * pad, width_y)],
+        (rim, full, surface, south_surface, north_surface, lhs, token),
+        name="patch",
+    )
     surface_before = ring(whole, "tiles", 1)
     surface_after = ring(whole, "tiles", -1)
+    near, hbm = pl.BlockSpec(memory_space=pltpu.VMEM), pl.BlockSpec(memory_space=pl.ANY)
+    field = pl.pallas_call(
+        functools.partial(output_ends_kernel, dims, subs, per_device),
+        out_shape=jax.ShapeDtypeStruct(field.shape, F32),
+        in_specs=[hbm, near, near],
+        out_specs=hbm,
+        scratch_shapes=[pltpu.VMEM((per_device, 2, pad, width_y), F32), pltpu.SemaphoreType.DMA((2 * per_device,))],
+        input_output_aliases={0: 0},
+        compiler_params=pltpu.CompilerParams(vmem_limit_bytes=VMEM_BYTES),
+        cost_estimate=pl.CostEstimate(flops=1000000, bytes_accessed=1000000, transcendentals=0),
+        name="output_ends",
+    )(field, *[pltpu.with_memory_space_constraint(v, pltpu.VMEM) for v in (seam, edge)])
     slots, elements = cell.shape
     hot, share = call(
         functools.partial(tables_kernel, dims, tiles, subs, n_rim),
@@ -691,9 +894,9 @@
         cost=2000000,
     )
     (partial,) = call(
-        functools.partial(sense_here_kernel, dims, per_device),
+        functools.partial(sense_here_kernel, dims, per_device, n_rim),
         [(per_device, elements)],
-        (hot, share, *strip),
+        (hot, share, whole),
         name="sense_here",
         cost=2000000,
     )

time: 29 us -> 27.9 us (0.962)
  waiting for transfers between devices: 4.69 us -> 2.41 us
  Pallas kernels: 10.7 us -> 12.1 us
  starting transfers between devices: 12.7 us -> 12.4 us
    ppermute x6, waiting for transfers between devices: 4.69 us -> 2.41 us  [ring(): lax.ppermute(value, axis, [(i, (i + steps) % count) for i in range(count)])]
    pallas_call x0 -> x1, Pallas kernels: none -> 0.94 us  [body(): pl.pallas_call(functools.partial(output_ends_kernel, dims, subs, per_devi...]
    pallas_call x10, Pallas kernels: 10.7 us -> 11.2 us  [call(): pl.pallas_call(kernel, out_shape=[(jax.ShapeDtypeStruct if at in far_out...]
  transfers between devices with their start and end apart: 6 -> 6, of which waited for: 3 -> 1; matrix products, arithmetic and copies ran while one was open for 0% -> 0% of each run, Pallas kernels for 19% -> 23%
where the time goes in v4:
time: 27.9 us; the launch traced here: 27.7 us
  starting transfers between devices  12.4 us (44%)
  Pallas kernels  12.1 us (43%)
  waiting for transfers between devices  2.41 us (9%)
  between operations  0.74 us (3%)
    ppermute x6, starting transfers between devices, ring(): lax.ppermute(value, axis, [(i, (i + steps) % count) for i in range(count)])  12.4 us
    pallas_call x10, Pallas kernels, call(): pl.pallas_call(kernel, out_shape=[(jax.ShapeDtypeStruct if at in far_out...  11.2 us
    ppermute x6, waiting for transfers between devices, ring(): lax.ppermute(value, axis, [(i, (i + steps) % count) for i in range(count)])  2.41 us
    pallas_call x1, Pallas kernels, body(): pl.pallas_call(functools.partial(output_ends_kernel, dims, subs, per_devi...  0.94 us
  transfers between devices with their start and end apart: 6, of which 1 were waited for; matrix products, arithmetic and copies ran while one was open for 0% of the time, Pallas kernels for 23%

profile of v4, /device:TPU:0, one launch (start us, length us, event | category | flops | bytes accessed | tf_op | source)
XLA Modules:
  0.0 27.7 jit_solution(10904457491994962582)
XLA Ops:
  0.6 2.2 %fetch.1 = (f32[640,128]{1,0:T(8,128)S(1)}, f32[640,128]{1,0:T(8,128)S(1)}, f32[640,128]{1,0:T(8,128)S(1)}, f32[16,128]{1,0:T(8,128)S(1)}, s32[16,128]{1,0:T(8,1...) custom-call(f32[576,128]{1,0:T(8,128)} %bitcast.7, ...), custom_call_target="tpu_custom_call" | custom-call | tf_op jit(solution)/shard_map/fetch/pallas_call | solution.py:23
  2.9 0.3 %first_mix.1 = (f32[16,40,128]{2,1,0:T(8,128)S(1)}, f32[184,128]{1,0:T(8,128)S(1)}, f32[148,128]{1,0:T(8,128)S(1)}) custom-call(f32[640,128]{1,0:T(8,128)S(1)} %get-tuple-element.30.refs_0_, f32[16,128]{1,0:T(8,128)S(1)} %get-tuple-element.31.refs_1_, f32[16,128]{1,0:T(8,128)S(1)} %get-tuple-element.32.refs_2_.strength_ref.refs_8_, ...), custom_call_target="tpu_custom_call" | custom-call | flops 400000 | bytes 400000 | tf_op jit(solution)/shard_map/first_mix/pallas_call | solution.py:23
  3.2 3.1 %collective-permute-start.1 = (f32[184,128]{1,0:T(8,128)S(1)}, f32[184,128]{1,0:T(8,128)S(1)}, u32[]{:S(2)}, u32[]{:S(2)}) collective-permute-start(f32[184,128]{1,0:T(8,128)S(1)} %get-tuple-element.36), channel_id=1, source_target_pairs={{0,4},{4,8},{8,12},{12,0},{1,5},{5,9},{9,13},{13,1},{2,6},{6,10},{... | collective-permute-start | bytes 282632 | tf_op jit(solution)/shard_map/ppermute | solution.py:756
  6.3 2.1 %collective-permute-start.2 = (f32[148,128]{1,0:T(8,128)S(1)}, f32[148,128]{1,0:T(8,128)S(1)}, u32[]{:S(2)}, u32[]{:S(2)}) collective-permute-start(f32[148,128]{1,0:T(8,128)S(1)} %get-tuple-element.39), channel_id=1, source_target_pairs={{0,12},{4,0},{8,4},{12,8},{1,13},{5,1},{9,5},{13,9},{2,14},{6,2},{... | collective-permute-start | bytes 227336 | tf_op jit(solution)/shard_map/ppermute | solution.py:756
  8.4 1.6 %collective-permute-start = (f32[88,128]{1,0:T(8,128)S(1)}, f32[88,128]{1,0:T(8,128)S(1)}, u32[]{:S(2)}, u32[]{:S(2)}) collective-permute-start(f32[88,128]{1,0:T(8,128)S(1)} %get-tuple-element.28.own_ref), channel_id=1, source_target_pairs={{0,2},{2,0},{1,3},{3,1},{4,6},{6,4},{5,7},{7,5},{8,10},{10,8},{9,1... | collective-permute-start | bytes 135176 | tf_op jit(solution)/shard_map/ppermute | solution.py:756
  10.0 2.4 %collective-permute-done.south_ref.north_ref = f32[88,128]{1,0:T(8,128)S(1)} collective-permute-done((f32[88,128]{1,0:T(8,128)S(1)}, f32[88,128]{1,0:T(8,128)S(1)}, u32[]{:S(2)}, u32[]{:S(2)}) %collective-permute-start) | collective-permute-done | bytes 45088 | tf_op jit(solution)/shard_map/ppermute | solution.py:756
  12.4 0.1 rim.1.rim_ref.refs_0_
  12.5 1.4 %inner.1 = (f32[4,14,40,128]{3,2,1,0:T(8,128)S(1)}, f32[4,24,128]{2,1,0:T(8,128)S(1)}) custom-call(f32[248,128]{1,0:T(8,128)S(1)} %rim.1.rim_ref.refs_0_, f32[16,40,128]{2,1,0:T(8,128)S(1)} %get-tuple-element.37.c_ref.refs_4_, f32[640,128]{1,0:T(8,128)S(1)} %get-tuple-element.33.refs_4_.wx_ref.refs_5_, ...), custom_call_target="tpu_custom_call" | custom-call | flops 4000000 | bytes 4000000 | tf_op jit(solution)/shard_map/inner/pallas_call | solution.py:23
  14.0 0.0 collective-permute-done.2.refs_2_
  14.0 0.0 collective-permute-done.1.refs_1_
  14.0 1.0 %ends.1 = (f32[4,4,40,128]{3,2,1,0:T(8,128)S(1)}, f32[2,48,128]{2,1,0:T(8,128)S(1)}, f32[80,128]{1,0:T(8,128)S(1)}, f32[128,128]{1,0:T(8,128)S(1)}) custom-call(f32[248,128]{1,0:T(8,128)S(1)} %rim.1.rim_ref.refs_0_, f32[184,128]{1,0:T(8,128)S(1)} %collective-permute-done.1.refs_1_, f32[148,128]{1,0:T(8,128)S(1)} %collective-permute-done.2.refs_2_, ...), custom_call_target="tpu_custom_call" | custom-call | tf_op jit(solution)/shard_map/ends/pallas_call | solution.py:23
  15.0 1.7 %collective-permute-start.3 = (f32[80,128]{1,0:T(8,128)S(1)}, f32[80,128]{1,0:T(8,128)S(1)}, u32[]{:S(2)}, u32[]{:S(2)}) collective-permute-start(f32[80,128]{1,0:T(8,128)S(1)} %get-tuple-element.45.refs_2_), channel_id=1, source_target_pairs={{0,2},{2,0},{1,3},{3,1},{4,6},{6,4},{5,7},{7,5},{8,10},{10,8},{9,1... | collective-permute-start | bytes 122888 | tf_op jit(solution)/shard_map/ppermute | solution.py:756
  16.7 2.4 %output.1 = (f32[4,36,16,1,128]{4,3,2,1,0:T(1,128)}, f32[8,128]{1,0:T(8,128)S(1)}, f32[4,2,40,128]{3,2,1,0:T(8,128)S(1)}) custom-call(f32[248,128]{1,0:T(8,128)S(1)} %rim.1.rim_ref.refs_0_, f32[184,128]{1,0:T(8,128)S(1)} %collective-permute-done.1.refs_1_, f32[4,14,40,128]{3,2,1,0:T(8,128)S(1)} %get-tuple-element.38.refs_2_, ...), custom_call_target="tpu_custom_call" | custom-call | flops 4000000 | bytes 4000000 | tf_op jit(solution)/shard_map/output/pallas_call | solution.py:23
  19.2 0.0 collective-permute-done.3.refs_3_.refs_4_
  19.2 0.6 %patch.1 = (f32[128,128]{1,0:T(8,128)S(1)}, f32[1,320,128]{2,1,0:T(8,128)S(1)}) custom-call(f32[248,128]{1,0:T(8,128)S(1)} %rim.1.rim_ref.refs_0_, f32[128,128]{1,0:T(8,128)S(1)} %get-tuple-element.44.refs_1_, f32[80,128]{1,0:T(8,128)S(1)} %get-tuple-element.45.refs_2_, f32[80,128]{1,0:T(8,128)S(1)} %collective-permute-done.3.refs_3_.refs_4_, ...), custom_call_target="tpu_custom_call" | custom-call | tf_op jit(solution)/shard_map/patch/pallas_call | solution.py:23
  19.7 0.1 collective-permute-start.4
  19.8 3.8 %collective-permute-start.5 = (f32[128,128]{1,0:T(8,128)S(1)}, f32[128,128]{1,0:T(8,128)S(1)}, u32[]{:S(2)}, u32[]{:S(2)}) collective-permute-start(f32[128,128]{1,0:T(8,128)S(1)} %get-tuple-element.53.here_ref), channel_id=1, source_target_pairs={{0,12},{4,0},{8,4},{12,8},{1,13},{5,1},{9,5},{13,9},{2,14},{6,2},{... | collective-permute-start | bytes 196616 | tf_op jit(solution)/shard_map/ppermute | solution.py:756
  23.6 0.8 %tables.1 = (bf16[8,256,768]{2,1,0:T(8,128)(2,1)S(1)}, f32[8,48,768]{2,1,0:T(8,128)S(1)}) custom-call(s32[8,768]{1,0:T(8,128)S(1)} %get-tuple-element.49.cell_ref, f32[8,768]{1,0:T(8,128)S(1)} %get-tuple-element.50.weight_ref), custom_call_target="tpu_custom_call" | custom-call | flops 2000000 | bytes 2000000 | tf_op jit(solution)/shard_map/tables/pallas_call | solution.py:23
  24.5 0.9 %output_ends.1 = f32[4,36,16,1,128]{4,3,2,1,0:T(1,128)} custom-call(f32[4,36,16,1,128]{4,3,2,1,0:T(1,128)} %get-tuple-element.43._, f32[1,320,128]{2,1,0:T(8,128)S(1)} %get-tuple-element.47.seam_ref, f32[4,2,40,128]{3,2,1,0:T(8,128)S(1)} %get-tuple-element.48.edge_ref), custom_call_target="tpu_custom_call", output_to_operand_aliasing={{}: (0, {})} | custom-call | flops 1000000 | bytes 1000000 | tf_op jit(solution)/shard_map/output_ends/pallas_call | solution.py:877
  25.4 0.6 %sense_here.1.partial_ref = f32[4,768]{1,0:T(4,128)S(1)} custom-call(bf16[8,256,768]{2,1,0:T(8,128)(2,1)S(1)} %get-tuple-element.51.hot_ref, f32[8,48,768]{2,1,0:T(8,128)S(1)} %get-tuple-element.52.share_ref, f32[128,128]{1,0:T(8,128)S(1)} %get-tuple-element.53.here_ref), custom_call_target="tpu_custom_call" | custom-call | flops 2000000 | bytes 2000000 | tf_op jit(solution)/shard_map/sense_here/pallas_call | solution.py:23
  26.0 0.0 collective-permute-done.4.before_ref
  26.0 0.0 collective-permute-done.5.after_ref
  26.0 1.6 %sense.1 = f32[4,768]{1,0:T(4,128)} custom-call(bf16[8,256,768]{2,1,0:T(8,128)(2,1)S(1)} %get-tuple-element.51.hot_ref, f32[8,48,768]{2,1,0:T(8,128)S(1)} %get-tuple-element.52.share_ref, f32[4,768]{1,0:T(4,128)S(1)} %sense_here.1.partial_ref, f32[128,128]{1,0:T(8,128)S(1)} %collective-permute-done.4.before_ref, f32[128,128]{1,0:T(8,128)S(1)} %collective-permute-done.5.after_ref), custom_call_target="tpu_custom_call" | custom-call | tf_op jit(solution)/shard_map/sense/pallas_call | solution.py:23
Async XLA Ops:
  3.2 10.9 %collective-permute-start.1 = (f32[184,128]{1,0:T(8,128)S(1)}, f32[184,128]{1,0:T(8,128)S(1)}, u32[]{:S(2)}, u32[]{:S(2)}) collective-permute-start(f32[184,128]{1,0:T(8,128)S(1)} %get-tuple-element.36), channel_id=1, source_target_pairs={{0,4},{4,8},{8,12},{12,0},{1,5},{5,9},{9,13},{13,1},{2,6},{6,10},{... | collective-permute-start | bytes 282632 | tf_op jit(solution)/shard_map/ppermute | solution.py:756
  6.3 7.7 %collective-permute-start.2 = (f32[148,128]{1,0:T(8,128)S(1)}, f32[148,128]{1,0:T(8,128)S(1)}, u32[]{:S(2)}, u32[]{:S(2)}) collective-permute-start(f32[148,128]{1,0:T(8,128)S(1)} %get-tuple-element.39), channel_id=1, source_target_pairs={{0,12},{4,0},{8,4},{12,8},{1,13},{5,1},{9,5},{13,9},{2,14},{6,2},{... | collective-permute-start | bytes 227336 | tf_op jit(solution)/shard_map/ppermute | solution.py:756
  8.4 4.0 %collective-permute-start = (f32[88,128]{1,0:T(8,128)S(1)}, f32[88,128]{1,0:T(8,128)S(1)}, u32[]{:S(2)}, u32[]{:S(2)}) collective-permute-start(f32[88,128]{1,0:T(8,128)S(1)} %get-tuple-element.28.own_ref), channel_id=1, source_target_pairs={{0,2},{2,0},{1,3},{3,1},{4,6},{6,4},{5,7},{7,5},{8,10},{10,8},{9,1... | collective-permute-start | bytes 135176 | tf_op jit(solution)/shard_map/ppermute | solution.py:756
  15.0 4.2 %collective-permute-start.3 = (f32[80,128]{1,0:T(8,128)S(1)}, f32[80,128]{1,0:T(8,128)S(1)}, u32[]{:S(2)}, u32[]{:S(2)}) collective-permute-start(f32[80,128]{1,0:T(8,128)S(1)} %get-tuple-element.45.refs_2_), channel_id=1, source_target_pairs={{0,2},{2,0},{1,3},{3,1},{4,6},{6,4},{5,7},{7,5},{8,10},{10,8},{9,1... | collective-permute-start | bytes 122888 | tf_op jit(solution)/shard_map/ppermute | solution.py:756
  19.7 6.3 %collective-permute-start.4 = (f32[128,128]{1,0:T(8,128)S(1)}, f32[128,128]{1,0:T(8,128)S(1)}, u32[]{:S(2)}, u32[]{:S(2)}) collective-permute-start(f32[128,128]{1,0:T(8,128)S(1)} %get-tuple-element.53.here_ref), channel_id=1, source_target_pairs={{0,4},{4,8},{8,12},{12,0},{1,5},{5,9},{9,13},{13,1},{2,6},{6,10},{... | collective-permute-start | bytes 196616 | tf_op jit(solution)/shard_map/ppermute | solution.py:756
  19.8 6.2 %collective-permute-start.5 = (f32[128,128]{1,0:T(8,128)S(1)}, f32[128,128]{1,0:T(8,128)S(1)}, u32[]{:S(2)}, u32[]{:S(2)}) collective-permute-start(f32[128,128]{1,0:T(8,128)S(1)} %get-tuple-element.53.here_ref), channel_id=1, source_target_pairs={{0,12},{4,0},{8,4},{12,8},{1,13},{5,1},{9,5},{13,9},{2,14},{6,2},{... | collective-permute-start | bytes 196616 | tf_op jit(solution)/shard_map/ppermute | solution.py:756

commit v5 on v4

--- a/solution.py
+++ b/solution.py
@@ -7,18 +7,18 @@
 from jax.experimental.pallas import tpu as pltpu
 from jax.sharding import PartitionSpec as P
 
+
 ADJ = 8
-NSTEP = 2
 F32 = jnp.float32
 BF16 = jnp.bfloat16
 VMEM_BYTES = 16 << 20
 RIM_TILES = 6
 
 
-def call(kernel, outs, args, scratch=(), far_in=False, far_out=(), name=None, cost=0):
+def call(kernel, outs, args, scratch=(), far_in=False, far_out=(), cost=0):
     near = pl.BlockSpec(memory_space=pltpu.VMEM)
     far = pl.BlockSpec(memory_space=pl.ANY)
-    outs = [out if isinstance(out[-1], int) else out for out in outs]
+    outs = [out for out in outs]
     shapes = [(out, F32) if isinstance(out[-1], int) else out for out in outs]
     return pl.pallas_call(
         kernel,
@@ -28,7 +28,6 @@
         scratch_shapes=list(scratch),
         compiler_params=pltpu.CompilerParams(vmem_limit_bytes=VMEM_BYTES),
         cost_estimate=pl.CostEstimate(flops=cost, bytes_accessed=cost, transcendentals=0) if cost else None,
-        name=name,
     )(*[pltpu.with_memory_space_constraint(arg, pltpu.HBM if far_in else pltpu.VMEM) for arg in args])
 
 
@@ -231,7 +230,7 @@
 
 
 def advance(dims, ids, lhs, x, at, rim):
-    lev, width_x, lanes = dims
+    lev, _, lanes = dims
     pad = round_up(lev, 8)
     own_cluster = at.cluster(x)
     rim_row = halo_of(rim.cluster, x)
@@ -330,7 +329,7 @@
 def inner_kernel(
     dims, per_device, rim_ref, c_ref, wx_ref, wy_ref, cluster_ref, strength_ref, lhs_ref, mixed_ref, ground_ref
 ):
-    lev, width_x, lanes = dims
+    lev, width_x, _ = dims
     pad = round_up(lev, 8)
     at = Columns(dims, c_ref, wx_ref, wy_ref, cluster_ref, strength_ref)
     base = RIM_TILES * pad
@@ -487,7 +486,7 @@
 
 
 def output_kernel(dims, per_device, *refs):
-    lev, width_x, lanes = dims
+    lev, width_x, _ = dims
     rim_ref, before_ref, inner_ref, ends_ref, far_ref, wx_ref, wy_ref, cluster_ref, strength_ref = refs[:9]
     out_ref, token_ref, edge_ref, field_ref, sem = refs[9:]
     token_ref[...] = jnp.zeros(token_ref.shape, F32)
@@ -554,7 +553,7 @@
                 share_ref[k, first : first + 16, lanes] = jnp.where(x == first, w, 0.0)
 
 
-def looked_up(dims, per_device, n_rim, blocks, hot_ref, share_ref, lanes):
+def looked_up(dims, per_device, blocks, hot_ref, share_ref, lanes):
     width_x = dims[1]
     rows = per_device * width_x
     surfaces = [split(jnp.concatenate(places, axis=1)) for _, places in blocks]
@@ -581,7 +580,7 @@
     rows = per_device * dims[1]
     blocks = [(0, [here_ref[k * rows : (k + 1) * rows, :] for k in range(n_rim)])]
     for lanes in wide_lanes(out_ref.shape[1]):
-        out_ref[:, lanes] = looked_up(dims, per_device, n_rim, blocks, hot_ref, share_ref, lanes)
+        out_ref[:, lanes] = looked_up(dims, per_device, blocks, hot_ref, share_ref, lanes)
 
 
 def sense_kernel(dims, per_device, n_rim, hot_ref, share_ref, partial_ref, before_ref, after_ref, out_ref, own_ref, sem):
@@ -591,7 +590,7 @@
         for step, ref in ((-1, before_ref), (1, after_ref))
     ]
     for lanes in wide_lanes(own_ref.shape[1]):
-        value = looked_up(dims, per_device, n_rim, blocks, hot_ref, share_ref, lanes)
+        value = looked_up(dims, per_device, blocks, hot_ref, share_ref, lanes)
         own_ref[:, lanes] = partial_ref[:, lanes] + value
     copy = pltpu.make_async_copy(own_ref, out_ref, sem)
     copy.start()
@@ -626,8 +625,7 @@
         return convect(lhs, fields, self.strength)
 
 
-def seam_transport(dims, rates, missing):
-    width_x = dims[1]
+def seam_transport(rates, missing):
     east, west, north, south = rates
     lane = lane_of((1, missing.shape[1]))
     place, slot = lane % 4, lane // 4
@@ -643,7 +641,7 @@
     return [jnp.int32(0), jnp.int32(1)]
 
 
-def patch_kernel(dims, subs, per_device, n_rim, *refs):
+def patch_kernel(dims, subs, per_device, *refs):
     lev, width_x, lanes = dims
     rim_ref, full_ref, own_ref, south_ref, north_ref, lhs_ref, _, whole_ref, seam_ref = refs
     pad = round_up(lev, 8)
@@ -721,7 +719,7 @@
         own_at = 0 if subs == 2 else 1
         own_lane = jnp.where(own_south > 0, lanes - 1, 0)
         for a, value in enumerate(missing):
-            change = seam_transport(dims, [rate[0:8] for rate in rates], value[0:8])[0:1]
+            change = seam_transport([rate[0:8] for rate in rates], value[0:8])[0:1]
             for x in (0, width_x - 1):
                 row = turn(change, -4 * x - 2)
                 for block, at_lane in ((own_at, own_lane), (far_at, lanes - 1 - own_lane)):
@@ -738,7 +736,7 @@
         columns = [edge_ref[a, 0], edge_ref[a, 1]]
         for k, own_south in enumerate(own_places(subs)):
             rates = [seam_ref[k, i * pad : (i + 1) * pad, :] for i in range(4)]
-            change = seam_transport(dims, rates, seam_ref[k, (4 + a) * pad : (5 + a) * pad, :])
+            change = seam_transport(rates, seam_ref[k, (4 + a) * pad : (5 + a) * pad, :])
             own = lane == jnp.where(own_south > 0, lanes - 1, 0)
             for i, x in enumerate((0, width_x - 1)):
                 columns[i] = columns[i] + jnp.where(own, turn(change, -4 * x - 2), 0.0)
@@ -806,7 +804,6 @@
         sources,
         scratch=(pltpu.SemaphoreType.DMA((len(sources),)),),
         far_in=True,
-        name="fetch",
     )
     air, wx, wy, innov, group, strength, _, cell, weight, lhs, own_rim = fetched
     south_rim, north_rim = across(own_rim)
@@ -814,7 +811,6 @@
         functools.partial(first_mix_kernel, dims),
         [(width_x, pad, width_y), (5 * lev + 4, width_y), (4 * lev + 4, width_y)],
         (air, innov, strength, lhs, wx, wy, group),
-        name="first_mix",
         cost=400000,
     )
     before = ring(to_east, "tiles", 1)
@@ -823,14 +819,12 @@
         functools.partial(rim_kernel, dims, subs),
         [(RIM_TILES * pad + 8, width_y)],
         (own_rim, south_rim, north_rim, lhs),
-        name="rim",
         cost=400000,
     )
     inner, ground = call(
         functools.partial(inner_kernel, dims, per_device),
         [(per_device, width_x - 2, pad, width_y), (per_device, width_x + 8, width_y)],
         (rim, first, wx, wy, group, strength, lhs),
-        name="inner",
         cost=4000000,
     )
     ends, far, surface, full = call(
@@ -847,7 +841,6 @@
             pltpu.VMEM((width_x + 8, width_y), F32),
             pltpu.VMEM((width_x * round_up(per_device + 1, 8), width_y), F32),
         ),
-        name="ends",
     )
     south_surface, north_surface = across(surface)
     field, token, edge = call(
@@ -859,17 +852,15 @@
             pltpu.SemaphoreType.DMA((per_device * width_x,)),
         ),
         far_out=(0,),
-        name="output",
         cost=4000000,
     )
     n_rim = min(subs, 3)
     rows = per_device * width_x
     seams = 1 if subs == 2 else 2
     whole, seam = call(
-        functools.partial(patch_kernel, dims, subs, per_device, n_rim),
+        functools.partial(patch_kernel, dims, subs, per_device),
         [(n_rim * rows, width_y), (seams, (4 + per_device) * pad, width_y)],
         (rim, full, surface, south_surface, north_surface, lhs, token),
-        name="patch",
     )
     surface_before = ring(whole, "tiles", 1)
     surface_after = ring(whole, "tiles", -1)
@@ -890,14 +881,12 @@
         functools.partial(tables_kernel, dims, tiles, subs, n_rim),
         [((slots, n_rim * width_y, elements), BF16), (slots, 3 * width_x, elements)],
         (cell, weight),
-        name="tables",
         cost=2000000,
     )
     (partial,) = call(
         functools.partial(sense_here_kernel, dims, per_device, n_rim),
         [(per_device, elements)],
         (hot, share, whole),
-        name="sense_here",
         cost=2000000,
     )
     (sensed,) = call(
@@ -906,7 +895,6 @@
         (hot, share, partial, surface_before, surface_after),
         scratch=(pltpu.VMEM((per_device, elements), F32), pltpu.SemaphoreType.DMA),
         far_out=(0,),
-        name="sense",
     )
     return (field.reshape(per_device, lev, width_x, width_y), sensed)
 

time: 27.9 us -> 27.9 us (level)
  no operation moved by 1% of the time
where the time goes in v5:
time: 27.9 us; the launch traced here: 27.7 us
  starting transfers between devices  12.4 us (44%)
  Pallas kernels  12.1 us (43%)
  waiting for transfers between devices  2.41 us (9%)
  between operations  0.74 us (3%)
    ppermute x6, starting transfers between devices, ring(): lax.ppermute(value, axis, [(i, (i + steps) % count) for i in range(count)])  12.4 us
    pallas_call x10, Pallas kernels, call(): pl.pallas_call(kernel, out_shape=[(jax.ShapeDtypeStruct if at in far_out...  11.2 us
    ppermute x6, waiting for transfers between devices, ring(): lax.ppermute(value, axis, [(i, (i + steps) % count) for i in range(count)])  2.41 us
    pallas_call x1, Pallas kernels, body(): pl.pallas_call(functools.partial(output_ends_kernel, dims, subs, per_devi...  0.94 us
  transfers between devices with their start and end apart: 6, of which 1 were waited for; matrix products, arithmetic and copies ran while one was open for 0% of the time, Pallas kernels for 23%

profile of v5, /device:TPU:0, one launch (start us, length us, event | category | flops | bytes accessed | tf_op | source)
XLA Modules:
  0.0 27.7 jit_solution(10904457491994962582)
XLA Ops:
  0.6 2.2 %shard_map.104 = (f32[640,128]{1,0:T(8,128)S(1)}, f32[640,128]{1,0:T(8,128)S(1)}, f32[640,128]{1,0:T(8,128)S(1)}, f32[16,128]{1,0:T(8,128)S(1)}, s32[16,128]{1,0...) custom-call(f32[576,128]{1,0:T(8,128)} %bitcast.7, ...), custom_call_target="tpu_custom_call" | custom-call | tf_op jit(solution)/shard_map/pallas_call | solution.py:23
  2.9 0.3 %shard_map.106 = (f32[16,40,128]{2,1,0:T(8,128)S(1)}, f32[184,128]{1,0:T(8,128)S(1)}, f32[148,128]{1,0:T(8,128)S(1)}) custom-call(f32[640,128]{1,0:T(8,128)S(1)} %get-tuple-element.30.refs_0_, f32[16,128]{1,0:T(8,128)S(1)} %get-tuple-element.31.refs_1_, f32[16,128]{1,0:T(8,128)S(1)} %get-tuple-element.32.refs_2_.strength_ref.refs_8_, ...), custom_call_target="tpu_custom_call" | custom-call | flops 400000 | bytes 400000 | tf_op jit(solution)/shard_map/pallas_call | solution.py:23
  3.2 3.1 %collective-permute-start.1 = (f32[184,128]{1,0:T(8,128)S(1)}, f32[184,128]{1,0:T(8,128)S(1)}, u32[]{:S(2)}, u32[]{:S(2)}) collective-permute-start(f32[184,128]{1,0:T(8,128)S(1)} %get-tuple-element.36), channel_id=1, source_target_pairs={{0,4},{4,8},{8,12},{12,0},{1,5},{5,9},{9,13},{13,1},{2,6},{6,10},{... | collective-permute-start | bytes 282632 | tf_op jit(solution)/shard_map/ppermute | solution.py:754
  6.3 2.1 %collective-permute-start.2 = (f32[148,128]{1,0:T(8,128)S(1)}, f32[148,128]{1,0:T(8,128)S(1)}, u32[]{:S(2)}, u32[]{:S(2)}) collective-permute-start(f32[148,128]{1,0:T(8,128)S(1)} %get-tuple-element.39), channel_id=1, source_target_pairs={{0,12},{4,0},{8,4},{12,8},{1,13},{5,1},{9,5},{13,9},{2,14},{6,2},{... | collective-permute-start | bytes 227336 | tf_op jit(solution)/shard_map/ppermute | solution.py:754
  8.4 1.6 %collective-permute-start = (f32[88,128]{1,0:T(8,128)S(1)}, f32[88,128]{1,0:T(8,128)S(1)}, u32[]{:S(2)}, u32[]{:S(2)}) collective-permute-start(f32[88,128]{1,0:T(8,128)S(1)} %get-tuple-element.28.own_ref), channel_id=1, source_target_pairs={{0,2},{2,0},{1,3},{3,1},{4,6},{6,4},{5,7},{7,5},{8,10},{10,8},{9,1... | collective-permute-start | bytes 135176 | tf_op jit(solution)/shard_map/ppermute | solution.py:754
  10.0 2.4 %collective-permute-done.south_ref.north_ref = f32[88,128]{1,0:T(8,128)S(1)} collective-permute-done((f32[88,128]{1,0:T(8,128)S(1)}, f32[88,128]{1,0:T(8,128)S(1)}, u32[]{:S(2)}, u32[]{:S(2)}) %collective-permute-start) | collective-permute-done | bytes 45088 | tf_op jit(solution)/shard_map/ppermute | solution.py:754
  12.4 0.1 shard_map.105.rim_ref.refs_0_
  12.5 1.4 %shard_map.107 = (f32[4,14,40,128]{3,2,1,0:T(8,128)S(1)}, f32[4,24,128]{2,1,0:T(8,128)S(1)}) custom-call(f32[248,128]{1,0:T(8,128)S(1)} %shard_map.105.rim_ref.refs_0_, f32[16,40,128]{2,1,0:T(8,128)S(1)} %get-tuple-element.37.c_ref.refs_4_, f32[640,128]{1,0:T(8,128)S(1)} %get-tuple-element.33.refs_4_.wx_ref.refs_5_, ...), custom_call_target="tpu_custom_call" | custom-call | flops 4000000 | bytes 4000000 | tf_op jit(solution)/shard_map/pallas_call | solution.py:23
  14.0 0.0 collective-permute-done.2.refs_2_
  14.0 0.0 collective-permute-done.1.refs_1_
  14.0 1.0 %shard_map.108 = (f32[4,4,40,128]{3,2,1,0:T(8,128)S(1)}, f32[2,48,128]{2,1,0:T(8,128)S(1)}, f32[80,128]{1,0:T(8,128)S(1)}, f32[128,128]{1,0:T(8,128)S(1)}) custom-call(f32[248,128]{1,0:T(8,128)S(1)} %shard_map.105.rim_ref.refs_0_, f32[184,128]{1,0:T(8,128)S(1)} %collective-permute-done.1.refs_1_, f32[148,128]{1,0:T(8,128)S(1)} %collective-permute-done.2.refs_2_, ...), custom_call_target="tpu_custom_call" | custom-call | tf_op jit(solution)/shard_map/pallas_call | solution.py:23
  15.0 1.7 %collective-permute-start.3 = (f32[80,128]{1,0:T(8,128)S(1)}, f32[80,128]{1,0:T(8,128)S(1)}, u32[]{:S(2)}, u32[]{:S(2)}) collective-permute-start(f32[80,128]{1,0:T(8,128)S(1)} %get-tuple-element.45.refs_2_), channel_id=1, source_target_pairs={{0,2},{2,0},{1,3},{3,1},{4,6},{6,4},{5,7},{7,5},{8,10},{10,8},{9,1... | collective-permute-start | bytes 122888 | tf_op jit(solution)/shard_map/ppermute | solution.py:754
  16.7 2.4 %shard_map.109 = (f32[4,36,16,1,128]{4,3,2,1,0:T(1,128)}, f32[8,128]{1,0:T(8,128)S(1)}, f32[4,2,40,128]{3,2,1,0:T(8,128)S(1)}) custom-call(f32[248,128]{1,0:T(8,128)S(1)} %shard_map.105.rim_ref.refs_0_, f32[184,128]{1,0:T(8,128)S(1)} %collective-permute-done.1.refs_1_, f32[4,14,40,128]{3,2,1,0:T(8,128)S(1)} %get-tuple-element.38.refs_2_, ...), custom_call_target="tpu_custom_call" | custom-call | flops 4000000 | bytes 4000000 | tf_op jit(solution)/shard_map/pallas_call | solution.py:23
  19.2 0.0 collective-permute-done.3.refs_3_.refs_4_
  19.2 0.6 %shard_map.110 = (f32[128,128]{1,0:T(8,128)S(1)}, f32[1,320,128]{2,1,0:T(8,128)S(1)}) custom-call(f32[248,128]{1,0:T(8,128)S(1)} %shard_map.105.rim_ref.refs_0_, f32[128,128]{1,0:T(8,128)S(1)} %get-tuple-element.44.refs_1_, f32[80,128]{1,0:T(8,128)S(1)} %get-tuple-element.45.refs_2_, f32[80,128]{1,0:T(8,128)S(1)} %collective-permute-done.3.refs_3_.refs_4_, ...), custom_call_target="tpu_custom_call" | custom-call | tf_op jit(solution)/shard_map/pallas_call | solution.py:23
  19.7 0.1 collective-permute-start.4
  19.8 3.8 %collective-permute-start.5 = (f32[128,128]{1,0:T(8,128)S(1)}, f32[128,128]{1,0:T(8,128)S(1)}, u32[]{:S(2)}, u32[]{:S(2)}) collective-permute-start(f32[128,128]{1,0:T(8,128)S(1)} %get-tuple-element.53.here_ref), channel_id=1, source_target_pairs={{0,12},{4,0},{8,4},{12,8},{1,13},{5,1},{9,5},{13,9},{2,14},{6,2},{... | collective-permute-start | bytes 196616 | tf_op jit(solution)/shard_map/ppermute | solution.py:754
  23.6 0.8 %shard_map.111 = (bf16[8,256,768]{2,1,0:T(8,128)(2,1)S(1)}, f32[8,48,768]{2,1,0:T(8,128)S(1)}) custom-call(s32[8,768]{1,0:T(8,128)S(1)} %get-tuple-element.49.cell_ref, f32[8,768]{1,0:T(8,128)S(1)} %get-tuple-element.50.weight_ref), custom_call_target="tpu_custom_call" | custom-call | flops 2000000 | bytes 2000000 | tf_op jit(solution)/shard_map/pallas_call | solution.py:23
  24.5 0.9 %output_ends.1 = f32[4,36,16,1,128]{4,3,2,1,0:T(1,128)} custom-call(f32[4,36,16,1,128]{4,3,2,1,0:T(1,128)} %get-tuple-element.43._, f32[1,320,128]{2,1,0:T(8,128)S(1)} %get-tuple-element.47.seam_ref, f32[4,2,40,128]{3,2,1,0:T(8,128)S(1)} %get-tuple-element.48.edge_ref), custom_call_target="tpu_custom_call", output_to_operand_aliasing={{}: (0, {})} | custom-call | flops 1000000 | bytes 1000000 | tf_op jit(solution)/shard_map/output_ends/pallas_call | solution.py:868
  25.4 0.6 %shard_map.112.partial_ref = f32[4,768]{1,0:T(4,128)S(1)} custom-call(bf16[8,256,768]{2,1,0:T(8,128)(2,1)S(1)} %get-tuple-element.51.hot_ref, f32[8,48,768]{2,1,0:T(8,128)S(1)} %get-tuple-element.52.share_ref, f32[128,128]{1,0:T(8,128)S(1)} %get-tuple-element.53.here_ref), custom_call_target="tpu_custom_call" | custom-call | flops 2000000 | bytes 2000000 | tf_op jit(solution)/shard_map/pallas_call | solution.py:23
  26.0 0.0 collective-permute-done.4.before_ref
  26.0 0.0 collective-permute-done.5.after_ref
  26.0 1.6 %shard_map.113 = f32[4,768]{1,0:T(4,128)} custom-call(bf16[8,256,768]{2,1,0:T(8,128)(2,1)S(1)} %get-tuple-element.51.hot_ref, f32[8,48,768]{2,1,0:T(8,128)S(1)} %get-tuple-element.52.share_ref, f32[4,768]{1,0:T(4,128)S(1)} %shard_map.112.partial_ref, f32[128,128]{1,0:T(8,128)S(1)} %collective-permute-done.4.before_ref, ...), custom_call_target="tpu_custom_call" | custom-call | tf_op jit(solution)/shard_map/pallas_call | solution.py:23
Async XLA Ops:
  3.2 10.9 %collective-permute-start.1 = (f32[184,128]{1,0:T(8,128)S(1)}, f32[184,128]{1,0:T(8,128)S(1)}, u32[]{:S(2)}, u32[]{:S(2)}) collective-permute-start(f32[184,128]{1,0:T(8,128)S(1)} %get-tuple-element.36), channel_id=1, source_target_pairs={{0,4},{4,8},{8,12},{12,0},{1,5},{5,9},{9,13},{13,1},{2,6},{6,10},{... | collective-permute-start | bytes 282632 | tf_op jit(solution)/shard_map/ppermute | solution.py:754
  6.3 7.7 %collective-permute-start.2 = (f32[148,128]{1,0:T(8,128)S(1)}, f32[148,128]{1,0:T(8,128)S(1)}, u32[]{:S(2)}, u32[]{:S(2)}) collective-permute-start(f32[148,128]{1,0:T(8,128)S(1)} %get-tuple-element.39), channel_id=1, source_target_pairs={{0,12},{4,0},{8,4},{12,8},{1,13},{5,1},{9,5},{13,9},{2,14},{6,2},{... | collective-permute-start | bytes 227336 | tf_op jit(solution)/shard_map/ppermute | solution.py:754
  8.4 4.0 %collective-permute-start = (f32[88,128]{1,0:T(8,128)S(1)}, f32[88,128]{1,0:T(8,128)S(1)}, u32[]{:S(2)}, u32[]{:S(2)}) collective-permute-start(f32[88,128]{1,0:T(8,128)S(1)} %get-tuple-element.28.own_ref), channel_id=1, source_target_pairs={{0,2},{2,0},{1,3},{3,1},{4,6},{6,4},{5,7},{7,5},{8,10},{10,8},{9,1... | collective-permute-start | bytes 135176 | tf_op jit(solution)/shard_map/ppermute | solution.py:754
  15.0 4.2 %collective-permute-start.3 = (f32[80,128]{1,0:T(8,128)S(1)}, f32[80,128]{1,0:T(8,128)S(1)}, u32[]{:S(2)}, u32[]{:S(2)}) collective-permute-start(f32[80,128]{1,0:T(8,128)S(1)} %get-tuple-element.45.refs_2_), channel_id=1, source_target_pairs={{0,2},{2,0},{1,3},{3,1},{4,6},{6,4},{5,7},{7,5},{8,10},{10,8},{9,1... | collective-permute-start | bytes 122888 | tf_op jit(solution)/shard_map/ppermute | solution.py:754
  19.7 6.3 %collective-permute-start.4 = (f32[128,128]{1,0:T(8,128)S(1)}, f32[128,128]{1,0:T(8,128)S(1)}, u32[]{:S(2)}, u32[]{:S(2)}) collective-permute-start(f32[128,128]{1,0:T(8,128)S(1)} %get-tuple-element.53.here_ref), channel_id=1, source_target_pairs={{0,4},{4,8},{8,12},{12,0},{1,5},{5,9},{9,13},{13,1},{2,6},{6,10},{... | collective-permute-start | bytes 196616 | tf_op jit(solution)/shard_map/ppermute | solution.py:754
  19.8 6.2 %collective-permute-start.5 = (f32[128,128]{1,0:T(8,128)S(1)}, f32[128,128]{1,0:T(8,128)S(1)}, u32[]{:S(2)}, u32[]{:S(2)}) collective-permute-start(f32[128,128]{1,0:T(8,128)S(1)} %get-tuple-element.53.here_ref), channel_id=1, source_target_pairs={{0,12},{4,0},{8,4},{12,8},{1,13},{5,1},{9,5},{13,9},{2,14},{6,2},{... | collective-permute-start | bytes 196616 | tf_op jit(solution)/shard_map/ppermute | solution.py:754

commit v6 on v5

--- a/solution.py
+++ b/solution.py
@@ -120,15 +120,22 @@
         copy.wait()
 
 
-def first_mix_kernel(dims, *refs):
+def first_columns(dims, kernel_ref, innov_ref, strength_ref, lhs, x):
     lev, width_x, lanes = dims
-    kernel_ref, innov_ref, strength_ref, lhs_ref, wx_ref, wy_ref, cluster_ref, out_ref, east_ref, west_ref = refs
+    pad = round_up(lev, 8)
+    tiles = [kernel_ref[pl.ds(at, pad, stride=width_x), :] * innov_ref[at : at + 1, :] for at in (x, x + 1)]
+    mixed = mix(lhs, jnp.concatenate(tiles, axis=1))
+    parts = [mixed[:, k * lanes : (k + 1) * lanes] for k in (0, 1)]
+    return [t + strength_ref[x + k : x + k + 1, :] * (p - t) for k, (t, p) in enumerate(zip(tiles, parts))]
+
+
+def first_ends_kernel(dims, *refs):
+    lev, width_x, lanes = dims
+    kernel_ref, innov_ref, strength_ref, lhs_ref, wx_ref, wy_ref, cluster_ref, east_ref, west_ref = refs
     pad = round_up(lev, 8)
     lhs = lhs_ref[...]
     last = width_x - 1
     cluster = cluster_ref[...].astype(F32)
-    held = {}
-    order = [0, width_x - 2] + list(range(2, width_x - 2, 2))
 
     def column(ref, x):
         return ref[pl.ds(x, pad, stride=width_x), :]
@@ -143,17 +150,22 @@
         ref[base + 2 : base + 3, :] = strength_ref[near : near + 1, :]
         ref[base + 3 : base + 4, :] = jnp.zeros((1, lanes), F32)
 
-    for x in order:
-        tiles = [column(kernel_ref, at) * innov_ref[at : at + 1, :] for at in (x, x + 1)]
-        mixed = mix(lhs, jnp.concatenate(tiles, axis=1))
-        for k, tile in enumerate(tiles):
-            part = mixed[:, k * lanes : (k + 1) * lanes]
-            held[x + k] = tile + strength_ref[x + k : x + k + 1, :] * (part - tile)
-            out_ref[x + k, :, :] = held[x + k]
-        if x == width_x - 2:
-            ends = (held[last], held[last - 1], column(wx_ref, last), column(wy_ref, last), column(wx_ref, last - 1))
-            put(east_ref, ends, last, last - 1)
-            put(west_ref, (held[0], held[1], column(wx_ref, 0), column(wy_ref, 0)), 0, 1)
+    inside, outer = first_columns(dims, kernel_ref, innov_ref, strength_ref, lhs, last - 1)
+    put(
+        east_ref,
+        (outer, inside, column(wx_ref, last), column(wy_ref, last), column(wx_ref, last - 1)),
+        last,
+        last - 1,
+    )
+    outer, inside = first_columns(dims, kernel_ref, innov_ref, strength_ref, lhs, 0)
+    put(west_ref, (outer, inside, column(wx_ref, 0), column(wy_ref, 0)), 0, 1)
+
+
+def first_mix_kernel(dims, kernel_ref, innov_ref, strength_ref, lhs_ref, out_ref):
+    lhs = lhs_ref[...]
+    for x in range(0, dims[1], 2):
+        for k, value in enumerate(first_columns(dims, kernel_ref, innov_ref, strength_ref, lhs, x)):
+            out_ref[x + k, :, :] = value
 
 
 def rim_kernel(dims, subs, own_ref, south_ref, north_ref, lhs_ref, rim_ref):
@@ -576,22 +588,18 @@
     return [slice(g, g + wide) for g in range(0, elements, wide)]
 
 
-def sense_here_kernel(dims, per_device, n_rim, hot_ref, share_ref, here_ref, out_ref):
+def sense_part_kernel(dims, per_device, n_rim, step, hot_ref, share_ref, block_ref, *refs):
+    *found, out_ref = refs
     rows = per_device * dims[1]
-    blocks = [(0, [here_ref[k * rows : (k + 1) * rows, :] for k in range(n_rim)])]
+    blocks = [(step, [block_ref[k * rows : (k + 1) * rows, :] for k in range(n_rim)])]
     for lanes in wide_lanes(out_ref.shape[1]):
-        out_ref[:, lanes] = looked_up(dims, per_device, blocks, hot_ref, share_ref, lanes)
-
-
-def sense_kernel(dims, per_device, n_rim, hot_ref, share_ref, partial_ref, before_ref, after_ref, out_ref, own_ref, sem):
-    rows = per_device * dims[1]
-    blocks = [
-        (step, [ref[k * rows : (k + 1) * rows, :] for k in range(n_rim)])
-        for step, ref in ((-1, before_ref), (1, after_ref))
-    ]
-    for lanes in wide_lanes(own_ref.shape[1]):
         value = looked_up(dims, per_device, blocks, hot_ref, share_ref, lanes)
-        own_ref[:, lanes] = partial_ref[:, lanes] + value
+        out_ref[:, lanes] = total([ref[:, lanes] for ref in found] + [value])
+
+
+def sense_last_kernel(*refs):
+    *inputs, out_ref, own_ref, sem = refs
+    sense_part_kernel(*inputs, own_ref)
     copy = pltpu.make_async_copy(own_ref, out_ref, sem)
     copy.start()
     copy.wait()
@@ -807,14 +815,16 @@
     )
     air, wx, wy, innov, group, strength, _, cell, weight, lhs, own_rim = fetched
     south_rim, north_rim = across(own_rim)
-    first, to_east, to_west = call(
-        functools.partial(first_mix_kernel, dims),
-        [(width_x, pad, width_y), (5 * lev + 4, width_y), (4 * lev + 4, width_y)],
+    to_east, to_west = call(
+        functools.partial(first_ends_kernel, dims),
+        [(5 * lev + 4, width_y), (4 * lev + 4, width_y)],
         (air, innov, strength, lhs, wx, wy, group),
-        cost=400000,
     )
     before = ring(to_east, "tiles", 1)
     after = ring(to_west, "tiles", -1)
+    (first,) = call(
+        functools.partial(first_mix_kernel, dims), [(width_x, pad, width_y)], (air, innov, strength, lhs), cost=400000
+    )
     (rim,) = call(
         functools.partial(rim_kernel, dims, subs),
         [(RIM_TILES * pad + 8, width_y)],
@@ -862,6 +872,10 @@
         [(n_rim * rows, width_y), (seams, (4 + per_device) * pad, width_y)],
         (rim, full, surface, south_surface, north_surface, lhs, token),
     )
+    if subs > 2:
+        own = whole[rows : 2 * rows]
+        south_surface, north_surface = across(own)
+        whole = jnp.concatenate([south_surface, own, north_surface], axis=0)
     surface_before = ring(whole, "tiles", 1)
     surface_after = ring(whole, "tiles", -1)
     near, hbm = pl.BlockSpec(memory_space=pltpu.VMEM), pl.BlockSpec(memory_space=pl.ANY)
@@ -883,16 +897,14 @@
         (cell, weight),
         cost=2000000,
     )
-    (partial,) = call(
-        functools.partial(sense_here_kernel, dims, per_device, n_rim),
-        [(per_device, elements)],
-        (hot, share, whole),
-        cost=2000000,
-    )
+    part = functools.partial(sense_part_kernel, dims, per_device, n_rim)
+    found = [(per_device, elements)]
+    (sensed,) = call(functools.partial(part, 0), found, (hot, share, whole), cost=2000000)
+    (sensed,) = call(functools.partial(part, 1), found, (hot, share, surface_after, sensed), cost=2000000)
     (sensed,) = call(
-        functools.partial(sense_kernel, dims, per_device, n_rim),
-        [(per_device, elements)],
-        (hot, share, partial, surface_before, surface_after),
+        functools.partial(sense_last_kernel, dims, per_device, n_rim, -1),
+        found,
+        (hot, share, surface_before, sensed),
         scratch=(pltpu.VMEM((per_device, elements), F32), pltpu.SemaphoreType.DMA),
         far_out=(0,),
     )

time: 27.9 us -> 29 us (1.039)
  waiting for transfers between devices: 2.41 us -> 5.02 us
  starting transfers between devices: 12.4 us -> 10.6 us
  Pallas kernels: 12.1 us -> 12.4 us
    ppermute x6, waiting for transfers between devices: 2.41 us -> 5.02 us  [ring(): lax.ppermute(value, axis, [(i, (i + steps) % count) for i in range(count)])]
    ppermute x6, starting transfers between devices: 12.4 us -> 10.6 us  [ring(): lax.ppermute(value, axis, [(i, (i + steps) % count) for i in range(count)])]
    pallas_call x10 -> x12, Pallas kernels: 11.2 us -> 11.5 us  [call(): pl.pallas_call(kernel, out_shape=[(jax.ShapeDtypeStruct if at in far_out...]
  transfers between devices with their start and end apart: 6 -> 6, of which waited for: 1 -> 2; matrix products, arithmetic and copies ran while one was open for 0% -> 0% of each run, Pallas kernels for 23% -> 25%
where the time goes in v6:
time: 29 us; the launch traced here: 28.8 us
  Pallas kernels  12.4 us (43%)
  starting transfers between devices  10.6 us (37%)
  waiting for transfers between devices  5.02 us (17%)
  between operations  0.73 us (3%)
    pallas_call x12, Pallas kernels, call(): pl.pallas_call(kernel, out_shape=[(jax.ShapeDtypeStruct if at in far_out...  11.5 us
    ppermute x6, starting transfers between devices, ring(): lax.ppermute(value, axis, [(i, (i + steps) % count) for i in range(count)])  10.6 us
    ppermute x6, waiting for transfers between devices, ring(): lax.ppermute(value, axis, [(i, (i + steps) % count) for i in range(count)])  5.02 us
    pallas_call x1, Pallas kernels, body(): pl.pallas_call(functools.partial(output_ends_kernel, dims, subs, per_devi...  0.94 us
  transfers between devices with their start and end apart: 6, of which 2 were waited for; matrix products, arithmetic and copies ran while one was open for 0% of the time, Pallas kernels for 25%

profile of v6, /device:TPU:0, one launch (start us, length us, event | category | flops | bytes accessed | tf_op | source)
XLA Modules:
  0.0 28.8 jit_solution(3933832373466225916)
XLA Ops:
  0.6 2.2 %shard_map.104 = (f32[640,128]{1,0:T(8,128)S(1)}, f32[640,128]{1,0:T(8,128)S(1)}, f32[640,128]{1,0:T(8,128)S(1)}, f32[16,128]{1,0:T(8,128)S(1)}, s32[16,128]{1,0...) custom-call(f32[576,128]{1,0:T(8,128)} %bitcast.7, ...), custom_call_target="tpu_custom_call" | custom-call | tf_op jit(solution)/shard_map/pallas_call | solution.py:23
  2.9 0.2 shard_map.106
  3.0 3.1 %collective-permute-start.1 = (f32[184,128]{1,0:T(8,128)S(1)}, f32[184,128]{1,0:T(8,128)S(1)}, u32[]{:S(2)}, u32[]{:S(2)}) collective-permute-start(f32[184,128]{1,0:T(8,128)S(1)} %get-tuple-element.35), channel_id=1, source_target_pairs={{0,4},{4,8},{8,12},{12,0},{1,5},{5,9},{9,13},{13,1},{2,6},{6,10},{... | collective-permute-start | bytes 282632 | tf_op jit(solution)/shard_map/ppermute | solution.py:762
  6.1 2.1 %collective-permute-start.2 = (f32[148,128]{1,0:T(8,128)S(1)}, f32[148,128]{1,0:T(8,128)S(1)}, u32[]{:S(2)}, u32[]{:S(2)}) collective-permute-start(f32[148,128]{1,0:T(8,128)S(1)} %get-tuple-element.37), channel_id=1, source_target_pairs={{0,12},{4,0},{8,4},{12,8},{1,13},{5,1},{9,5},{13,9},{2,14},{6,2},{... | collective-permute-start | bytes 227336 | tf_op jit(solution)/shard_map/ppermute | solution.py:762
  8.2 1.6 %collective-permute-start = (f32[88,128]{1,0:T(8,128)S(1)}, f32[88,128]{1,0:T(8,128)S(1)}, u32[]{:S(2)}, u32[]{:S(2)}) collective-permute-start(f32[88,128]{1,0:T(8,128)S(1)} %get-tuple-element.27.own_ref), channel_id=1, source_target_pairs={{0,2},{2,0},{1,3},{3,1},{4,6},{6,4},{5,7},{7,5},{8,10},{10,8},{9,1... | collective-permute-start | bytes 135176 | tf_op jit(solution)/shard_map/ppermute | solution.py:762
  9.9 0.3 shard_map.107.c_ref.refs_4_
  10.2 2.1 %collective-permute-done.south_ref.north_ref = f32[88,128]{1,0:T(8,128)S(1)} collective-permute-done((f32[88,128]{1,0:T(8,128)S(1)}, f32[88,128]{1,0:T(8,128)S(1)}, u32[]{:S(2)}, u32[]{:S(2)}) %collective-permute-start) | collective-permute-done | bytes 45088 | tf_op jit(solution)/shard_map/ppermute | solution.py:762
  12.3 0.1 shard_map.105.rim_ref.refs_0_
  12.4 1.4 %shard_map.108 = (f32[4,14,40,128]{3,2,1,0:T(8,128)S(1)}, f32[4,24,128]{2,1,0:T(8,128)S(1)}) custom-call(f32[248,128]{1,0:T(8,128)S(1)} %shard_map.105.rim_ref.refs_0_, f32[16,40,128]{2,1,0:T(8,128)S(1)} %shard_map.107.c_ref.refs_4_, f32[640,128]{1,0:T(8,128)S(1)} %get-tuple-element.32.refs_4_.wx_ref.refs_5_, ...), custom_call_target="tpu_custom_call" | custom-call | flops 4000000 | bytes 4000000 | tf_op jit(solution)/shard_map/pallas_call | solution.py:23
  13.9 0.0 collective-permute-done.2.refs_2_
  13.9 0.0 collective-permute-done.1.refs_1_
  13.9 1.0 %shard_map.109 = (f32[4,4,40,128]{3,2,1,0:T(8,128)S(1)}, f32[2,48,128]{2,1,0:T(8,128)S(1)}, f32[80,128]{1,0:T(8,128)S(1)}, f32[128,128]{1,0:T(8,128)S(1)}) custom-call(f32[248,128]{1,0:T(8,128)S(1)} %shard_map.105.rim_ref.refs_0_, f32[184,128]{1,0:T(8,128)S(1)} %collective-permute-done.1.refs_1_, f32[148,128]{1,0:T(8,128)S(1)} %collective-permute-done.2.refs_2_, ...), custom_call_target="tpu_custom_call" | custom-call | tf_op jit(solution)/shard_map/pallas_call | solution.py:23
  14.9 1.7 %collective-permute-start.3 = (f32[80,128]{1,0:T(8,128)S(1)}, f32[80,128]{1,0:T(8,128)S(1)}, u32[]{:S(2)}, u32[]{:S(2)}) collective-permute-start(f32[80,128]{1,0:T(8,128)S(1)} %get-tuple-element.43.refs_2_), channel_id=1, source_target_pairs={{0,2},{2,0},{1,3},{3,1},{4,6},{6,4},{5,7},{7,5},{8,10},{10,8},{9,1... | collective-permute-start | bytes 122888 | tf_op jit(solution)/shard_map/ppermute | solution.py:762
  16.6 2.4 %shard_map.110 = (f32[4,36,16,1,128]{4,3,2,1,0:T(1,128)}, f32[8,128]{1,0:T(8,128)S(1)}, f32[4,2,40,128]{3,2,1,0:T(8,128)S(1)}) custom-call(f32[248,128]{1,0:T(8,128)S(1)} %shard_map.105.rim_ref.refs_0_, f32[184,128]{1,0:T(8,128)S(1)} %collective-permute-done.1.refs_1_, f32[4,14,40,128]{3,2,1,0:T(8,128)S(1)} %get-tuple-element.36.refs_2_, ...), custom_call_target="tpu_custom_call" | custom-call | flops 4000000 | bytes 4000000 | tf_op jit(solution)/shard_map/pallas_call | solution.py:23
  19.1 0.0 collective-permute-done.3.refs_3_.refs_4_
  19.1 0.6 %shard_map.111 = (f32[128,128]{1,0:T(8,128)S(1)}, f32[1,320,128]{2,1,0:T(8,128)S(1)}) custom-call(f32[248,128]{1,0:T(8,128)S(1)} %shard_map.105.rim_ref.refs_0_, f32[128,128]{1,0:T(8,128)S(1)} %get-tuple-element.42.refs_1_, f32[80,128]{1,0:T(8,128)S(1)} %get-tuple-element.43.refs_2_, f32[80,128]{1,0:T(8,128)S(1)} %collective-permute-done.3.refs_3_.refs_4_, ...), custom_call_target="tpu_custom_call" | custom-call | tf_op jit(solution)/shard_map/pallas_call | solution.py:23
  19.6 1.9 %collective-permute-start.5 = (f32[128,128]{1,0:T(8,128)S(1)}, f32[128,128]{1,0:T(8,128)S(1)}, u32[]{:S(2)}, u32[]{:S(2)}) collective-permute-start(f32[128,128]{1,0:T(8,128)S(1)} %get-tuple-element.51.block_ref), channel_id=1, source_target_pairs={{0,12},{4,0},{8,4},{12,8},{1,13},{5,1},{9,5},{13,9},{2,14},{6,2},{... | collective-permute-start | bytes 196616 | tf_op jit(solution)/shard_map/ppermute | solution.py:762
  21.5 0.2 collective-permute-start.4
  21.7 0.8 %shard_map.112 = (bf16[8,256,768]{2,1,0:T(8,128)(2,1)S(1)}, f32[8,48,768]{2,1,0:T(8,128)S(1)}) custom-call(s32[8,768]{1,0:T(8,128)S(1)} %get-tuple-element.47.cell_ref, f32[8,768]{1,0:T(8,128)S(1)} %get-tuple-element.48.weight_ref), custom_call_target="tpu_custom_call" | custom-call | flops 2000000 | bytes 2000000 | tf_op jit(solution)/shard_map/pallas_call | solution.py:23
  22.6 0.9 %output_ends.1 = f32[4,36,16,1,128]{4,3,2,1,0:T(1,128)} custom-call(f32[4,36,16,1,128]{4,3,2,1,0:T(1,128)} %get-tuple-element.41._, f32[1,320,128]{2,1,0:T(8,128)S(1)} %get-tuple-element.45.seam_ref, f32[4,2,40,128]{3,2,1,0:T(8,128)S(1)} %get-tuple-element.46.edge_ref), custom_call_target="tpu_custom_call", output_to_operand_aliasing={{}: (0, {})} | custom-call | flops 1000000 | bytes 1000000 | tf_op jit(solution)/shard_map/output_ends/pallas_call | solution.py:882
  23.5 0.6 %shard_map.113.refs_0_ = f32[4,768]{1,0:T(4,128)S(1)} custom-call(bf16[8,256,768]{2,1,0:T(8,128)(2,1)S(1)} %get-tuple-element.49.hot_ref.refs_0_, f32[8,48,768]{2,1,0:T(8,128)S(1)} %get-tuple-element.50.share_ref.refs_1_, f32[128,128]{1,0:T(8,128)S(1)} %get-tuple-element.51.block_ref), custom_call_target="tpu_custom_call" | custom-call | flops 2000000 | bytes 2000000 | tf_op jit(solution)/shard_map/pallas_call | solution.py:23
  24.1 0.0 collective-permute-done.5.block_ref
  24.1 0.6 %shard_map.114.refs_3_ = f32[4,768]{1,0:T(4,128)S(1)} custom-call(bf16[8,256,768]{2,1,0:T(8,128)(2,1)S(1)} %get-tuple-element.49.hot_ref.refs_0_, f32[8,48,768]{2,1,0:T(8,128)S(1)} %get-tuple-element.50.share_ref.refs_1_, f32[128,128]{1,0:T(8,128)S(1)} %collective-permute-done.5.block_ref, f32[4,768]{1,0:T(4,128)S(1)} %shard_map.113.refs_0_), custom_call_target="tpu_custom_call" | custom-call | flops 2000000 | bytes 2000000 | tf_op jit(solution)/shard_map/pallas_call | solution.py:23
  24.8 2.8 %collective-permute-done.4.refs_2_ = f32[128,128]{1,0:T(8,128)S(1)} collective-permute-done((f32[128,128]{1,0:T(8,128)S(1)}, f32[128,128]{1,0:T(8,128)S(1)}, u32[]{:S(2)}, u32[]{:S(2)}) %collective-permute-start.4) | collective-permute-done | bytes 65568 | tf_op jit(solution)/shard_map/ppermute | solution.py:762
  27.6 1.2 %shard_map.115 = f32[4,768]{1,0:T(4,128)} custom-call(bf16[8,256,768]{2,1,0:T(8,128)(2,1)S(1)} %get-tuple-element.49.hot_ref.refs_0_, f32[8,48,768]{2,1,0:T(8,128)S(1)} %get-tuple-element.50.share_ref.refs_1_, f32[128,128]{1,0:T(8,128)S(1)} %collective-permute-done.4.refs_2_, f32[4,768]{1,0:T(4,128)S(1)} %shard_map.114.refs_3_), custom_call_target="tpu_custom_call" | custom-call | tf_op jit(solution)/shard_map/pallas_call | solution.py:23
Async XLA Ops:
  3.0 10.9 %collective-permute-start.1 = (f32[184,128]{1,0:T(8,128)S(1)}, f32[184,128]{1,0:T(8,128)S(1)}, u32[]{:S(2)}, u32[]{:S(2)}) collective-permute-start(f32[184,128]{1,0:T(8,128)S(1)} %get-tuple-element.35), channel_id=1, source_target_pairs={{0,4},{4,8},{8,12},{12,0},{1,5},{5,9},{9,13},{13,1},{2,6},{6,10},{... | collective-permute-start | bytes 282632 | tf_op jit(solution)/shard_map/ppermute | solution.py:762
  6.1 7.7 %collective-permute-start.2 = (f32[148,128]{1,0:T(8,128)S(1)}, f32[148,128]{1,0:T(8,128)S(1)}, u32[]{:S(2)}, u32[]{:S(2)}) collective-permute-start(f32[148,128]{1,0:T(8,128)S(1)} %get-tuple-element.37), channel_id=1, source_target_pairs={{0,12},{4,0},{8,4},{12,8},{1,13},{5,1},{9,5},{13,9},{2,14},{6,2},{... | collective-permute-start | bytes 227336 | tf_op jit(solution)/shard_map/ppermute | solution.py:762
  8.2 4.0 %collective-permute-start = (f32[88,128]{1,0:T(8,128)S(1)}, f32[88,128]{1,0:T(8,128)S(1)}, u32[]{:S(2)}, u32[]{:S(2)}) collective-permute-start(f32[88,128]{1,0:T(8,128)S(1)} %get-tuple-element.27.own_ref), channel_id=1, source_target_pairs={{0,2},{2,0},{1,3},{3,1},{4,6},{6,4},{5,7},{7,5},{8,10},{10,8},{9,1... | collective-permute-start | bytes 135176 | tf_op jit(solution)/shard_map/ppermute | solution.py:762
  14.9 4.2 %collective-permute-start.3 = (f32[80,128]{1,0:T(8,128)S(1)}, f32[80,128]{1,0:T(8,128)S(1)}, u32[]{:S(2)}, u32[]{:S(2)}) collective-permute-start(f32[80,128]{1,0:T(8,128)S(1)} %get-tuple-element.43.refs_2_), channel_id=1, source_target_pairs={{0,2},{2,0},{1,3},{3,1},{4,6},{6,4},{5,7},{7,5},{8,10},{10,8},{9,1... | collective-permute-start | bytes 122888 | tf_op jit(solution)/shard_map/ppermute | solution.py:762
  19.6 4.5 %collective-permute-start.5 = (f32[128,128]{1,0:T(8,128)S(1)}, f32[128,128]{1,0:T(8,128)S(1)}, u32[]{:S(2)}, u32[]{:S(2)}) collective-permute-start(f32[128,128]{1,0:T(8,128)S(1)} %get-tuple-element.51.block_ref), channel_id=1, source_target_pairs={{0,12},{4,0},{8,4},{12,8},{1,13},{5,1},{9,5},{13,9},{2,14},{6,2},{... | collective-permute-start | bytes 196616 | tf_op jit(solution)/shard_map/ppermute | solution.py:762
  21.5 6.1 %collective-permute-start.4 = (f32[128,128]{1,0:T(8,128)S(1)}, f32[128,128]{1,0:T(8,128)S(1)}, u32[]{:S(2)}, u32[]{:S(2)}) collective-permute-start(f32[128,128]{1,0:T(8,128)S(1)} %get-tuple-element.51.block_ref), channel_id=1, source_target_pairs={{0,4},{4,8},{8,12},{12,0},{1,5},{5,9},{9,13},{13,1},{2,6},{6,10},{... | collective-permute-start | bytes 196616 | tf_op jit(solution)/shard_map/ppermute | solution.py:762

commit v7 on v6

--- a/solution.py
+++ b/solution.py
@@ -102,7 +102,8 @@
     rim[2 * pad + 1 : 2 * pad + 2, :] = packed_row(cluster[...].astype(F32))
     rim[2 * pad + 2 : 2 * pad + 3, :] = packed_row(strength[...])
     rim[2 * pad + 3 : 2 * pad + 8, :] = jnp.zeros((5, lanes), F32)
-    turned = matrix[...].T
+    square = [lax.broadcasted_iota(jnp.int32, (lev, lev), axis) for axis in (0, 1)]
+    turned = matrix[...].T - jnp.where(square[0] == square[1], 1.0, 0.0)
     turned = jnp.concatenate([turned, jnp.zeros((pad - lev, lev), F32)], axis=0)
     turned = jnp.concatenate([turned, jnp.zeros((pad, deep - lev), F32)], axis=1)
     high = turned.astype(BF16).astype(F32)
@@ -124,9 +125,8 @@
     lev, width_x, lanes = dims
     pad = round_up(lev, 8)
     tiles = [kernel_ref[pl.ds(at, pad, stride=width_x), :] * innov_ref[at : at + 1, :] for at in (x, x + 1)]
-    mixed = mix(lhs, jnp.concatenate(tiles, axis=1))
-    parts = [mixed[:, k * lanes : (k + 1) * lanes] for k in (0, 1)]
-    return [t + strength_ref[x + k : x + k + 1, :] * (p - t) for k, (t, p) in enumerate(zip(tiles, parts))]
+    moved = mix(lhs, jnp.concatenate([strength_ref[x + k : x + k + 1, :] * t for k, t in enumerate(tiles)], axis=1))
+    return [t + moved[:, k * lanes : (k + 1) * lanes] for k, t in enumerate(tiles)]
 
 
 def first_ends_kernel(dims, *refs):
@@ -190,9 +190,10 @@
         jnp.where(lower, own, 0.0) * own_misc[0:1],
         jnp.where(lower, far, 0.0) * far_misc[0:1],
     ]
-    mixed = mix(lhs_ref[...], jnp.concatenate(sources, axis=1))
-    rim_c = sources[0] + own_misc[2:3] * (mixed[:, :lanes] - sources[0])
-    far_c = sources[1] + far_misc[2:3] * (mixed[:, lanes:] - sources[1])
+    lifted = [sources[0] * own_misc[2:3], sources[1] * far_misc[2:3]]
+    moved = mix(lhs_ref[...], jnp.concatenate(lifted, axis=1))
+    rim_c = sources[0] + moved[:, :lanes]
+    far_c = sources[1] + moved[:, lanes:]
     own_wy = jnp.where(lower, turn(own, half), 0.0)
     far_wy = jnp.where(lower, turn(far, half), 0.0)
     far_wx = halo(slice(pad, 2 * pad))
@@ -237,8 +238,8 @@
 
 def convect(lhs, fields, strength):
     lanes = strength.shape[1]
-    mixed = mix(lhs, jnp.concatenate(fields, axis=1))
-    return [f + strength * (mixed[:, k * lanes : (k + 1) * lanes] - f) for k, f in enumerate(fields)]
+    moved = mix(lhs, jnp.concatenate([strength * f for f in fields], axis=1))
+    return [f + moved[:, k * lanes : (k + 1) * lanes] for k, f in enumerate(fields)]
 
 
 def advance(dims, ids, lhs, x, at, rim):

time: 29 us -> 29 us (level)
  no operation moved by 1% of the time
where the time goes in v7:
time: 29 us; the launch traced here: 28.8 us
  Pallas kernels  12.4 us (43%)
  starting transfers between devices  10.6 us (37%)
  waiting for transfers between devices  5.01 us (17%)
  between operations  0.73 us (3%)
    pallas_call x12, Pallas kernels, call(): pl.pallas_call(kernel, out_shape=[(jax.ShapeDtypeStruct if at in far_out...  11.5 us
    ppermute x6, starting transfers between devices, ring(): lax.ppermute(value, axis, [(i, (i + steps) % count) for i in range(count)])  10.6 us
    ppermute x6, waiting for transfers between devices, ring(): lax.ppermute(value, axis, [(i, (i + steps) % count) for i in range(count)])  5.01 us
    pallas_call x1, Pallas kernels, body(): pl.pallas_call(functools.partial(output_ends_kernel, dims, subs, per_devi...  0.94 us
  transfers between devices with their start and end apart: 6, of which 2 were waited for; matrix products, arithmetic and copies ran while one was open for 0% of the time, Pallas kernels for 25%

profile of v7, /device:TPU:0, one launch (start us, length us, event | category | flops | bytes accessed | tf_op | source)
XLA Modules:
  0.0 28.8 jit_solution(15527013187586767104)
XLA Ops:
  0.6 2.2 %shard_map.104 = (f32[640,128]{1,0:T(8,128)S(1)}, f32[640,128]{1,0:T(8,128)S(1)}, f32[640,128]{1,0:T(8,128)S(1)}, f32[16,128]{1,0:T(8,128)S(1)}, s32[16,128]{1,0...) custom-call(f32[576,128]{1,0:T(8,128)} %bitcast.7, ...), custom_call_target="tpu_custom_call" | custom-call | tf_op jit(solution)/shard_map/pallas_call | solution.py:23
  2.9 0.2 shard_map.106
  3.1 3.1 %collective-permute-start.1 = (f32[184,128]{1,0:T(8,128)S(1)}, f32[184,128]{1,0:T(8,128)S(1)}, u32[]{:S(2)}, u32[]{:S(2)}) collective-permute-start(f32[184,128]{1,0:T(8,128)S(1)} %get-tuple-element.35), channel_id=1, source_target_pairs={{0,4},{4,8},{8,12},{12,0},{1,5},{5,9},{9,13},{13,1},{2,6},{6,10},{... | collective-permute-start | bytes 282632 | tf_op jit(solution)/shard_map/ppermute | solution.py:763
  6.2 2.1 %collective-permute-start.2 = (f32[148,128]{1,0:T(8,128)S(1)}, f32[148,128]{1,0:T(8,128)S(1)}, u32[]{:S(2)}, u32[]{:S(2)}) collective-permute-start(f32[148,128]{1,0:T(8,128)S(1)} %get-tuple-element.37), channel_id=1, source_target_pairs={{0,12},{4,0},{8,4},{12,8},{1,13},{5,1},{9,5},{13,9},{2,14},{6,2},{... | collective-permute-start | bytes 227336 | tf_op jit(solution)/shard_map/ppermute | solution.py:763
  8.3 1.6 %collective-permute-start = (f32[88,128]{1,0:T(8,128)S(1)}, f32[88,128]{1,0:T(8,128)S(1)}, u32[]{:S(2)}, u32[]{:S(2)}) collective-permute-start(f32[88,128]{1,0:T(8,128)S(1)} %get-tuple-element.27.own_ref), channel_id=1, source_target_pairs={{0,2},{2,0},{1,3},{3,1},{4,6},{6,4},{5,7},{7,5},{8,10},{10,8},{9,1... | collective-permute-start | bytes 135176 | tf_op jit(solution)/shard_map/ppermute | solution.py:763
  9.9 0.3 shard_map.107.c_ref.refs_4_
  10.2 2.1 %collective-permute-done.south_ref.north_ref = f32[88,128]{1,0:T(8,128)S(1)} collective-permute-done((f32[88,128]{1,0:T(8,128)S(1)}, f32[88,128]{1,0:T(8,128)S(1)}, u32[]{:S(2)}, u32[]{:S(2)}) %collective-permute-start) | collective-permute-done | bytes 45088 | tf_op jit(solution)/shard_map/ppermute | solution.py:763
  12.3 0.1 shard_map.105.rim_ref.refs_0_
  12.5 1.4 %shard_map.108 = (f32[4,14,40,128]{3,2,1,0:T(8,128)S(1)}, f32[4,24,128]{2,1,0:T(8,128)S(1)}) custom-call(f32[248,128]{1,0:T(8,128)S(1)} %shard_map.105.rim_ref.refs_0_, f32[16,40,128]{2,1,0:T(8,128)S(1)} %shard_map.107.c_ref.refs_4_, f32[640,128]{1,0:T(8,128)S(1)} %get-tuple-element.32.refs_4_.wx_ref.refs_5_, ...), custom_call_target="tpu_custom_call" | custom-call | flops 4000000 | bytes 4000000 | tf_op jit(solution)/shard_map/pallas_call | solution.py:23
  13.9 0.0 collective-permute-done.2.refs_2_
  13.9 0.0 collective-permute-done.1.refs_1_
  13.9 1.0 %shard_map.109 = (f32[4,4,40,128]{3,2,1,0:T(8,128)S(1)}, f32[2,48,128]{2,1,0:T(8,128)S(1)}, f32[80,128]{1,0:T(8,128)S(1)}, f32[128,128]{1,0:T(8,128)S(1)}) custom-call(f32[248,128]{1,0:T(8,128)S(1)} %shard_map.105.rim_ref.refs_0_, f32[184,128]{1,0:T(8,128)S(1)} %collective-permute-done.1.refs_1_, f32[148,128]{1,0:T(8,128)S(1)} %collective-permute-done.2.refs_2_, ...), custom_call_target="tpu_custom_call" | custom-call | tf_op jit(solution)/shard_map/pallas_call | solution.py:23
  14.9 1.7 %collective-permute-start.3 = (f32[80,128]{1,0:T(8,128)S(1)}, f32[80,128]{1,0:T(8,128)S(1)}, u32[]{:S(2)}, u32[]{:S(2)}) collective-permute-start(f32[80,128]{1,0:T(8,128)S(1)} %get-tuple-element.43.refs_2_), channel_id=1, source_target_pairs={{0,2},{2,0},{1,3},{3,1},{4,6},{6,4},{5,7},{7,5},{8,10},{10,8},{9,1... | collective-permute-start | bytes 122888 | tf_op jit(solution)/shard_map/ppermute | solution.py:763
  16.6 2.4 %shard_map.110 = (f32[4,36,16,1,128]{4,3,2,1,0:T(1,128)}, f32[8,128]{1,0:T(8,128)S(1)}, f32[4,2,40,128]{3,2,1,0:T(8,128)S(1)}) custom-call(f32[248,128]{1,0:T(8,128)S(1)} %shard_map.105.rim_ref.refs_0_, f32[184,128]{1,0:T(8,128)S(1)} %collective-permute-done.1.refs_1_, f32[4,14,40,128]{3,2,1,0:T(8,128)S(1)} %get-tuple-element.36.refs_2_, ...), custom_call_target="tpu_custom_call" | custom-call | flops 4000000 | bytes 4000000 | tf_op jit(solution)/shard_map/pallas_call | solution.py:23
  19.1 0.0 collective-permute-done.3.refs_3_.refs_4_
  19.1 0.6 %shard_map.111 = (f32[128,128]{1,0:T(8,128)S(1)}, f32[1,320,128]{2,1,0:T(8,128)S(1)}) custom-call(f32[248,128]{1,0:T(8,128)S(1)} %shard_map.105.rim_ref.refs_0_, f32[128,128]{1,0:T(8,128)S(1)} %get-tuple-element.42.refs_1_, f32[80,128]{1,0:T(8,128)S(1)} %get-tuple-element.43.refs_2_, f32[80,128]{1,0:T(8,128)S(1)} %collective-permute-done.3.refs_3_.refs_4_, ...), custom_call_target="tpu_custom_call" | custom-call | tf_op jit(solution)/shard_map/pallas_call | solution.py:23
  19.6 1.9 %collective-permute-start.5 = (f32[128,128]{1,0:T(8,128)S(1)}, f32[128,128]{1,0:T(8,128)S(1)}, u32[]{:S(2)}, u32[]{:S(2)}) collective-permute-start(f32[128,128]{1,0:T(8,128)S(1)} %get-tuple-element.51.block_ref), channel_id=1, source_target_pairs={{0,12},{4,0},{8,4},{12,8},{1,13},{5,1},{9,5},{13,9},{2,14},{6,2},{... | collective-permute-start | bytes 196616 | tf_op jit(solution)/shard_map/ppermute | solution.py:763
  21.6 0.2 collective-permute-start.4
  21.7 0.8 %shard_map.112 = (bf16[8,256,768]{2,1,0:T(8,128)(2,1)S(1)}, f32[8,48,768]{2,1,0:T(8,128)S(1)}) custom-call(s32[8,768]{1,0:T(8,128)S(1)} %get-tuple-element.47.cell_ref, f32[8,768]{1,0:T(8,128)S(1)} %get-tuple-element.48.weight_ref), custom_call_target="tpu_custom_call" | custom-call | flops 2000000 | bytes 2000000 | tf_op jit(solution)/shard_map/pallas_call | solution.py:23
  22.6 0.9 %output_ends.1 = f32[4,36,16,1,128]{4,3,2,1,0:T(1,128)} custom-call(f32[4,36,16,1,128]{4,3,2,1,0:T(1,128)} %get-tuple-element.41._, f32[1,320,128]{2,1,0:T(8,128)S(1)} %get-tuple-element.45.seam_ref, f32[4,2,40,128]{3,2,1,0:T(8,128)S(1)} %get-tuple-element.46.edge_ref), custom_call_target="tpu_custom_call", output_to_operand_aliasing={{}: (0, {})} | custom-call | flops 1000000 | bytes 1000000 | tf_op jit(solution)/shard_map/output_ends/pallas_call | solution.py:883
  23.5 0.6 %shard_map.113.refs_0_ = f32[4,768]{1,0:T(4,128)S(1)} custom-call(bf16[8,256,768]{2,1,0:T(8,128)(2,1)S(1)} %get-tuple-element.49.hot_ref.refs_0_, f32[8,48,768]{2,1,0:T(8,128)S(1)} %get-tuple-element.50.share_ref.refs_1_, f32[128,128]{1,0:T(8,128)S(1)} %get-tuple-element.51.block_ref), custom_call_target="tpu_custom_call" | custom-call | flops 2000000 | bytes 2000000 | tf_op jit(solution)/shard_map/pallas_call | solution.py:23
  24.1 0.0 collective-permute-done.5.block_ref
  24.2 0.6 %shard_map.114.refs_3_ = f32[4,768]{1,0:T(4,128)S(1)} custom-call(bf16[8,256,768]{2,1,0:T(8,128)(2,1)S(1)} %get-tuple-element.49.hot_ref.refs_0_, f32[8,48,768]{2,1,0:T(8,128)S(1)} %get-tuple-element.50.share_ref.refs_1_, f32[128,128]{1,0:T(8,128)S(1)} %collective-permute-done.5.block_ref, f32[4,768]{1,0:T(4,128)S(1)} %shard_map.113.refs_0_), custom_call_target="tpu_custom_call" | custom-call | flops 2000000 | bytes 2000000 | tf_op jit(solution)/shard_map/pallas_call | solution.py:23
  24.8 2.8 %collective-permute-done.4.refs_2_ = f32[128,128]{1,0:T(8,128)S(1)} collective-permute-done((f32[128,128]{1,0:T(8,128)S(1)}, f32[128,128]{1,0:T(8,128)S(1)}, u32[]{:S(2)}, u32[]{:S(2)}) %collective-permute-start.4) | collective-permute-done | bytes 65568 | tf_op jit(solution)/shard_map/ppermute | solution.py:763
  27.6 1.2 %shard_map.115 = f32[4,768]{1,0:T(4,128)} custom-call(bf16[8,256,768]{2,1,0:T(8,128)(2,1)S(1)} %get-tuple-element.49.hot_ref.refs_0_, f32[8,48,768]{2,1,0:T(8,128)S(1)} %get-tuple-element.50.share_ref.refs_1_, f32[128,128]{1,0:T(8,128)S(1)} %collective-permute-done.4.refs_2_, f32[4,768]{1,0:T(4,128)S(1)} %shard_map.114.refs_3_), custom_call_target="tpu_custom_call" | custom-call | tf_op jit(solution)/shard_map/pallas_call | solution.py:23
Async XLA Ops:
  3.1 10.8 %collective-permute-start.1 = (f32[184,128]{1,0:T(8,128)S(1)}, f32[184,128]{1,0:T(8,128)S(1)}, u32[]{:S(2)}, u32[]{:S(2)}) collective-permute-start(f32[184,128]{1,0:T(8,128)S(1)} %get-tuple-element.35), channel_id=1, source_target_pairs={{0,4},{4,8},{8,12},{12,0},{1,5},{5,9},{9,13},{13,1},{2,6},{6,10},{... | collective-permute-start | bytes 282632 | tf_op jit(solution)/shard_map/ppermute | solution.py:763
  6.2 7.7 %collective-permute-start.2 = (f32[148,128]{1,0:T(8,128)S(1)}, f32[148,128]{1,0:T(8,128)S(1)}, u32[]{:S(2)}, u32[]{:S(2)}) collective-permute-start(f32[148,128]{1,0:T(8,128)S(1)} %get-tuple-element.37), channel_id=1, source_target_pairs={{0,12},{4,0},{8,4},{12,8},{1,13},{5,1},{9,5},{13,9},{2,14},{6,2},{... | collective-permute-start | bytes 227336 | tf_op jit(solution)/shard_map/ppermute | solution.py:763
  8.3 4.0 %collective-permute-start = (f32[88,128]{1,0:T(8,128)S(1)}, f32[88,128]{1,0:T(8,128)S(1)}, u32[]{:S(2)}, u32[]{:S(2)}) collective-permute-start(f32[88,128]{1,0:T(8,128)S(1)} %get-tuple-element.27.own_ref), channel_id=1, source_target_pairs={{0,2},{2,0},{1,3},{3,1},{4,6},{6,4},{5,7},{7,5},{8,10},{10,8},{9,1... | collective-permute-start | bytes 135176 | tf_op jit(solution)/shard_map/ppermute | solution.py:763
  14.9 4.2 %collective-permute-start.3 = (f32[80,128]{1,0:T(8,128)S(1)}, f32[80,128]{1,0:T(8,128)S(1)}, u32[]{:S(2)}, u32[]{:S(2)}) collective-permute-start(f32[80,128]{1,0:T(8,128)S(1)} %get-tuple-element.43.refs_2_), channel_id=1, source_target_pairs={{0,2},{2,0},{1,3},{3,1},{4,6},{6,4},{5,7},{7,5},{8,10},{10,8},{9,1... | collective-permute-start | bytes 122888 | tf_op jit(solution)/shard_map/ppermute | solution.py:763
  19.6 4.5 %collective-permute-start.5 = (f32[128,128]{1,0:T(8,128)S(1)}, f32[128,128]{1,0:T(8,128)S(1)}, u32[]{:S(2)}, u32[]{:S(2)}) collective-permute-start(f32[128,128]{1,0:T(8,128)S(1)} %get-tuple-element.51.block_ref), channel_id=1, source_target_pairs={{0,12},{4,0},{8,4},{12,8},{1,13},{5,1},{9,5},{13,9},{2,14},{6,2},{... | collective-permute-start | bytes 196616 | tf_op jit(solution)/shard_map/ppermute | solution.py:763
  21.6 6.1 %collective-permute-start.4 = (f32[128,128]{1,0:T(8,128)S(1)}, f32[128,128]{1,0:T(8,128)S(1)}, u32[]{:S(2)}, u32[]{:S(2)}) collective-permute-start(f32[128,128]{1,0:T(8,128)S(1)} %get-tuple-element.51.block_ref), channel_id=1, source_target_pairs={{0,4},{4,8},{8,12},{12,0},{1,5},{5,9},{9,13},{13,1},{2,6},{6,10},{... | collective-permute-start | bytes 196616 | tf_op jit(solution)/shard_map/ppermute | solution.py:763

commit v8 on v7

--- a/solution.py
+++ b/solution.py
@@ -65,20 +65,20 @@
 
 def fetch_kernel(dims, *refs):
     lev, width_x, lanes = dims
-    sources, (kernel, wx, wy, innov, cluster, strength, matrix, cell, weight, lhs, rim), scratch = (
-        refs[:9],
-        refs[9:20],
-        refs[20:],
+    sources, (kernel, wx, wy, innov, cluster, strength, matrix, lhs, rim), scratch = (
+        refs[:7],
+        refs[7:16],
+        refs[16:],
     )
     (sem,) = scratch
     pad = round_up(lev, 8)
     deep = lhs.shape[1] // 3
     half = 4 * width_x
     whole = lev * width_x
-    copies = [pltpu.make_async_copy(s, t, sem.at[i]) for i, (s, t) in enumerate(zip(sources[3:], refs[12:18]))]
+    copies = [pltpu.make_async_copy(s, t, sem.at[i]) for i, (s, t) in enumerate(zip(sources[3:], refs[10:14]))]
     targets = [ref.at[pl.ds(0, whole), :] for ref in (kernel, wx, wy)]
-    large = [pltpu.make_async_copy(s, t, sem.at[6 + i]) for i, (s, t) in enumerate(zip(sources, targets))]
-    for copy in copies[:4] + large + copies[4:]:
+    large = [pltpu.make_async_copy(s, t, sem.at[4 + i]) for i, (s, t) in enumerate(zip(sources, targets))]
+    for copy in copies + large:
         copy.start()
     for ref in (kernel, wx, wy):
         ref[pl.ds(whole, (pad - lev) * width_x), :] = jnp.zeros(((pad - lev) * width_x, lanes), F32)
@@ -117,8 +117,6 @@
     large[1].wait()
     for r in range(pad // 8):
         rim[pad + 8 * r : pad + 8 * r + 8, :] = packed(wx, 0, r)
-    for copy in copies[4:]:
-        copy.wait()
 
 
 def first_columns(dims, kernel_ref, innov_ref, strength_ref, lhs, x):
@@ -802,11 +800,10 @@
         cluster,
         conv_strength,
         conv_matrix,
-        margin_cell.T,
-        margin_weight.T,
-    )
+    )
+    cell, weight = margin_cell.T, margin_weight.T
     outs = [tall, tall, tall, small, (small, jnp.int32), small, conv_matrix.shape]
-    outs += [(sources[7].shape, jnp.int32), sources[8].shape, ((pad, 3 * deep), BF16), (2 * pad + 8, width_y)]
+    outs += [((pad, 3 * deep), BF16), (2 * pad + 8, width_y)]
     fetched = call(
         functools.partial(fetch_kernel, dims),
         outs,
@@ -814,7 +811,7 @@
         scratch=(pltpu.SemaphoreType.DMA((len(sources),)),),
         far_in=True,
     )
-    air, wx, wy, innov, group, strength, _, cell, weight, lhs, own_rim = fetched
+    air, wx, wy, innov, group, strength, _, lhs, own_rim = fetched
     south_rim, north_rim = across(own_rim)
     to_east, to_west = call(
         functools.partial(first_ends_kernel, dims),

time: 29 us -> 28.9 us (level)
  no operation moved by 1% of the time
where the time goes in v8:
time: 28.9 us; the launch traced here: 28.7 us
  Pallas kernels  12.4 us (43%)
  starting transfers between devices  10.6 us (37%)
  waiting for transfers between devices  4.99 us (17%)
  between operations  0.74 us (3%)
    pallas_call x12, Pallas kernels, call(): pl.pallas_call(kernel, out_shape=[(jax.ShapeDtypeStruct if at in far_out...  11.4 us
    ppermute x6, starting transfers between devices, ring(): lax.ppermute(value, axis, [(i, (i + steps) % count) for i in range(count)])  10.6 us
    ppermute x6, waiting for transfers between devices, ring(): lax.ppermute(value, axis, [(i, (i + steps) % count) for i in range(count)])  4.99 us
    pallas_call x1, Pallas kernels, body(): pl.pallas_call(functools.partial(output_ends_kernel, dims, subs, per_devi...  0.94 us
  transfers between devices with their start and end apart: 6, of which 2 were waited for; matrix products, arithmetic and copies ran while one was open for 0% of the time, Pallas kernels for 25%

profile of v8, /device:TPU:0, one launch (start us, length us, event | category | flops | bytes accessed | tf_op | source)
XLA Modules:
  0.0 28.7 jit_solution(2032569639593896347)
XLA Ops:
  0.6 2.1 %shard_map.104 = (f32[640,128]{1,0:T(8,128)S(1)}, f32[640,128]{1,0:T(8,128)S(1)}, f32[640,128]{1,0:T(8,128)S(1)}, f32[16,128]{1,0:T(8,128)S(1)}, s32[16,128]{1,0...) custom-call(f32[576,128]{1,0:T(8,128)} %bitcast.9, ...), custom_call_target="tpu_custom_call" | custom-call | tf_op jit(solution)/shard_map/pallas_call | solution.py:23
  2.8 0.2 shard_map.106
  3.0 3.1 %collective-permute-start.1 = (f32[184,128]{1,0:T(8,128)S(1)}, f32[184,128]{1,0:T(8,128)S(1)}, u32[]{:S(2)}, u32[]{:S(2)}) collective-permute-start(f32[184,128]{1,0:T(8,128)S(1)} %get-tuple-element.33), channel_id=1, source_target_pairs={{0,4},{4,8},{8,12},{12,0},{1,5},{5,9},{9,13},{13,1},{2,6},{6,10},{... | collective-permute-start | bytes 282632 | tf_op jit(solution)/shard_map/ppermute | solution.py:761
  6.1 2.1 %collective-permute-start.2 = (f32[148,128]{1,0:T(8,128)S(1)}, f32[148,128]{1,0:T(8,128)S(1)}, u32[]{:S(2)}, u32[]{:S(2)}) collective-permute-start(f32[148,128]{1,0:T(8,128)S(1)} %get-tuple-element.35), channel_id=1, source_target_pairs={{0,12},{4,0},{8,4},{12,8},{1,13},{5,1},{9,5},{13,9},{2,14},{6,2},{... | collective-permute-start | bytes 227336 | tf_op jit(solution)/shard_map/ppermute | solution.py:761
  8.2 1.6 %collective-permute-start = (f32[88,128]{1,0:T(8,128)S(1)}, f32[88,128]{1,0:T(8,128)S(1)}, u32[]{:S(2)}, u32[]{:S(2)}) collective-permute-start(f32[88,128]{1,0:T(8,128)S(1)} %get-tuple-element.25.own_ref), channel_id=1, source_target_pairs={{0,2},{2,0},{1,3},{3,1},{4,6},{6,4},{5,7},{7,5},{8,10},{10,8},{9,1... | collective-permute-start | bytes 135176 | tf_op jit(solution)/shard_map/ppermute | solution.py:761
  9.8 0.3 shard_map.107.c_ref.refs_4_
  10.1 2.1 %collective-permute-done.south_ref.north_ref = f32[88,128]{1,0:T(8,128)S(1)} collective-permute-done((f32[88,128]{1,0:T(8,128)S(1)}, f32[88,128]{1,0:T(8,128)S(1)}, u32[]{:S(2)}, u32[]{:S(2)}) %collective-permute-start) | collective-permute-done | bytes 45088 | tf_op jit(solution)/shard_map/ppermute | solution.py:761
  12.2 0.1 shard_map.105.rim_ref.refs_0_
  12.4 1.4 %shard_map.108 = (f32[4,14,40,128]{3,2,1,0:T(8,128)S(1)}, f32[4,24,128]{2,1,0:T(8,128)S(1)}) custom-call(f32[248,128]{1,0:T(8,128)S(1)} %shard_map.105.rim_ref.refs_0_, f32[16,40,128]{2,1,0:T(8,128)S(1)} %shard_map.107.c_ref.refs_4_, f32[640,128]{1,0:T(8,128)S(1)} %get-tuple-element.30.refs_4_.wx_ref.refs_5_, ...), custom_call_target="tpu_custom_call" | custom-call | flops 4000000 | bytes 4000000 | tf_op jit(solution)/shard_map/pallas_call | solution.py:23
  13.8 0.0 collective-permute-done.2.refs_2_
  13.8 0.0 collective-permute-done.1.refs_1_
  13.8 1.0 %shard_map.109 = (f32[4,4,40,128]{3,2,1,0:T(8,128)S(1)}, f32[2,48,128]{2,1,0:T(8,128)S(1)}, f32[80,128]{1,0:T(8,128)S(1)}, f32[128,128]{1,0:T(8,128)S(1)}) custom-call(f32[248,128]{1,0:T(8,128)S(1)} %shard_map.105.rim_ref.refs_0_, f32[184,128]{1,0:T(8,128)S(1)} %collective-permute-done.1.refs_1_, f32[148,128]{1,0:T(8,128)S(1)} %collective-permute-done.2.refs_2_, ...), custom_call_target="tpu_custom_call" | custom-call | tf_op jit(solution)/shard_map/pallas_call | solution.py:23
  14.8 1.7 %collective-permute-start.3 = (f32[80,128]{1,0:T(8,128)S(1)}, f32[80,128]{1,0:T(8,128)S(1)}, u32[]{:S(2)}, u32[]{:S(2)}) collective-permute-start(f32[80,128]{1,0:T(8,128)S(1)} %get-tuple-element.41.refs_2_), channel_id=1, source_target_pairs={{0,2},{2,0},{1,3},{3,1},{4,6},{6,4},{5,7},{7,5},{8,10},{10,8},{9,1... | collective-permute-start | bytes 122888 | tf_op jit(solution)/shard_map/ppermute | solution.py:761
  16.5 0.0 copy-start
  16.5 0.0 copy-start.1
  16.5 2.4 %shard_map.110 = (f32[4,36,16,1,128]{4,3,2,1,0:T(1,128)}, f32[8,128]{1,0:T(8,128)S(1)}, f32[4,2,40,128]{3,2,1,0:T(8,128)S(1)}) custom-call(f32[248,128]{1,0:T(8,128)S(1)} %shard_map.105.rim_ref.refs_0_, f32[184,128]{1,0:T(8,128)S(1)} %collective-permute-done.1.refs_1_, f32[4,14,40,128]{3,2,1,0:T(8,128)S(1)} %get-tuple-element.34.refs_2_, ...), custom_call_target="tpu_custom_call" | custom-call | flops 4000000 | bytes 4000000 | tf_op jit(solution)/shard_map/pallas_call | solution.py:23
  19.0 0.0 collective-permute-done.3.refs_3_.refs_4_
  19.0 0.6 %shard_map.111 = (f32[128,128]{1,0:T(8,128)S(1)}, f32[1,320,128]{2,1,0:T(8,128)S(1)}) custom-call(f32[248,128]{1,0:T(8,128)S(1)} %shard_map.105.rim_ref.refs_0_, f32[128,128]{1,0:T(8,128)S(1)} %get-tuple-element.40.refs_1_, f32[80,128]{1,0:T(8,128)S(1)} %get-tuple-element.41.refs_2_, f32[80,128]{1,0:T(8,128)S(1)} %collective-permute-done.3.refs_3_.refs_4_, ...), custom_call_target="tpu_custom_call" | custom-call | tf_op jit(solution)/shard_map/pallas_call | solution.py:23
  19.5 1.9 %collective-permute-start.5 = (f32[128,128]{1,0:T(8,128)S(1)}, f32[128,128]{1,0:T(8,128)S(1)}, u32[]{:S(2)}, u32[]{:S(2)}) collective-permute-start(f32[128,128]{1,0:T(8,128)S(1)} %get-tuple-element.47.block_ref), channel_id=1, source_target_pairs={{0,12},{4,0},{8,4},{12,8},{1,13},{5,1},{9,5},{13,9},{2,14},{6,2},{... | collective-permute-start | bytes 196616 | tf_op jit(solution)/shard_map/ppermute | solution.py:761
  21.5 0.2 collective-permute-start.4
  21.6 0.0 copy-done
  21.6 0.0 copy-done.1
  21.6 0.8 %shard_map.112 = (bf16[8,256,768]{2,1,0:T(8,128)(2,1)S(1)}, f32[8,48,768]{2,1,0:T(8,128)S(1)}) custom-call(s32[8,768]{1,0:T(8,128)S(1)} %bitcast.6, f32[8,768]{1,0:T(8,128)S(1)} %bitcast.7), custom_call_target="tpu_custom_call" | custom-call | flops 2000000 | bytes 2000000 | tf_op jit(solution)/shard_map/pallas_call | solution.py:23
  22.5 0.9 %output_ends.1 = f32[4,36,16,1,128]{4,3,2,1,0:T(1,128)} custom-call(f32[4,36,16,1,128]{4,3,2,1,0:T(1,128)} %get-tuple-element.39._, f32[1,320,128]{2,1,0:T(8,128)S(1)} %get-tuple-element.43.seam_ref, f32[4,2,40,128]{3,2,1,0:T(8,128)S(1)} %get-tuple-element.44.edge_ref), custom_call_target="tpu_custom_call", output_to_operand_aliasing={{}: (0, {})} | custom-call | flops 1000000 | bytes 1000000 | tf_op jit(solution)/shard_map/output_ends/pallas_call | solution.py:880
  23.4 0.6 %shard_map.113.refs_0_ = f32[4,768]{1,0:T(4,128)S(1)} custom-call(bf16[8,256,768]{2,1,0:T(8,128)(2,1)S(1)} %get-tuple-element.45.hot_ref.refs_0_, f32[8,48,768]{2,1,0:T(8,128)S(1)} %get-tuple-element.46.share_ref.refs_1_, f32[128,128]{1,0:T(8,128)S(1)} %get-tuple-element.47.block_ref), custom_call_target="tpu_custom_call" | custom-call | flops 2000000 | bytes 2000000 | tf_op jit(solution)/shard_map/pallas_call | solution.py:23
  24.0 0.0 collective-permute-done.5.block_ref
  24.1 0.6 %shard_map.114.refs_3_ = f32[4,768]{1,0:T(4,128)S(1)} custom-call(bf16[8,256,768]{2,1,0:T(8,128)(2,1)S(1)} %get-tuple-element.45.hot_ref.refs_0_, f32[8,48,768]{2,1,0:T(8,128)S(1)} %get-tuple-element.46.share_ref.refs_1_, f32[128,128]{1,0:T(8,128)S(1)} %collective-permute-done.5.block_ref, f32[4,768]{1,0:T(4,128)S(1)} %shard_map.113.refs_0_), custom_call_target="tpu_custom_call" | custom-call | flops 2000000 | bytes 2000000 | tf_op jit(solution)/shard_map/pallas_call | solution.py:23
  24.7 2.8 %collective-permute-done.4.refs_2_ = f32[128,128]{1,0:T(8,128)S(1)} collective-permute-done((f32[128,128]{1,0:T(8,128)S(1)}, f32[128,128]{1,0:T(8,128)S(1)}, u32[]{:S(2)}, u32[]{:S(2)}) %collective-permute-start.4) | collective-permute-done | bytes 65568 | tf_op jit(solution)/shard_map/ppermute | solution.py:761
  27.5 1.2 %shard_map.115 = f32[4,768]{1,0:T(4,128)} custom-call(bf16[8,256,768]{2,1,0:T(8,128)(2,1)S(1)} %get-tuple-element.45.hot_ref.refs_0_, f32[8,48,768]{2,1,0:T(8,128)S(1)} %get-tuple-element.46.share_ref.refs_1_, f32[128,128]{1,0:T(8,128)S(1)} %collective-permute-done.4.refs_2_, f32[4,768]{1,0:T(4,128)S(1)} %shard_map.114.refs_3_), custom_call_target="tpu_custom_call" | custom-call | tf_op jit(solution)/shard_map/pallas_call | solution.py:23
Async XLA Ops:
  3.0 10.8 %collective-permute-start.1 = (f32[184,128]{1,0:T(8,128)S(1)}, f32[184,128]{1,0:T(8,128)S(1)}, u32[]{:S(2)}, u32[]{:S(2)}) collective-permute-start(f32[184,128]{1,0:T(8,128)S(1)} %get-tuple-element.33), channel_id=1, source_target_pairs={{0,4},{4,8},{8,12},{12,0},{1,5},{5,9},{9,13},{13,1},{2,6},{6,10},{... | collective-permute-start | bytes 282632 | tf_op jit(solution)/shard_map/ppermute | solution.py:761
  6.1 7.7 %collective-permute-start.2 = (f32[148,128]{1,0:T(8,128)S(1)}, f32[148,128]{1,0:T(8,128)S(1)}, u32[]{:S(2)}, u32[]{:S(2)}) collective-permute-start(f32[148,128]{1,0:T(8,128)S(1)} %get-tuple-element.35), channel_id=1, source_target_pairs={{0,12},{4,0},{8,4},{12,8},{1,13},{5,1},{9,5},{13,9},{2,14},{6,2},{... | collective-permute-start | bytes 227336 | tf_op jit(solution)/shard_map/ppermute | solution.py:761
  8.2 4.0 %collective-permute-start = (f32[88,128]{1,0:T(8,128)S(1)}, f32[88,128]{1,0:T(8,128)S(1)}, u32[]{:S(2)}, u32[]{:S(2)}) collective-permute-start(f32[88,128]{1,0:T(8,128)S(1)} %get-tuple-element.25.own_ref), channel_id=1, source_target_pairs={{0,2},{2,0},{1,3},{3,1},{4,6},{6,4},{5,7},{7,5},{8,10},{10,8},{9,1... | collective-permute-start | bytes 135176 | tf_op jit(solution)/shard_map/ppermute | solution.py:761
  14.8 4.2 %collective-permute-start.3 = (f32[80,128]{1,0:T(8,128)S(1)}, f32[80,128]{1,0:T(8,128)S(1)}, u32[]{:S(2)}, u32[]{:S(2)}) collective-permute-start(f32[80,128]{1,0:T(8,128)S(1)} %get-tuple-element.41.refs_2_), channel_id=1, source_target_pairs={{0,2},{2,0},{1,3},{3,1},{4,6},{6,4},{5,7},{7,5},{8,10},{10,8},{9,1... | collective-permute-start | bytes 122888 | tf_op jit(solution)/shard_map/ppermute | solution.py:761
  16.5 5.1 %copy-start = (s32[768,8]{0,1:T(8,128)S(1)}, s32[768,8]{0,1:T(8,128)}, u32[]{:S(2)}) copy-start(s32[768,8]{0,1:T(8,128)} %param.16) | copy-start | bytes 73732
  16.5 5.1 %copy-start.1 = (f32[768,8]{0,1:T(8,128)S(1)}, f32[768,8]{0,1:T(8,128)}, u32[]{:S(2)}) copy-start(f32[768,8]{0,1:T(8,128)} %param.17) | copy-start | bytes 73732
  19.5 4.5 %collective-permute-start.5 = (f32[128,128]{1,0:T(8,128)S(1)}, f32[128,128]{1,0:T(8,128)S(1)}, u32[]{:S(2)}, u32[]{:S(2)}) collective-permute-start(f32[128,128]{1,0:T(8,128)S(1)} %get-tuple-element.47.block_ref), channel_id=1, source_target_pairs={{0,12},{4,0},{8,4},{12,8},{1,13},{5,1},{9,5},{13,9},{2,14},{6,2},{... | collective-permute-start | bytes 196616 | tf_op jit(solution)/shard_map/ppermute | solution.py:761
  21.5 6.1 %collective-permute-start.4 = (f32[128,128]{1,0:T(8,128)S(1)}, f32[128,128]{1,0:T(8,128)S(1)}, u32[]{:S(2)}, u32[]{:S(2)}) collective-permute-start(f32[128,128]{1,0:T(8,128)S(1)} %get-tuple-element.47.block_ref), channel_id=1, source_target_pairs={{0,4},{4,8},{8,12},{12,0},{1,5},{5,9},{9,13},{13,1},{2,6},{6,10},{... | collective-permute-start | bytes 196616 | tf_op jit(solution)/shard_map/ppermute | solution.py:761
